TPU v7x, 32 devices: a whole 2x2x4 slice. The times are simulated.
32 devices in a mesh: dp: 4 (over y, x), psg: 8 (over z, core).
Axes of the slice: x: 2, y: 2, z: 4, core: 2. Of those that a mesh axis runs over, the one named last changes fastest.
Arguments:
- queries: bfloat16 [4, 128, 2048], P('dp', None, 'psg'), may hold values from -4 to 4
- keys: bfloat16 [4, 16, 256, 2048], P('dp', 'psg'), may hold values from -4 to 4
- values: bfloat16 [4, 16, 256, 2048], P('dp', 'psg'), may hold values from -6 to 6
- lengths: int32 [4, 16], P('dp', 'psg'), may hold values from 16 to 256, as said below
- out_weight: bfloat16 [4096, 2048], P('psg'), may hold values from -0.125 to 0.125
- out_cotangent: bfloat16 [4, 128, 4096], P('dp', None, 'psg'), may hold values from -6 to 6
Outputs:
- layer_out: bfloat16 [4, 128, 4096], P('dp', None, 'psg')
- weight_grad: float32 [4096, 2048], P('psg')
- query_grad: bfloat16 [4, 128, 2048], P('dp', None, 'psg')
- key_grad: bfloat16 [4, 16, 256, 2048], P('dp', 'psg')
- value_grad: bfloat16 [4, 16, 256, 2048], P('dp', 'psg')
Inputs may be any that keep to these rules, and one draw needn't show every extreme that they name: `lengths`: every passage has at least 16 valid tokens, counted from its start; in every question some passage has all 256.
All inputs are finite; a program needn't handle non-finite values.
Results may differ from a plain program's by a relative error of at most 0.025.
Values may be sent and summed in bfloat16 or wider, within the bound.
No kernel may reach another device: no remote copies, remote signals or barrier semaphores. Data moves between devices by JAX's collectives and lax.ppermute only.
A program may use at most 64 MiB of HBM per device.

v0:
```python
import functools

import jax
import jax.numpy as jnp
from jax import lax
from jax.experimental import pallas as pl
from jax.experimental.pallas import tpu as pltpu
from jax.sharding import PartitionSpec as P

HEAD_SIZE = 64
PAIR = 2 * HEAD_SIZE
MASKED = -1e30
EXTRA = 16
MIB = 1 << 20

NT = (((1,), (1,)), ((), ()))
NN = (((1,), (0,)), ((), ()))
TN = (((0,), (0,)), ((), ()))
ANY = pl.BlockSpec(memory_space=pl.ANY)
VMEM = pl.BlockSpec(memory_space=pltpu.VMEM)
SMEM = pl.BlockSpec(memory_space=pltpu.SMEM)


def dot(a, b, dims):
    return lax.dot_general(a, b, dims, preferred_element_type=jnp.float32)


def swap(x, axis, size, distance):
    return lax.ppermute(x, axis, [(j, j ^ distance) for j in range(size)])


def call(kernel, *args, out, ins, outs, scratch=(), vmem=8, alias=None):
    return pl.pallas_call(
        kernel,
        out_shape=out,
        in_specs=ins,
        out_specs=outs,
        scratch_shapes=list(scratch),
        input_output_aliases=alias or {},
        compiler_params=pltpu.CompilerParams(vmem_limit_bytes=vmem * MIB),
    )(*args)


def far_first(size):
    return range(size - 2, 0, -2)


def spread(x, size):
    even = [x] + [None] * (size // 2 - 1)
    for d in far_first(size):
        even[d // 2] = swap(x, "psg", size, d)
    return even


def across(blocks, size):
    return [swap(b, "psg", size, 1) for b in blocks]


def block_stack(x, lane_low):
    zero = jnp.zeros_like(x)
    return jnp.concatenate([jnp.where(lane_low, x, zero), jnp.where(lane_low, zero, x)], axis=0)


def diagonal(x):
    rows = x.shape[1] // 2
    return jnp.concatenate([x[:HEAD_SIZE, :rows], x[HEAD_SIZE:, rows:]], axis=0)


def mask_bias(lengths_ref, passages, passage_len):
    row = lax.broadcasted_iota(jnp.int32, (passage_len, PAIR), 0)
    return jnp.concatenate([jnp.where(row < lengths_ref[0, p], 0.0, MASKED) for p in range(passages)], axis=0)


def thirds(x):
    high = x.astype(jnp.bfloat16)
    rest = x - high.astype(jnp.float32)
    middle = rest.astype(jnp.bfloat16)
    low = (rest - middle.astype(jnp.float32)).astype(jnp.bfloat16)
    parts = [high.astype(jnp.float32), middle.astype(jnp.float32), low.astype(jnp.float32)]
    pad = EXTRA - 3 * x.shape[0]
    return jnp.concatenate(parts + [jnp.zeros((pad, x.shape[1]), jnp.float32)], axis=0).astype(jnp.bfloat16)


def unite(rows, heads):
    wide = rows.astype(jnp.float32)
    return wide[:heads] + wide[heads : 2 * heads] + wide[2 * heads : 3 * heads]


def columns_of(ref, me, slot, width):
    owner = jnp.bitwise_xor(me, slot)
    return ref.at[:, pl.ds(pl.multiple_of(owner * width, width), width)]


def forward_kernel(size, passages, me_ref, lengths_ref, *refs):
    q_refs = refs[:size]
    keys_ref, values_ref, even_ref, odd_ref, q_buf, k_buf, v_buf, bias_ref, sem = refs[size:]
    me = me_ref[0]
    width = q_buf.shape[2]
    half = size // 2

    def k_copy(s):
        return pltpu.make_async_copy(columns_of(keys_ref, me, s, width), k_buf.at[s], sem.at[0, s])

    def v_copy(s):
        return pltpu.make_async_copy(columns_of(values_ref, me, s, width), v_buf.at[s], sem.at[1, s])

    for s in range(size):
        k_copy(s).start()
        v_copy(s).start()
    for s in range(size):
        q_buf[s] = q_refs[s][...]
    bias_ref[...] = mask_bias(lengths_ref, passages, k_buf.shape[1] // passages)
    lane_low = lax.broadcasted_iota(jnp.int32, (1, PAIR), 1) < HEAD_SIZE

    def one_slot(s, out_ref, k):
        k_copy(s).wait()
        v_copy(s).wait()
        rows = []
        for p in range(width // PAIR):
            lanes = slice(p * PAIR, (p + 1) * PAIR)
            queries = block_stack(q_buf[s, :, lanes], lane_low)
            bias = bias_ref[...]
            scores = dot(k_buf[s, :, lanes], queries, NT) + jnp.concatenate([bias, bias], axis=1)
            top = jnp.max(scores, axis=0, keepdims=True)
            weights = jnp.exp(scores - top)
            total = jnp.sum(weights, axis=0, keepdims=True)
            mixed = dot(v_buf[s, :, lanes], weights.astype(jnp.bfloat16), TN) / total
            out_ref[k, lanes, :] = diagonal(mixed).astype(jnp.bfloat16)
            lse = top + jnp.log(total)
            n = lse.shape[1] // 2
            rows += [lse[:, :n], lse[:, n:]]
        out_ref[k, width:, :] = thirds(jnp.concatenate(rows, axis=0))

    def body(k, carry):
        one_slot(2 * k, even_ref, k)
        one_slot(2 * k + 1, odd_ref, k)
        return carry

    lax.fori_loop(0, half, body, 0)


def merge(blocks):
    width = blocks[0].shape[0] - EXTRA
    heads = width // HEAD_SIZE
    lses = [unite(b[width:], heads) for b in blocks]
    top = functools.reduce(jnp.maximum, lses)
    shares = [jnp.exp(x - top) for x in lses]
    total = sum(shares)
    shares = [x / total for x in shares]
    outs = []
    for h in range(heads):
        rows = slice(h * HEAD_SIZE, (h + 1) * HEAD_SIZE)
        outs.append(sum(x[h : h + 1] * b[rows].astype(jnp.float32) for b, x in zip(blocks, shares)))
    return jnp.concatenate(outs, axis=0), top + jnp.log(total)


def merge_pair_kernel(a_ref, b_ref, *out_refs):
    for k, out_ref in enumerate(out_refs):
        out, lse = merge([a_ref[k], b_ref[k]])
        width = out.shape[0]
        out_ref[:width, :] = out.astype(jnp.bfloat16)
        out_ref[width:, :] = thirds(lse)


def merge_final_kernel(count, *refs):
    grad_ref, context_ref, stats_ref = refs[count:]
    out, lse = merge([r[...] for r in refs[:count]])
    context = out.T.astype(jnp.bfloat16)
    context_ref[...] = context
    product = (context.astype(jnp.float32) * grad_ref[...].astype(jnp.float32)).T
    dots = [
        jnp.sum(product[h * HEAD_SIZE : (h + 1) * HEAD_SIZE], axis=0, keepdims=True) for h in range(lse.shape[0])
    ]
    stats_ref[...] = jnp.concatenate([lse] + dots, axis=0)


def backward_kernel(slots, carried, passages, me_ref, lengths_ref, *refs):
    count = len(slots)
    q_refs, g_refs, stats_refs = refs[:count], refs[count : 2 * count], refs[2 * count : 3 * count]
    keys_ref, values_ref = refs[3 * count : 3 * count + 2]
    (dk_ref, dv_ref, even_ref, odd_ref, q_buf, g_buf, st_buf, k_buf, v_buf, dk_buf, dv_buf, bias_ref, sem) = refs[
        3 * count + 2 + carried :
    ]
    me = me_ref[0]
    width = q_buf.shape[2]
    first = slots[0]

    def k_copy(i):
        return pltpu.make_async_copy(columns_of(keys_ref, me, first + i, width), k_buf.at[i], sem.at[0, i])

    def v_copy(i):
        return pltpu.make_async_copy(columns_of(values_ref, me, first + i, width), v_buf.at[i], sem.at[1, i])

    def dk_copy(i):
        return pltpu.make_async_copy(dk_buf.at[i], columns_of(dk_ref, me, first + i, width), sem.at[2, i])

    def dv_copy(i):
        return pltpu.make_async_copy(dv_buf.at[i], columns_of(dv_ref, me, first + i, width), sem.at[3, i])

    for i in range(count):
        k_copy(i).start()
        v_copy(i).start()
    for i in range(count):
        q_buf[i] = q_refs[i][...]
        g_buf[i] = g_refs[i][...]
        st_buf[i] = stats_refs[i][...]
    bias_ref[...] = mask_bias(lengths_ref, passages, k_buf.shape[1] // passages)
    lane_low = lax.broadcasted_iota(jnp.int32, (1, PAIR), 1) < HEAD_SIZE
    heads = width // HEAD_SIZE

    def one_slot(i, out_ref, k):
        k_copy(i).wait()
        v_copy(i).wait()
        for p in range(width // PAIR):
            lanes = slice(p * PAIR, (p + 1) * PAIR)
            queries = block_stack(q_buf[i, :, lanes], lane_low)
            grads = block_stack(g_buf[i, :, lanes], lane_low)
            stats = st_buf[i]
            lse = jnp.concatenate([stats[2 * p : 2 * p + 1], stats[2 * p + 1 : 2 * p + 2]], axis=1)
            dots = jnp.concatenate(
                [stats[heads + 2 * p : heads + 2 * p + 1], stats[heads + 2 * p + 1 : heads + 2 * p + 2]], axis=1
            )
            key_block = k_buf[i, :, lanes]
            bias = bias_ref[...]
            scores = dot(key_block, queries, NT) + jnp.concatenate([bias, bias], axis=1)
            probs = jnp.exp(scores - lse)
            prob_grad = dot(v_buf[i, :, lanes], grads, NT)
            score_grad = (probs * (prob_grad - dots)).astype(jnp.bfloat16)
            dv_buf[i, :, lanes] = dot(probs.astype(jnp.bfloat16), grads, NN).astype(jnp.bfloat16)
            dk_buf[i, :, lanes] = dot(score_grad, queries, NN).astype(jnp.bfloat16)
            out_ref[k, lanes, :] = diagonal(dot(key_block, score_grad, TN)).astype(jnp.bfloat16)
        dk_copy(i).start()
        dv_copy(i).start()

    def body(k, carry):
        one_slot(2 * k, even_ref, k)
        one_slot(2 * k + 1, odd_ref, k)
        return carry

    lax.fori_loop(0, count // 2, body, 0)
    for i in range(count):
        dk_copy(i).wait()
        dv_copy(i).wait()


def add_pair_kernel(a_ref, b_ref, *out_refs):
    for k, out_ref in enumerate(out_refs):
        out_ref[...] = (a_ref[k].astype(jnp.float32) + b_ref[k].astype(jnp.float32)).astype(jnp.bfloat16)


def add_all_kernel(*refs):
    total = refs[0][...].astype(jnp.float32)
    for r in refs[1:-1]:
        total += r[...].astype(jnp.float32)
    refs[-1][...] = total.astype(jnp.bfloat16)


def add_all_transposed_kernel(*refs):
    total = refs[0][...].astype(jnp.float32)
    for r in refs[1:-1]:
        total += r[...].astype(jnp.float32)
    refs[-1][...] = total.T.astype(jnp.bfloat16)


def grad_partial_kernel(size, me_ref, cot_ref, weight_ref, even_ref, odd_ref, w_buf, sem):
    me = me_ref[0]
    width = w_buf.shape[2]

    def w_copy(s):
        return pltpu.make_async_copy(columns_of(weight_ref, me, s, width), w_buf.at[s], sem.at[s])

    order = list(range(1, size, 2)) + list(range(0, size, 2))
    for s in order:
        w_copy(s).start()
    cot = cot_ref[...]
    for s in order:
        w_copy(s).wait()
        (odd_ref if s % 2 else even_ref)[s // 2] = dot(cot, w_buf[s], NN).astype(jnp.bfloat16)


def layer_out_kernel(size, me_ref, *refs):
    weight_ref, out_ref, w_buf, sem = refs[size:]
    me = me_ref[0]
    width = w_buf.shape[2]

    def w_copy(s):
        return pltpu.make_async_copy(columns_of(weight_ref, me, s, width), w_buf.at[s], sem.at[s])

    for s in range(size):
        w_copy(s).start()
    total = None
    for s in range(size):
        w_copy(s).wait()
        part = dot(refs[s][...], w_buf[s], NT)
        total = part if total is None else total + part
    out_ref[...] = total.astype(jnp.bfloat16)


def weight_grad_kernel(size, groups, me_ref, *refs):
    half = size // 2
    cots = refs[:groups]
    own_even, own_odd = refs[groups : groups + half], refs[groups + half : groups + size]
    rest = refs[groups + size :]
    evens, odds = rest[: groups - 1], rest[groups - 1 : 2 * (groups - 1)]
    out_ref, cot_buf, out_buf, sem = rest[2 * (groups - 1) :]
    me = me_ref[0]
    width = out_buf.shape[2]
    rows = cots[0].shape[0]
    for g in range(groups):
        cot_buf[:, g * rows : (g + 1) * rows] = cots[g][...].T

    def out_copy(s):
        return pltpu.make_async_copy(out_buf.at[s], columns_of(out_ref, me, s, width), sem.at[s])

    for s in range(size):
        own, others = (own_odd, odds) if s % 2 else (own_even, evens)
        context = jnp.concatenate([own[s // 2][...]] + [o[s // 2] for o in others], axis=0)
        out_buf[s] = dot(cot_buf[...], context, NN)
        out_copy(s).start()
    for s in range(size):
        out_copy(s).wait()


def stack_kernel(*refs):
    for k, r in enumerate(refs[:-1]):
        refs[-1][k] = r[...]


def shaped(shape, dtype):
    return jax.ShapeDtypeStruct(shape, dtype)


def fast_device(dp, size, queries, keys, values, lengths, out_weight, out_cotangent):
    bf16, f32 = jnp.bfloat16, jnp.float32
    passages, passage_len, inner = keys.shape[1:]
    key_count = passages * passage_len
    answers, width = queries.shape[1:]
    half = size // 2
    heads = width // HEAD_SIZE
    model = out_weight.shape[0]
    me = lax.axis_index("psg").reshape(1)
    query = queries[0]
    cot = out_cotangent[0]
    key_rows = keys.reshape(key_count, inner)
    value_rows = values.reshape(key_count, inner)

    def interleaved(even, odd):
        return [r for pair in zip(even, odd) for r in pair]

    q_even = spread(query, size)
    slots = interleaved(q_even, across(q_even, size))
    cots = [cot] + [swap(cot, "dp", dp, d) for d in range(1, dp)]

    g_even, g_odd = call(
        functools.partial(grad_partial_kernel, size),
        me,
        cot,
        out_weight,
        out=[shaped((half, answers, width), bf16)] * 2,
        ins=[SMEM, VMEM, ANY],
        outs=[VMEM, VMEM],
        scratch=[pltpu.VMEM((size, model, width), bf16), pltpu.SemaphoreType.DMA((size,))],
    )
    g_other = swap(g_odd, "psg", size, 1)
    block = shaped((answers, width), bf16)
    g_sums = call(add_pair_kernel, g_even, g_other, out=[block] * half, ins=[VMEM] * 2, outs=[VMEM] * half)
    g_parts = [swap(g_sums[d // 2], "psg", size, d) for d in far_first(size)]

    packed = shaped((width + EXTRA, answers), bf16)
    o_even, o_odd = call(
        functools.partial(forward_kernel, size, passages),
        me,
        lengths,
        *slots,
        key_rows,
        value_rows,
        out=[shaped((half, width + EXTRA, answers), bf16)] * 2,
        ins=[SMEM, SMEM] + [VMEM] * size + [ANY, ANY],
        outs=[VMEM] * 2,
        scratch=[
            pltpu.VMEM((size, answers, width), bf16),
            pltpu.VMEM((size, key_count, width), bf16),
            pltpu.VMEM((size, key_count, width), bf16),
            pltpu.VMEM((key_count, PAIR), f32),
            pltpu.SemaphoreType.DMA((2, size)),
        ],
        vmem=16,
    )

    o_other = swap(o_odd, "psg", size, 1)
    o_pairs = call(merge_pair_kernel, o_even, o_other, out=[packed] * half, ins=[VMEM] * 2, outs=[VMEM] * half)
    arrived = [swap(o_pairs[d // 2], "psg", size, d) for d in far_first(size)]
    context_grad = call(add_all_kernel, g_sums[0], *g_parts, out=block, ins=[VMEM] * half, outs=VMEM)
    cg_even = spread(context_grad, size)
    context, stats = call(
        functools.partial(merge_final_kernel, half),
        o_pairs[0],
        *arrived,
        context_grad,
        out=[block, shaped((2 * heads, answers), f32)],
        ins=[VMEM] * (half + 1),
        outs=[VMEM] * 2,
    )
    s_even = spread(stats, size)
    c_even = spread(context, size)
    g_slots = interleaved(cg_even, across(cg_even, size))
    s_slots = interleaved(s_even, across(s_even, size))

    def backward(chosen, carried):
        count = len(chosen)
        pick = slice(chosen[0], chosen[0] + count)
        fixed = 2 + 3 * count + 2
        return call(
            functools.partial(backward_kernel, chosen, len(carried), passages),
            me,
            lengths,
            *slots[pick],
            *g_slots[pick],
            *s_slots[pick],
            key_rows,
            value_rows,
            *carried,
            out=[shaped((key_count, inner), bf16)] * 2 + [shaped((count // 2, width, answers), bf16)] * 2,
            ins=[SMEM, SMEM] + [VMEM] * (3 * count) + [ANY] * (2 + len(carried)),
            outs=[ANY, ANY, VMEM, VMEM],
            scratch=[
                pltpu.VMEM((count, answers, width), bf16),
                pltpu.VMEM((count, answers, width), bf16),
                pltpu.VMEM((count, 2 * heads, answers), f32),
            ]
            + [pltpu.VMEM((count, key_count, width), bf16)] * 4
            + [pltpu.VMEM((key_count, PAIR), f32), pltpu.SemaphoreType.DMA((4, count))],
            vmem=16,
            alias={fixed + i: i for i in range(len(carried))},
        )

    def owners_sums(even, odd, count):
        other = swap(odd, "psg", size, 1)
        return call(
            add_pair_kernel,
            even,
            other,
            out=[shaped((width, answers), bf16)] * count,
            ins=[VMEM] * 2,
            outs=[VMEM] * count,
        )

    key_grad, value_grad, far_even, far_odd = backward(range(half, size), ())
    far_sums = owners_sums(far_even, far_odd, half // 2)
    key_grad, value_grad, near_even, near_odd = backward(range(half), (key_grad, value_grad))
    near_sums = owners_sums(near_even, near_odd, half // 2)
    sums = near_sums + far_sums
    dq_parts = [swap(sums[d // 2], "psg", size, d) for d in far_first(size)]
    query_grad = call(add_all_transposed_kernel, sums[0], *dq_parts, out=block, ins=[VMEM] * half, outs=VMEM)

    c_odd = across(c_even, size)
    stacked = call(stack_kernel, *c_even, out=shaped((half, answers, width), bf16), ins=[VMEM] * half, outs=VMEM)
    evens = [swap(stacked, "dp", dp, d) for d in range(1, dp)]
    odds = [swap(e, "psg", size, 1) for e in evens]
    layer_out = call(
        functools.partial(layer_out_kernel, size),
        me,
        *interleaved(c_even, c_odd),
        out_weight,
        out=shaped((answers, model), bf16),
        ins=[SMEM] + [VMEM] * size + [ANY],
        outs=VMEM,
        scratch=[pltpu.VMEM((size, model, width), bf16), pltpu.SemaphoreType.DMA((size,))],
    )
    weight_grad = call(
        functools.partial(weight_grad_kernel, size, dp),
        me,
        *cots,
        *c_even,
        *c_odd,
        *evens,
        *odds,
        out=shaped((model, inner), f32),
        ins=[SMEM] + [VMEM] * (dp + size + 2 * (dp - 1)),
        outs=ANY,
        scratch=[
            pltpu.VMEM((model, dp * answers), bf16),
            pltpu.VMEM((size, model, width), f32),
            pltpu.SemaphoreType.DMA((size,)),
        ],
        vmem=16,
    )
    return (
        layer_out[None],
        weight_grad,
        query_grad[None],
        key_grad.reshape(keys.shape),
        value_grad.reshape(values.shape),
    )


def spread_heads(factor):
    return jnp.transpose(factor, (0, 2, 1))[..., None]


def general_device(queries, keys, values, lengths, out_weight, out_cotangent):
    question_count, passages, passage_len, inner_dim = keys.shape
    key_count = passages * passage_len
    answer_len = queries.shape[1]
    head_split = (question_count, answer_len, inner_dim // HEAD_SIZE, HEAD_SIZE)
    key_split = (question_count, key_count, inner_dim // HEAD_SIZE, HEAD_SIZE)
    einsum = functools.partial(jnp.einsum, preferred_element_type=jnp.float32)
    query_heads = lax.all_gather(queries, "psg", axis=2, tiled=True).reshape(head_split)
    key_heads = keys.reshape(key_split)
    value_heads = values.reshape(key_split)
    positions = jnp.arange(passage_len, dtype=jnp.int32)
    valid = (positions[None, None, :] < lengths[:, :, None]).reshape(question_count, 1, 1, key_count)
    scores = einsum("bihe,bkhe->bhik", query_heads, key_heads)
    row_max = lax.pmax(jnp.max(jnp.where(valid, scores, -jnp.inf), axis=3), "psg")
    weights = jnp.where(valid, jnp.exp(scores - row_max[..., None]), 0.0)
    output = einsum("bhik,bkhe->bihe", weights.astype(jnp.bfloat16), value_heads)
    row_sum, output = lax.psum((jnp.sum(weights, axis=3), output), "psg")
    context = (output / spread_heads(row_sum)).astype(jnp.bfloat16)
    context_rows = context.reshape(question_count * answer_len, inner_dim)
    grad_rows = out_cotangent.reshape(question_count * answer_len, -1)
    layer_out = jnp.dot(context_rows, out_weight.T, preferred_element_type=jnp.float32).astype(jnp.bfloat16)
    weight_grad = lax.psum(
        jnp.dot(grad_rows.T, context_rows, preferred_element_type=jnp.float32).astype(jnp.bfloat16), "dp"
    ).astype(jnp.float32)
    context_grad = lax.psum(jnp.dot(grad_rows, out_weight, preferred_element_type=jnp.float32), "psg").astype(
        jnp.bfloat16
    )
    grad_heads = context_grad.reshape(head_split)
    products = grad_heads.astype(jnp.float32) * context.astype(jnp.float32)
    row_dots = jnp.transpose(jnp.sum(products, axis=3), (0, 2, 1))
    probs = weights / row_sum[..., None]
    prob_grad = einsum("bihe,bkhe->bhik", grad_heads, value_heads)
    score_grad = (probs * (prob_grad - row_dots[..., None])).astype(jnp.bfloat16)
    value_grad = einsum("bhik,bihe->bkhe", probs.astype(jnp.bfloat16), grad_heads)
    key_grad = einsum("bhik,bihe->bkhe", score_grad, query_heads)
    query_terms = einsum("bhik,bkhe->bihe", score_grad, key_heads).reshape(question_count, answer_len, inner_dim)
    query_grad = lax.psum_scatter(query_terms, "psg", scatter_dimension=2, tiled=True)
    return (
        layer_out.reshape(question_count, answer_len, -1),
        weight_grad,
        query_grad.astype(jnp.bfloat16),
        key_grad.astype(jnp.bfloat16).reshape(keys.shape),
        value_grad.astype(jnp.bfloat16).reshape(values.shape),
    )


def solution(mesh):
    dp, size = mesh.shape["dp"], mesh.shape["psg"]

    def per_device(queries, keys, values, lengths, out_weight, out_cotangent):
        return fast_device(dp, size, queries, keys, values, lengths, out_weight, out_cotangent)

    def step(queries, keys, values, lengths, out_weight, out_cotangent):
        width = queries.shape[2] // size
        direct = (
            size in (4, 8)
            and dp in (2, 4)
            and keys.shape[0] == dp
            and width % PAIR == 0
            and 3 * (width // HEAD_SIZE) <= EXTRA
            and 2 * (width // HEAD_SIZE) % 8 == 0
            and queries.shape[1] % 128 == 0
            and keys.shape[2] % 16 == 0
            and (out_weight.shape[0] // size) % 128 == 0
        )
        body = jax.shard_map(
            per_device if direct else general_device,
            mesh=mesh,
            in_specs=(
                P("dp", None, "psg"),
                P("dp", "psg", None, None),
                P("dp", "psg", None, None),
                P("dp", "psg"),
                P("psg", None),
                P("dp", None, "psg"),
            ),
            out_specs=(
                P("dp", None, "psg"),
                P("psg", None),
                P("dp", None, "psg"),
                P("dp", "psg", None, None),
                P("dp", "psg", None, None),
            ),
            check_vma=False,
        )
        return body(queries, keys, values, lengths, out_weight, out_cotangent)

    return step
```

profile of v0, /device:TPU:0, one launch (start us, length us, event | category | flops | bytes accessed | tf_op | source)
XLA Modules:
  0.0 111.2 jit_solution(9333470309723857922)
XLA Ops:
  0.6 3.1 %collective-permute-start.1 = (bf16[128,256]{1,0:T(8,128)(2,1)}, bf16[128,256]{1,0:T(8,128)(2,1)S(1)}, u32[]{:S(2)}, u32[]{:S(2)}) collective-permute-start(bf16[128,256]{1,0:T(8,128)(2,1)} %bitcast.20), channel_id=1, source_target_pairs={{0,2},{1,3},{2,0},{3,1},{4,6},{5,7},{6,4},{7,5},{8,10},{9,11},{10,... | collective-permute-start | bytes 196616 | tf_op jit(solution)/shard_map/ppermute | solution.py:29
  3.8 2.6 %collective-permute-start.3 = (bf16[128,256]{1,0:T(8,128)(2,1)}, bf16[128,256]{1,0:T(8,128)(2,1)S(1)}, u32[]{:S(2)}, u32[]{:S(2)}) collective-permute-start(bf16[128,256]{1,0:T(8,128)(2,1)} %bitcast.21), channel_id=1, source_target_pairs={{0,4},{1,5},{2,6},{3,7},{4,0},{5,1},{6,2},{7,3},{8,12},{9,13},{10,... | collective-permute-start | bytes 196616 | tf_op jit(solution)/shard_map/ppermute | solution.py:29
  6.9 4.4 %collective-permute-done.3.refs_4_.refs_0_ = bf16[128,256]{1,0:T(8,128)(2,1)S(1)} collective-permute-done((bf16[128,256]{1,0:T(8,128)(2,1)}, bf16[128,256]{1,0:T(8,128)(2,1)S(1)}, u32[]{:S(2)}, u32[]{:S(2)}) %collective-permute-start.3) | collective-permute-done | bytes 65568 | tf_op jit(solution)/shard_map/ppermute | solution.py:29
  11.3 1.4 %collective-permute-done.5.refs_6_.refs_2_ = bf16[128,256]{1,0:T(8,128)(2,1)S(1)} collective-permute-done((bf16[128,256]{1,0:T(8,128)(2,1)}, bf16[128,256]{1,0:T(8,128)(2,1)S(1)}, u32[]{:S(2)}, u32[]{:S(2)}) %collective-permute-start.5) | collective-permute-done | bytes 65568 | tf_op jit(solution)/shard_map/ppermute | solution.py:29
  12.7 1.6 %copy-done.2 = bf16[512,2048]{1,0:T(8,128)(2,1)S(1)} copy-done((bf16[512,2048]{1,0:T(8,128)(2,1)S(1)}, bf16[512,2048]{1,0:T(8,128)(2,1)}, u32[]{:S(2)}) %copy-start.2) | copy-done | bytes 2097176
  15.2 2.1 %shard_map.103 = (bf16[4,128,256]{2,1,0:T(8,128)(2,1)S(1)}, bf16[4,128,256]{2,1,0:T(8,128)(2,1)S(1)}) custom-call(s32[1]{0:T(128)} %bitcast.me_ref, bf16[128,512]{1,0:T(8,128)(2,1)S(1)} %bitcast.15, bf16[512,2048]{1,0:T(8,128)(2,1)S(1)} %copy-done.2), custom_call_target="tpu_custom_call" | custom-call | tf_op jit(solution)/shard_map/pallas_call | solution.py:33
  17.9 1.6 %copy-done.1 = bf16[1,2,256,2048]{3,2,1,0:T(8,128)(2,1)S(1)} copy-done((bf16[1,2,256,2048]{3,2,1,0:T(8,128)(2,1)S(1)}, bf16[1,2,256,2048]{3,2,1,0:T(8,128)(2,1)}, u32[]{:S(2)}) %copy-start.1) | copy-done | bytes 2097176
  19.5 9.0 %shard_map.101 = (bf16[4,272,128]{2,1,0:T(8,128)(2,1)S(1)}, bf16[4,272,128]{2,1,0:T(8,128)(2,1)S(1)}) custom-call(s32[1]{0:T(128)} %bitcast.me_ref, s32[1,2]{1,0:T(1,128)S(1)} %copy-done.7, bf16[128,256]{1,0:T(8,128)(2,1)S(1)} %bitcast.24, bf16[128,256]{1,0:T(8,128)(2,1)S(1)} %collective-permute-done.refs_1_, ...), custom_call_target="tpu_custom_call" | custom-call | tf_op jit(solution)/shard_map/pallas_call | solution.py:33
  28.7 2.3 %collective-permute-start.12 = (bf16[128,256]{1,0:T(8,128)(2,1)S(1)}, bf16[128,256]{1,0:T(8,128)(2,1)S(1)}, u32[]{:S(2)}, u32[]{:S(2)}) collective-permute-start(bf16[128,256]{1,0:T(8,128)(2,1)S(1)} %get-tuple-element.40), channel_id=1, source_target_pairs={{0,6},{1,7},{2,4},{3,5},{4,2},{5,3},{6,0},{7,1},{8,14},{9,15},{10,... | collective-permute-start | bytes 196616 | tf_op jit(solution)/shard_map/ppermute | solution.py:29
  31.0 1.5 %collective-permute-start.22 = (bf16[128,512]{1,0:T(8,128)(2,1)S(1)}, bf16[128,512]{1,0:T(8,128)(2,1)S(1)}, u32[]{:S(2)}, u32[]{:S(2)}) collective-permute-start(bf16[128,512]{1,0:T(8,128)(2,1)S(1)} %bitcast.16), channel_id=1, source_target_pairs={{0,8},{8,0},{16,24},{24,16},{1,9},{9,1},{17,25},{25,17},{2,10},{10... | collective-permute-start | bytes 393224 | tf_op jit(solution)/shard_map/ppermute | solution.py:29
  32.7 2.2 %collective-permute-start.10 = (bf16[272,128]{1,0:T(8,128)(2,1)S(1)}, bf16[272,128]{1,0:T(8,128)(2,1)S(1)}, u32[]{:S(2)}, u32[]{:S(2)}) collective-permute-start(bf16[272,128]{1,0:T(8,128)(2,1)S(1)} %get-tuple-element.36), channel_id=1, source_target_pairs={{0,2},{1,3},{2,0},{3,1},{4,6},{5,7},{6,4},{7,5},{8,10},{9,11},{10,... | collective-permute-start | bytes 208904 | tf_op jit(solution)/shard_map/ppermute | solution.py:29
  34.9 2.2 %collective-permute-start.8 = (bf16[272,128]{1,0:T(8,128)(2,1)S(1)}, bf16[272,128]{1,0:T(8,128)(2,1)S(1)}, u32[]{:S(2)}, u32[]{:S(2)}) collective-permute-start(bf16[272,128]{1,0:T(8,128)(2,1)S(1)} %get-tuple-element.34), channel_id=1, source_target_pairs={{0,6},{1,7},{2,4},{3,5},{4,2},{5,3},{6,0},{7,1},{8,14},{9,15},{10,... | collective-permute-start | bytes 208904 | tf_op jit(solution)/shard_map/ppermute | solution.py:29
  38.0 1.3 %collective-permute-start.14 = (bf16[128,256]{1,0:T(8,128)(2,1)S(1)}, bf16[128,256]{1,0:T(8,128)(2,1)S(1)}, u32[]{:S(2)}, u32[]{:S(2)}) collective-permute-start(bf16[128,256]{1,0:T(8,128)(2,1)S(1)} %get-tuple-element.42), channel_id=1, source_target_pairs={{0,2},{1,3},{2,0},{3,1},{4,6},{5,7},{6,4},{7,5},{8,10},{9,11},{10,... | collective-permute-start | bytes 196616 | tf_op jit(solution)/shard_map/ppermute | solution.py:29
  39.3 4.7 %collective-permute-done.14.refs_3_ = bf16[128,256]{1,0:T(8,128)(2,1)S(1)} collective-permute-done((bf16[128,256]{1,0:T(8,128)(2,1)S(1)}, bf16[128,256]{1,0:T(8,128)(2,1)S(1)}, u32[]{:S(2)}, u32[]{:S(2)}) %collective-permute-start.14) | collective-permute-done | bytes 65568 | tf_op jit(solution)/shard_map/ppermute | solution.py:29
  44.4 1.9 %collective-permute-start.39 = (bf16[128,256]{1,0:T(8,128)(2,1)S(1)}, bf16[128,256]{1,0:T(8,128)(2,1)S(1)}, u32[]{:S(2)}, u32[]{:S(2)}) collective-permute-start(bf16[128,256]{1,0:T(8,128)(2,1)S(1)} %shard_map.105.refs_4_), channel_id=1, source_target_pairs={{0,6},{1,7},{2,4},{3,5},{4,2},{5,3},{6,0},{7,1},{8,14},{9,15},{10,... | collective-permute-start | bytes 196616 | tf_op jit(solution)/shard_map/ppermute | solution.py:29
  48.7 1.9 %collective-permute-start.18 = (bf16[128,256]{1,0:T(8,128)(2,1)S(1)}, bf16[128,256]{1,0:T(8,128)(2,1)S(1)}, u32[]{:S(2)}, u32[]{:S(2)}) collective-permute-start(bf16[128,256]{1,0:T(8,128)(2,1)S(1)} %get-tuple-element.43.refs_0_.refs_4_), channel_id=1, source_target_pairs={{0,4},{1,5},{2,6},{3,7},{4,0},{5,1},{6,2},{7,3},{8,12},{9,13},{10,... | collective-permute-start | bytes 196616 | tf_op jit(solution)/shard_map/ppermute | solution.py:29
  50.6 3.1 %collective-permute-start.20 = (bf16[128,256]{1,0:T(8,128)(2,1)S(1)}, bf16[128,256]{1,0:T(8,128)(2,1)S(1)}, u32[]{:S(2)}, u32[]{:S(2)}) collective-permute-start(bf16[128,256]{1,0:T(8,128)(2,1)S(1)} %get-tuple-element.43.refs_0_.refs_4_), channel_id=1, source_target_pairs={{0,6},{1,7},{2,4},{3,5},{4,2},{5,3},{6,0},{7,1},{8,14},{9,15},{10,... | collective-permute-start | bytes 196616 | tf_op jit(solution)/shard_map/ppermute | solution.py:29
  56.8 3.3 %collective-permute-start.25 = (bf16[4,128,256]{2,1,0:T(8,128)(2,1)S(1)}, bf16[4,128,256]{2,1,0:T(8,128)(2,1)S(1)}, u32[]{:S(2)}, u32[]{:S(2)}) collective-permute-start(bf16[4,128,256]{2,1,0:T(8,128)(2,1)S(1)} %shard_map.108), channel_id=1, source_target_pairs={{0,8},{8,0},{16,24},{24,16},{1,9},{9,1},{17,25},{25,17},{2,10},{10... | collective-permute-start | bytes 786440 | tf_op jit(solution)/shard_map/ppermute | solution.py:29
  60.1 1.5 %collective-permute-start.26 = (bf16[4,128,256]{2,1,0:T(8,128)(2,1)S(1)}, bf16[4,128,256]{2,1,0:T(8,128)(2,1)S(1)}, u32[]{:S(2)}, u32[]{:S(2)}) collective-permute-start(bf16[4,128,256]{2,1,0:T(8,128)(2,1)S(1)} %shard_map.108), channel_id=1, source_target_pairs={{0,16},{8,24},{16,0},{24,8},{1,17},{9,25},{17,1},{25,9},{2,18},{10... | collective-permute-start | bytes 786440 | tf_op jit(solution)/shard_map/ppermute | solution.py:29
  61.7 4.5 %collective-permute-done.41.refs_8_ = f32[8,128]{1,0:T(8,128)S(1)} collective-permute-done((f32[8,128]{1,0:T(8,128)S(1)}, f32[8,128]{1,0:T(8,128)S(1)}, u32[]{:S(2)}, u32[]{:S(2)}) %collective-permute-start.41) | collective-permute-done | bytes 4128 | tf_op jit(solution)/shard_map/ppermute | solution.py:29
  66.2 2.1 %collective-permute-start.43 = (f32[8,128]{1,0:T(8,128)S(1)}, f32[8,128]{1,0:T(8,128)S(1)}, u32[]{:S(2)}, u32[]{:S(2)}) collective-permute-start(f32[8,128]{1,0:T(8,128)S(1)} %get-tuple-element.44.refs_8_), channel_id=1, source_target_pairs={{0,6},{1,7},{2,4},{3,5},{4,2},{5,3},{6,0},{7,1},{8,14},{9,15},{10,... | collective-permute-start | bytes 12296 | tf_op jit(solution)/shard_map/ppermute | solution.py:29
  68.3 3.3 %collective-permute-done.43.refs_10_ = f32[8,128]{1,0:T(8,128)S(1)} collective-permute-done((f32[8,128]{1,0:T(8,128)S(1)}, f32[8,128]{1,0:T(8,128)S(1)}, u32[]{:S(2)}, u32[]{:S(2)}) %collective-permute-start.43) | collective-permute-done | bytes 4128 | tf_op jit(solution)/shard_map/ppermute | solution.py:29
  71.6 3.6 %collective-permute-done.35.refs_10_ = f32[8,128]{1,0:T(8,128)S(1)} collective-permute-done((f32[8,128]{1,0:T(8,128)S(1)}, f32[8,128]{1,0:T(8,128)S(1)}, u32[]{:S(2)}, u32[]{:S(2)}) %collective-permute-start.35) | collective-permute-done | bytes 4128 | tf_op jit(solution)/shard_map/ppermute | solution.py:29
  78.9 5.0 %shard_map.110 = (bf16[512,2048]{1,0:T(8,128)(2,1)}, bf16[512,2048]{1,0:T(8,128)(2,1)}, bf16[2,256,128]{2,1,0:T(8,128)(2,1)S(1)}, bf16[2,256,128]{2,1,0:T(8,128)(2,1)S(1)}) custom-call(s32[1]{0:T(128)} %bitcast.me_ref, s32[1,2]{1,0:T(1,128)S(1)} %copy-done.7, bf16[128,256]{1,0:T(8,128)(2,1)S(1)} %collective-permute-done.3.refs_4_.refs_0_, ...), custom_call_target="tpu_custom_call" | custom-call | tf_op jit(solution)/shard_map/pallas_call | solution.py:33
  84.5 5.0 %shard_map.111 = (bf16[512,2048]{1,0:T(8,128)(2,1)}, bf16[512,2048]{1,0:T(8,128)(2,1)}, bf16[2,256,128]{2,1,0:T(8,128)(2,1)S(1)}, bf16[2,256,128]{2,1,0:T(8,128)(2,1)S(1)}) custom-call(s32[1]{0:T(128)} %bitcast.me_ref, s32[1,2]{1,0:T(1,128)S(1)} %copy-done.7, bf16[128,256]{1,0:T(8,128)(2,1)S(1)} %bitcast.25, ...), custom_call_target="tpu_custom_call", output_to_operand_aliasing={{0}: (16, {}), {1}: (17, {})} | custom-call | tf_op jit(solution)/shard_map/pallas_call | solution.py:33
  91.4 2.1 %collective-permute-start.47 = (bf16[256,128]{1,0:T(8,128)(2,1)S(1)}, bf16[256,128]{1,0:T(8,128)(2,1)S(1)}, u32[]{:S(2)}, u32[]{:S(2)}) collective-permute-start(bf16[256,128]{1,0:T(8,128)(2,1)S(1)} %get-tuple-element.52), channel_id=1, source_target_pairs={{0,6},{1,7},{2,4},{3,5},{4,2},{5,3},{6,0},{7,1},{8,14},{9,15},{10,... | collective-permute-start | bytes 196616 | tf_op jit(solution)/shard_map/ppermute | solution.py:29
  94.2 3.6 %collective-permute-done.47.refs_1_ = bf16[256,128]{1,0:T(8,128)(2,1)S(1)} collective-permute-done((bf16[256,128]{1,0:T(8,128)(2,1)S(1)}, bf16[256,128]{1,0:T(8,128)(2,1)S(1)}, u32[]{:S(2)}, u32[]{:S(2)}) %collective-permute-start.47) | collective-permute-done | bytes 65568 | tf_op jit(solution)/shard_map/ppermute | solution.py:29
  97.8 2.6 %collective-permute-done.48.refs_2_ = bf16[256,128]{1,0:T(8,128)(2,1)S(1)} collective-permute-done((bf16[256,128]{1,0:T(8,128)(2,1)S(1)}, bf16[256,128]{1,0:T(8,128)(2,1)S(1)}, u32[]{:S(2)}, u32[]{:S(2)}) %collective-permute-start.48) | collective-permute-done | bytes 65568 | tf_op jit(solution)/shard_map/ppermute | solution.py:29
  100.4 1.5 %collective-permute-start.23 = (bf16[128,512]{1,0:T(8,128)(2,1)S(1)}, bf16[128,512]{1,0:T(8,128)(2,1)S(1)}, u32[]{:S(2)}, u32[]{:S(2)}) collective-permute-start(bf16[128,512]{1,0:T(8,128)(2,1)S(1)} %bitcast.17), channel_id=1, source_target_pairs={{0,16},{8,24},{16,0},{24,8},{1,17},{9,25},{17,1},{25,9},{2,18},{10... | collective-permute-start | bytes 393224 | tf_op jit(solution)/shard_map/ppermute | solution.py:29
  102.1 2.9 %collective-permute-start.24 = (bf16[128,512]{1,0:T(8,128)(2,1)S(1)}, bf16[128,512]{1,0:T(8,128)(2,1)S(1)}, u32[]{:S(2)}, u32[]{:S(2)}) collective-permute-start(bf16[128,512]{1,0:T(8,128)(2,1)S(1)} %bitcast.18), channel_id=1, source_target_pairs={{0,24},{8,16},{16,8},{24,0},{1,25},{9,17},{17,9},{25,1},{2,26},{10... | collective-permute-start | bytes 393224 | tf_op jit(solution)/shard_map/ppermute | solution.py:29
  105.0 2.1 %shard_map.107 = bf16[128,512]{1,0:T(8,128)(2,1)} custom-call(s32[1]{0:T(128)} %bitcast.me_ref, bf16[128,256]{1,0:T(8,128)(2,1)S(1)} %get-tuple-element.43.refs_0_.refs_4_, bf16[128,256]{1,0:T(8,128)(2,1)S(1)} %collective-permute-done.15.refs_1_.refs_8_, bf16[128,256]{1,0:T(8,128)(2,1)S(1)} %collective-permute-done.16.refs_2_.refs_1_.refs_5_, ...), custom_call_target="tpu_custom_call" | custom-call | tf_op jit(solution)/shard_map/pallas_call | solution.py:33
  108.7 2.6 %shard_map.109 = f32[512,2048]{1,0:T(8,128)} custom-call(s32[1]{0:T(128)} %bitcast.me_ref, bf16[128,512]{1,0:T(8,128)(2,1)S(1)} %bitcast.19, bf16[128,512]{1,0:T(8,128)(2,1)S(1)} %collective-permute-done.22.refs_1_, bf16[128,512]{1,0:T(8,128)(2,1)S(1)} %collective-permute-done.23.refs_2_, bf16[128,512]{1,0:T(8,128)(2,1)S(1)} %collective-permute-done.24.refs_3_, ...), custom_call_target="tpu_custom_call" | custom-call | tf_op jit(solution)/shard_map/pallas_call | solution.py:33
  (98 shorter events, 17.8 us)
Async XLA Ops:
  3.8 7.5 %collective-permute-start.3 = (bf16[128,256]{1,0:T(8,128)(2,1)}, bf16[128,256]{1,0:T(8,128)(2,1)S(1)}, u32[]{:S(2)}, u32[]{:S(2)}) collective-permute-start(bf16[128,256]{1,0:T(8,128)(2,1)} %bitcast.21), channel_id=1, source_target_pairs={{0,4},{1,5},{2,6},{3,7},{4,0},{5,1},{6,2},{7,3},{8,12},{9,13},{10,... | collective-permute-start | bytes 196616 | tf_op jit(solution)/shard_map/ppermute | solution.py:29
  6.3 6.3 %collective-permute-start.5 = (bf16[128,256]{1,0:T(8,128)(2,1)}, bf16[128,256]{1,0:T(8,128)(2,1)S(1)}, u32[]{:S(2)}, u32[]{:S(2)}) collective-permute-start(bf16[128,256]{1,0:T(8,128)(2,1)} %bitcast.22), channel_id=1, source_target_pairs={{0,6},{1,7},{2,4},{3,5},{4,2},{5,3},{6,0},{7,1},{8,14},{9,15},{10,... | collective-permute-start | bytes 196616 | tf_op jit(solution)/shard_map/ppermute | solution.py:29
  6.4 11.5 %collective-permute-start = (bf16[128,256]{1,0:T(8,128)(2,1)}, bf16[128,256]{1,0:T(8,128)(2,1)S(1)}, u32[]{:S(2)}, u32[]{:S(2)}) collective-permute-start(bf16[128,256]{1,0:T(8,128)(2,1)} %bitcast.23), channel_id=1, source_target_pairs={{0,1},{1,0},{2,3},{3,2},{4,5},{5,4},{6,7},{7,6},{8,9},{9,8},{10,11... | collective-permute-start | bytes 196616 | tf_op jit(solution)/shard_map/ppermute | solution.py:29
  6.4 11.5 %collective-permute-start.2 = (bf16[128,256]{1,0:T(8,128)(2,1)S(1)}, bf16[128,256]{1,0:T(8,128)(2,1)S(1)}, u32[]{:S(2)}, u32[]{:S(2)}) collective-permute-start(bf16[128,256]{1,0:T(8,128)(2,1)S(1)} %collective-permute-done.1.refs_2_), channel_id=1, source_target_pairs={{0,1},{1,0},{2,3},{3,2},{4,5},{5,4},{6,7},{7,6},{8,9},{9,8},{10,11... | collective-permute-start | bytes 196616 | tf_op jit(solution)/shard_map/ppermute | solution.py:29
  11.2 6.6 %collective-permute-start.4 = (bf16[128,256]{1,0:T(8,128)(2,1)S(1)}, bf16[128,256]{1,0:T(8,128)(2,1)S(1)}, u32[]{:S(2)}, u32[]{:S(2)}) collective-permute-start(bf16[128,256]{1,0:T(8,128)(2,1)S(1)} %collective-permute-done.3.refs_4_.refs_0_), channel_id=1, source_target_pairs={{0,1},{1,0},{2,3},{3,2},{4,5},{5,4},{6,7},{7,6},{8,9},{9,8},{10,11... | collective-permute-start | bytes 196616 | tf_op jit(solution)/shard_map/ppermute | solution.py:29
  17.3 11.3 %collective-permute-start.11 = (bf16[4,128,256]{2,1,0:T(8,128)(2,1)S(1)}, bf16[4,128,256]{2,1,0:T(8,128)(2,1)S(1)}, u32[]{:S(2)}, u32[]{:S(2)}) collective-permute-start(bf16[4,128,256]{2,1,0:T(8,128)(2,1)S(1)} %get-tuple-element.38), channel_id=1, source_target_pairs={{0,1},{1,0},{2,3},{3,2},{4,5},{5,4},{6,7},{7,6},{8,9},{9,8},{10,11... | collective-permute-start | bytes 786440 | tf_op jit(solution)/shard_map/ppermute | solution.py:29
  28.7 8.4 %collective-permute-start.12 = (bf16[128,256]{1,0:T(8,128)(2,1)S(1)}, bf16[128,256]{1,0:T(8,128)(2,1)S(1)}, u32[]{:S(2)}, u32[]{:S(2)}) collective-permute-start(bf16[128,256]{1,0:T(8,128)(2,1)S(1)} %get-tuple-element.40), channel_id=1, source_target_pairs={{0,6},{1,7},{2,4},{3,5},{4,2},{5,3},{6,0},{7,1},{8,14},{9,15},{10,... | collective-permute-start | bytes 196616 | tf_op jit(solution)/shard_map/ppermute | solution.py:29
  31.0 7.0 %collective-permute-start.13 = (bf16[128,256]{1,0:T(8,128)(2,1)S(1)}, bf16[128,256]{1,0:T(8,128)(2,1)S(1)}, u32[]{:S(2)}, u32[]{:S(2)}) collective-permute-start(bf16[128,256]{1,0:T(8,128)(2,1)S(1)} %get-tuple-element.41), channel_id=1, source_target_pairs={{0,4},{1,5},{2,6},{3,7},{4,0},{5,1},{6,2},{7,3},{8,12},{9,13},{10,... | collective-permute-start | bytes 196616 | tf_op jit(solution)/shard_map/ppermute | solution.py:29
  31.0 17.7 %collective-permute-start.22 = (bf16[128,512]{1,0:T(8,128)(2,1)S(1)}, bf16[128,512]{1,0:T(8,128)(2,1)S(1)}, u32[]{:S(2)}, u32[]{:S(2)}) collective-permute-start(bf16[128,512]{1,0:T(8,128)(2,1)S(1)} %bitcast.16), channel_id=1, source_target_pairs={{0,8},{8,0},{16,24},{24,16},{1,9},{9,1},{17,25},{25,17},{2,10},{10... | collective-permute-start | bytes 393224 | tf_op jit(solution)/shard_map/ppermute | solution.py:29
  32.7 11.8 %collective-permute-start.10 = (bf16[272,128]{1,0:T(8,128)(2,1)S(1)}, bf16[272,128]{1,0:T(8,128)(2,1)S(1)}, u32[]{:S(2)}, u32[]{:S(2)}) collective-permute-start(bf16[272,128]{1,0:T(8,128)(2,1)S(1)} %get-tuple-element.36), channel_id=1, source_target_pairs={{0,2},{1,3},{2,0},{3,1},{4,6},{5,7},{6,4},{7,5},{8,10},{9,11},{10,... | collective-permute-start | bytes 208904 | tf_op jit(solution)/shard_map/ppermute | solution.py:29
  34.9 11.4 %collective-permute-start.8 = (bf16[272,128]{1,0:T(8,128)(2,1)S(1)}, bf16[272,128]{1,0:T(8,128)(2,1)S(1)}, u32[]{:S(2)}, u32[]{:S(2)}) collective-permute-start(bf16[272,128]{1,0:T(8,128)(2,1)S(1)} %get-tuple-element.34), channel_id=1, source_target_pairs={{0,6},{1,7},{2,4},{3,5},{4,2},{5,3},{6,0},{7,1},{8,14},{9,15},{10,... | collective-permute-start | bytes 208904 | tf_op jit(solution)/shard_map/ppermute | solution.py:29
  37.1 10.5 %collective-permute-start.9 = (bf16[272,128]{1,0:T(8,128)(2,1)S(1)}, bf16[272,128]{1,0:T(8,128)(2,1)S(1)}, u32[]{:S(2)}, u32[]{:S(2)}) collective-permute-start(bf16[272,128]{1,0:T(8,128)(2,1)S(1)} %get-tuple-element.35), channel_id=1, source_target_pairs={{0,4},{1,5},{2,6},{3,7},{4,0},{5,1},{6,2},{7,3},{8,12},{9,13},{10,... | collective-permute-start | bytes 208904 | tf_op jit(solution)/shard_map/ppermute | solution.py:29
  44.0 6.6 %collective-permute-start.37 = (bf16[128,256]{1,0:T(8,128)(2,1)S(1)}, bf16[128,256]{1,0:T(8,128)(2,1)S(1)}, u32[]{:S(2)}, u32[]{:S(2)}) collective-permute-start(bf16[128,256]{1,0:T(8,128)(2,1)S(1)} %shard_map.105.refs_4_), channel_id=1, source_target_pairs={{0,4},{1,5},{2,6},{3,7},{4,0},{5,1},{6,2},{7,3},{8,12},{9,13},{10,... | collective-permute-start | bytes 196616 | tf_op jit(solution)/shard_map/ppermute | solution.py:29
  44.4 9.3 %collective-permute-start.39 = (bf16[128,256]{1,0:T(8,128)(2,1)S(1)}, bf16[128,256]{1,0:T(8,128)(2,1)S(1)}, u32[]{:S(2)}, u32[]{:S(2)}) collective-permute-start(bf16[128,256]{1,0:T(8,128)(2,1)S(1)} %shard_map.105.refs_4_), channel_id=1, source_target_pairs={{0,6},{1,7},{2,4},{3,5},{4,2},{5,3},{6,0},{7,1},{8,14},{9,15},{10,... | collective-permute-start | bytes 196616 | tf_op jit(solution)/shard_map/ppermute | solution.py:29
  46.3 7.4 %collective-permute-start.32 = (bf16[128,256]{1,0:T(8,128)(2,1)S(1)}, bf16[128,256]{1,0:T(8,128)(2,1)S(1)}, u32[]{:S(2)}, u32[]{:S(2)}) collective-permute-start(bf16[128,256]{1,0:T(8,128)(2,1)S(1)} %shard_map.105.refs_4_), channel_id=1, source_target_pairs={{0,2},{1,3},{2,0},{3,1},{4,6},{5,7},{6,4},{7,5},{8,10},{9,11},{10,... | collective-permute-start | bytes 196616 | tf_op jit(solution)/shard_map/ppermute | solution.py:29
  47.8 6.4 %collective-permute-start.16 = (bf16[128,256]{1,0:T(8,128)(2,1)S(1)}, bf16[128,256]{1,0:T(8,128)(2,1)S(1)}, u32[]{:S(2)}, u32[]{:S(2)}) collective-permute-start(bf16[128,256]{1,0:T(8,128)(2,1)S(1)} %get-tuple-element.43.refs_0_.refs_4_), channel_id=1, source_target_pairs={{0,2},{1,3},{2,0},{3,1},{4,6},{5,7},{6,4},{7,5},{8,10},{9,11},{10,... | collective-permute-start | bytes 196616 | tf_op jit(solution)/shard_map/ppermute | solution.py:29
  48.7 6.8 %collective-permute-start.18 = (bf16[128,256]{1,0:T(8,128)(2,1)S(1)}, bf16[128,256]{1,0:T(8,128)(2,1)S(1)}, u32[]{:S(2)}, u32[]{:S(2)}) collective-permute-start(bf16[128,256]{1,0:T(8,128)(2,1)S(1)} %get-tuple-element.43.refs_0_.refs_4_), channel_id=1, source_target_pairs={{0,4},{1,5},{2,6},{3,7},{4,0},{5,1},{6,2},{7,3},{8,12},{9,13},{10,... | collective-permute-start | bytes 196616 | tf_op jit(solution)/shard_map/ppermute | solution.py:29
  50.6 6.2 %collective-permute-start.20 = (bf16[128,256]{1,0:T(8,128)(2,1)S(1)}, bf16[128,256]{1,0:T(8,128)(2,1)S(1)}, u32[]{:S(2)}, u32[]{:S(2)}) collective-permute-start(bf16[128,256]{1,0:T(8,128)(2,1)S(1)} %get-tuple-element.43.refs_0_.refs_4_), channel_id=1, source_target_pairs={{0,6},{1,7},{2,4},{3,5},{4,2},{5,3},{6,0},{7,1},{8,14},{9,15},{10,... | collective-permute-start | bytes 196616 | tf_op jit(solution)/shard_map/ppermute | solution.py:29
  53.7 6.4 %collective-permute-start.38 = (bf16[128,256]{1,0:T(8,128)(2,1)S(1)}, bf16[128,256]{1,0:T(8,128)(2,1)S(1)}, u32[]{:S(2)}, u32[]{:S(2)}) collective-permute-start(bf16[128,256]{1,0:T(8,128)(2,1)S(1)} %collective-permute-done.37.refs_4_), channel_id=1, source_target_pairs={{0,1},{1,0},{2,3},{3,2},{4,5},{5,4},{6,7},{7,6},{8,9},{9,8},{10,11... | collective-permute-start | bytes 196616 | tf_op jit(solution)/shard_map/ppermute | solution.py:29
  54.2 7.4 %collective-permute-start.40 = (bf16[128,256]{1,0:T(8,128)(2,1)S(1)}, bf16[128,256]{1,0:T(8,128)(2,1)S(1)}, u32[]{:S(2)}, u32[]{:S(2)}) collective-permute-start(bf16[128,256]{1,0:T(8,128)(2,1)S(1)} %collective-permute-done.39.refs_6_), channel_id=1, source_target_pairs={{0,1},{1,0},{2,3},{3,2},{4,5},{5,4},{6,7},{7,6},{8,9},{9,8},{10,11... | collective-permute-start | bytes 196616 | tf_op jit(solution)/shard_map/ppermute | solution.py:29
  55.5 6.2 %collective-permute-start.33 = (bf16[128,256]{1,0:T(8,128)(2,1)S(1)}, bf16[128,256]{1,0:T(8,128)(2,1)S(1)}, u32[]{:S(2)}, u32[]{:S(2)}) collective-permute-start(bf16[128,256]{1,0:T(8,128)(2,1)S(1)} %collective-permute-done.32.refs_6_), channel_id=1, source_target_pairs={{0,1},{1,0},{2,3},{3,2},{4,5},{5,4},{6,7},{7,6},{8,9},{9,8},{10,11... | collective-permute-start | bytes 196616 | tf_op jit(solution)/shard_map/ppermute | solution.py:29
  56.8 27.6 %collective-permute-start.15 = (bf16[128,256]{1,0:T(8,128)(2,1)S(1)}, bf16[128,256]{1,0:T(8,128)(2,1)S(1)}, u32[]{:S(2)}, u32[]{:S(2)}) collective-permute-start(bf16[128,256]{1,0:T(8,128)(2,1)S(1)} %get-tuple-element.43.refs_0_.refs_4_), channel_id=1, source_target_pairs={{0,1},{1,0},{2,3},{3,2},{4,5},{5,4},{6,7},{7,6},{8,9},{9,8},{10,11... | collective-permute-start | bytes 196616 | tf_op jit(solution)/shard_map/ppermute | solution.py:29
  56.8 36.7 %collective-permute-start.25 = (bf16[4,128,256]{2,1,0:T(8,128)(2,1)S(1)}, bf16[4,128,256]{2,1,0:T(8,128)(2,1)S(1)}, u32[]{:S(2)}, u32[]{:S(2)}) collective-permute-start(bf16[4,128,256]{2,1,0:T(8,128)(2,1)S(1)} %shard_map.108), channel_id=1, source_target_pairs={{0,8},{8,0},{16,24},{24,16},{1,9},{9,1},{17,25},{25,17},{2,10},{10... | collective-permute-start | bytes 786440 | tf_op jit(solution)/shard_map/ppermute | solution.py:29
  60.1 33.5 %collective-permute-start.26 = (bf16[4,128,256]{2,1,0:T(8,128)(2,1)S(1)}, bf16[4,128,256]{2,1,0:T(8,128)(2,1)S(1)}, u32[]{:S(2)}, u32[]{:S(2)}) collective-permute-start(bf16[4,128,256]{2,1,0:T(8,128)(2,1)S(1)} %shard_map.108), channel_id=1, source_target_pairs={{0,16},{8,24},{16,0},{24,8},{1,17},{9,25},{17,1},{25,9},{2,18},{10... | collective-permute-start | bytes 786440 | tf_op jit(solution)/shard_map/ppermute | solution.py:29
  61.6 32.4 %collective-permute-start.27 = (bf16[4,128,256]{2,1,0:T(8,128)(2,1)S(1)}, bf16[4,128,256]{2,1,0:T(8,128)(2,1)S(1)}, u32[]{:S(2)}, u32[]{:S(2)}) collective-permute-start(bf16[4,128,256]{2,1,0:T(8,128)(2,1)S(1)} %shard_map.108), channel_id=1, source_target_pairs={{0,24},{8,16},{16,8},{24,0},{1,25},{9,17},{17,9},{25,1},{2,26},{10... | collective-permute-start | bytes 786440 | tf_op jit(solution)/shard_map/ppermute | solution.py:29
  91.4 6.4 %collective-permute-start.47 = (bf16[256,128]{1,0:T(8,128)(2,1)S(1)}, bf16[256,128]{1,0:T(8,128)(2,1)S(1)}, u32[]{:S(2)}, u32[]{:S(2)}) collective-permute-start(bf16[256,128]{1,0:T(8,128)(2,1)S(1)} %get-tuple-element.52), channel_id=1, source_target_pairs={{0,6},{1,7},{2,4},{3,5},{4,2},{5,3},{6,0},{7,1},{8,14},{9,15},{10,... | collective-permute-start | bytes 196616 | tf_op jit(solution)/shard_map/ppermute | solution.py:29
  93.5 15.1 %collective-permute-start.28 = (bf16[4,128,256]{2,1,0:T(8,128)(2,1)S(1)}, bf16[4,128,256]{2,1,0:T(8,128)(2,1)S(1)}, u32[]{:S(2)}, u32[]{:S(2)}) collective-permute-start(bf16[4,128,256]{2,1,0:T(8,128)(2,1)S(1)} %collective-permute-done.25.refs_12_), channel_id=1, source_target_pairs={{0,1},{1,0},{2,3},{3,2},{4,5},{5,4},{6,7},{7,6},{8,9},{9,8},{10,11... | collective-permute-start | bytes 786440 | tf_op jit(solution)/shard_map/ppermute | solution.py:29
  93.6 15.1 %collective-permute-start.29 = (bf16[4,128,256]{2,1,0:T(8,128)(2,1)S(1)}, bf16[4,128,256]{2,1,0:T(8,128)(2,1)S(1)}, u32[]{:S(2)}, u32[]{:S(2)}) collective-permute-start(bf16[4,128,256]{2,1,0:T(8,128)(2,1)S(1)} %collective-permute-done.26.refs_13_), channel_id=1, source_target_pairs={{0,1},{1,0},{2,3},{3,2},{4,5},{5,4},{6,7},{7,6},{8,9},{9,8},{10,11... | collective-permute-start | bytes 786440 | tf_op jit(solution)/shard_map/ppermute | solution.py:29
  94.0 14.6 %collective-permute-start.30 = (bf16[4,128,256]{2,1,0:T(8,128)(2,1)S(1)}, bf16[4,128,256]{2,1,0:T(8,128)(2,1)S(1)}, u32[]{:S(2)}, u32[]{:S(2)}) collective-permute-start(bf16[4,128,256]{2,1,0:T(8,128)(2,1)S(1)} %collective-permute-done.27.refs_14_), channel_id=1, source_target_pairs={{0,1},{1,0},{2,3},{3,2},{4,5},{5,4},{6,7},{7,6},{8,9},{9,8},{10,11... | collective-permute-start | bytes 786440 | tf_op jit(solution)/shard_map/ppermute | solution.py:29
  94.2 6.3 %collective-permute-start.48 = (bf16[256,128]{1,0:T(8,128)(2,1)S(1)}, bf16[256,128]{1,0:T(8,128)(2,1)S(1)}, u32[]{:S(2)}, u32[]{:S(2)}) collective-permute-start(bf16[256,128]{1,0:T(8,128)(2,1)S(1)} %get-tuple-element.53), channel_id=1, source_target_pairs={{0,4},{1,5},{2,6},{3,7},{4,0},{5,1},{6,2},{7,3},{8,12},{9,13},{10,... | collective-permute-start | bytes 196616 | tf_op jit(solution)/shard_map/ppermute | solution.py:29
  100.4 8.2 %collective-permute-start.23 = (bf16[128,512]{1,0:T(8,128)(2,1)S(1)}, bf16[128,512]{1,0:T(8,128)(2,1)S(1)}, u32[]{:S(2)}, u32[]{:S(2)}) collective-permute-start(bf16[128,512]{1,0:T(8,128)(2,1)S(1)} %bitcast.17), channel_id=1, source_target_pairs={{0,16},{8,24},{16,0},{24,8},{1,17},{9,25},{17,1},{25,9},{2,18},{10... | collective-permute-start | bytes 393224 | tf_op jit(solution)/shard_map/ppermute | solution.py:29
  102.1 6.5 %collective-permute-start.24 = (bf16[128,512]{1,0:T(8,128)(2,1)S(1)}, bf16[128,512]{1,0:T(8,128)(2,1)S(1)}, u32[]{:S(2)}, u32[]{:S(2)}) collective-permute-start(bf16[128,512]{1,0:T(8,128)(2,1)S(1)} %bitcast.18), channel_id=1, source_target_pairs={{0,24},{8,16},{16,8},{24,0},{1,25},{9,17},{17,9},{25,1},{2,26},{10... | collective-permute-start | bytes 393224 | tf_op jit(solution)/shard_map/ppermute | solution.py:29
  (26 other events, 126.6 us)
where the time goes:
time: 111 us
  starting transfers between devices  43.1 us (39%)
  waiting for transfers between devices  36.1 us (33%)
  Pallas kernels  27.1 us (24%)
  local copies, waits for them, and re-layouts  4.1 us (4%)
    ppermute x50, starting transfers between devices, swap(): return lax.ppermute(x, axis, [(j, j ^ distance) for j in range(size)])  43.1 us
    ppermute x50, waiting for transfers between devices, swap(): return lax.ppermute(x, axis, [(j, j ^ distance) for j in range(size)])  36.1 us
    pallas_call x14, Pallas kernels, call(): pl.pallas_call(kernel, out_shape=out, in_specs=ins, out_specs=outs, scrat...  27.1 us
    unnamed x16, local copies, waits for them, and re-layouts  4.1 us
  transfers between devices with their start and end apart: 50, of which 17 were waited for; matrix products, arithmetic and copies ran while one was open for 0% of the time, Pallas kernels for 22%

commit v1 on v0

--- a/solution.py
+++ b/solution.py
@@ -19,6 +19,7 @@
 ANY = pl.BlockSpec(memory_space=pl.ANY)
 VMEM = pl.BlockSpec(memory_space=pltpu.VMEM)
 SMEM = pl.BlockSpec(memory_space=pltpu.SMEM)
+HBM = pl.BlockSpec(memory_space=pltpu.HBM)
 
 
 def dot(a, b, dims):
@@ -71,14 +72,15 @@
     return jnp.concatenate([jnp.where(row < lengths_ref[0, p], 0.0, MASKED) for p in range(passages)], axis=0)
 
 
+def split3(x):
+    high = x.astype(jnp.bfloat16).astype(jnp.float32)
+    middle = (x - high).astype(jnp.bfloat16).astype(jnp.float32)
+    return high, middle, (x - high - middle).astype(jnp.bfloat16).astype(jnp.float32)
+
+
 def thirds(x):
-    high = x.astype(jnp.bfloat16)
-    rest = x - high.astype(jnp.float32)
-    middle = rest.astype(jnp.bfloat16)
-    low = (rest - middle.astype(jnp.float32)).astype(jnp.bfloat16)
-    parts = [high.astype(jnp.float32), middle.astype(jnp.float32), low.astype(jnp.float32)]
-    pad = EXTRA - 3 * x.shape[0]
-    return jnp.concatenate(parts + [jnp.zeros((pad, x.shape[1]), jnp.float32)], axis=0).astype(jnp.bfloat16)
+    pad = jnp.zeros((EXTRA - 3 * x.shape[0], x.shape[1]), jnp.float32)
+    return jnp.concatenate([*split3(x), pad], axis=0).astype(jnp.bfloat16)
 
 
 def unite(rows, heads):
@@ -91,40 +93,26 @@
     return ref.at[:, pl.ds(pl.multiple_of(owner * width, width), width)]
 
 
-def forward_kernel(size, passages, me_ref, lengths_ref, *refs):
+def forward_kernel(size, passages, lengths_ref, *refs):
     q_refs = refs[:size]
-    keys_ref, values_ref, even_ref, odd_ref, q_buf, k_buf, v_buf, bias_ref, sem = refs[size:]
-    me = me_ref[0]
+    keys_ref, values_ref, even_ref, odd_ref, q_buf, bias_ref = refs[size:]
     width = q_buf.shape[2]
-    half = size // 2
-
-    def k_copy(s):
-        return pltpu.make_async_copy(columns_of(keys_ref, me, s, width), k_buf.at[s], sem.at[0, s])
-
-    def v_copy(s):
-        return pltpu.make_async_copy(columns_of(values_ref, me, s, width), v_buf.at[s], sem.at[1, s])
-
-    for s in range(size):
-        k_copy(s).start()
-        v_copy(s).start()
     for s in range(size):
         q_buf[s] = q_refs[s][...]
-    bias_ref[...] = mask_bias(lengths_ref, passages, k_buf.shape[1] // passages)
+    bias_ref[...] = mask_bias(lengths_ref, passages, keys_ref.shape[1] // passages)
     lane_low = lax.broadcasted_iota(jnp.int32, (1, PAIR), 1) < HEAD_SIZE
 
     def one_slot(s, out_ref, k):
-        k_copy(s).wait()
-        v_copy(s).wait()
         rows = []
         for p in range(width // PAIR):
             lanes = slice(p * PAIR, (p + 1) * PAIR)
             queries = block_stack(q_buf[s, :, lanes], lane_low)
             bias = bias_ref[...]
-            scores = dot(k_buf[s, :, lanes], queries, NT) + jnp.concatenate([bias, bias], axis=1)
+            scores = dot(keys_ref[s, :, lanes], queries, NT) + jnp.concatenate([bias, bias], axis=1)
             top = jnp.max(scores, axis=0, keepdims=True)
             weights = jnp.exp(scores - top)
             total = jnp.sum(weights, axis=0, keepdims=True)
-            mixed = dot(v_buf[s, :, lanes], weights.astype(jnp.bfloat16), TN) / total
+            mixed = dot(values_ref[s, :, lanes], weights.astype(jnp.bfloat16), TN) / total
             out_ref[k, lanes, :] = diagonal(mixed).astype(jnp.bfloat16)
             lse = top + jnp.log(total)
             n = lse.shape[1] // 2
@@ -136,7 +124,7 @@
         one_slot(2 * k + 1, odd_ref, k)
         return carry
 
-    lax.fori_loop(0, half, body, 0)
+    lax.fori_loop(0, size // 2, body, 0)
 
 
 def merge(blocks):
@@ -163,54 +151,53 @@
 
 
 def merge_final_kernel(count, *refs):
-    grad_ref, context_ref, stats_ref = refs[count:]
+    grad_ref, out_ref = refs[count:]
     out, lse = merge([r[...] for r in refs[:count]])
     context = out.T.astype(jnp.bfloat16)
-    context_ref[...] = context
+    answers, _ = context.shape
+    out_ref[:answers, :] = context
     product = (context.astype(jnp.float32) * grad_ref[...].astype(jnp.float32)).T
     dots = [
         jnp.sum(product[h * HEAD_SIZE : (h + 1) * HEAD_SIZE], axis=0, keepdims=True) for h in range(lse.shape[0])
     ]
-    stats_ref[...] = jnp.concatenate([lse] + dots, axis=0)
+    high, middle, low = split3(jnp.concatenate([lse] + dots, axis=0))
+    top = jnp.concatenate([high, middle], axis=1)
+    bottom = jnp.concatenate([low, jnp.zeros_like(low)], axis=1)
+    out_ref[answers:, :] = jnp.concatenate([top, bottom], axis=0).astype(jnp.bfloat16)
+
+
+def stats_of(block_ref, answers):
+    rows = block_ref[answers:, :].astype(jnp.float32)
+    n = rows.shape[0] // 2
+    return rows[:n, :answers] + rows[:n, answers:] + rows[n:, :answers]
 
 
 def backward_kernel(slots, carried, passages, me_ref, lengths_ref, *refs):
     count = len(slots)
-    q_refs, g_refs, stats_refs = refs[:count], refs[count : 2 * count], refs[2 * count : 3 * count]
+    q_refs, g_refs, c_refs = refs[:count], refs[count : 2 * count], refs[2 * count : 3 * count]
     keys_ref, values_ref = refs[3 * count : 3 * count + 2]
-    (dk_ref, dv_ref, even_ref, odd_ref, q_buf, g_buf, st_buf, k_buf, v_buf, dk_buf, dv_buf, bias_ref, sem) = refs[
+    dk_ref, dv_ref, even_ref, odd_ref, q_buf, g_buf, st_buf, dk_buf, dv_buf, bias_ref, sem = refs[
         3 * count + 2 + carried :
     ]
     me = me_ref[0]
-    width = q_buf.shape[2]
+    answers, width = q_buf.shape[1:]
     first = slots[0]
 
-    def k_copy(i):
-        return pltpu.make_async_copy(columns_of(keys_ref, me, first + i, width), k_buf.at[i], sem.at[0, i])
-
-    def v_copy(i):
-        return pltpu.make_async_copy(columns_of(values_ref, me, first + i, width), v_buf.at[i], sem.at[1, i])
-
     def dk_copy(i):
-        return pltpu.make_async_copy(dk_buf.at[i], columns_of(dk_ref, me, first + i, width), sem.at[2, i])
+        return pltpu.make_async_copy(dk_buf.at[i], columns_of(dk_ref, me, first + i, width), sem.at[0, i])
 
     def dv_copy(i):
-        return pltpu.make_async_copy(dv_buf.at[i], columns_of(dv_ref, me, first + i, width), sem.at[3, i])
-
-    for i in range(count):
-        k_copy(i).start()
-        v_copy(i).start()
+        return pltpu.make_async_copy(dv_buf.at[i], columns_of(dv_ref, me, first + i, width), sem.at[1, i])
+
     for i in range(count):
         q_buf[i] = q_refs[i][...]
         g_buf[i] = g_refs[i][...]
-        st_buf[i] = stats_refs[i][...]
-    bias_ref[...] = mask_bias(lengths_ref, passages, k_buf.shape[1] // passages)
+        st_buf[i] = stats_of(c_refs[i], answers)
+    bias_ref[...] = mask_bias(lengths_ref, passages, keys_ref.shape[1] // passages)
     lane_low = lax.broadcasted_iota(jnp.int32, (1, PAIR), 1) < HEAD_SIZE
     heads = width // HEAD_SIZE
 
     def one_slot(i, out_ref, k):
-        k_copy(i).wait()
-        v_copy(i).wait()
         for p in range(width // PAIR):
             lanes = slice(p * PAIR, (p + 1) * PAIR)
             queries = block_stack(q_buf[i, :, lanes], lane_low)
@@ -220,11 +207,11 @@
             dots = jnp.concatenate(
                 [stats[heads + 2 * p : heads + 2 * p + 1], stats[heads + 2 * p + 1 : heads + 2 * p + 2]], axis=1
             )
-            key_block = k_buf[i, :, lanes]
+            key_block = keys_ref[first + i, :, lanes]
             bias = bias_ref[...]
             scores = dot(key_block, queries, NT) + jnp.concatenate([bias, bias], axis=1)
             probs = jnp.exp(scores - lse)
-            prob_grad = dot(v_buf[i, :, lanes], grads, NT)
+            prob_grad = dot(values_ref[first + i, :, lanes], grads, NT)
             score_grad = (probs * (prob_grad - dots)).astype(jnp.bfloat16)
             dv_buf[i, :, lanes] = dot(probs.astype(jnp.bfloat16), grads, NN).astype(jnp.bfloat16)
             dk_buf[i, :, lanes] = dot(score_grad, queries, NN).astype(jnp.bfloat16)
@@ -262,26 +249,37 @@
     refs[-1][...] = total.T.astype(jnp.bfloat16)
 
 
-def grad_partial_kernel(size, me_ref, cot_ref, weight_ref, even_ref, odd_ref, w_buf, sem):
+def grad_partial_kernel(size, me_ref, cot_ref, weight_ref, keys_ref, values_ref, *refs):
+    even_ref, odd_ref, k_out, v_out, cot_buf, w_buf, sem, cot_sem = refs
     me = me_ref[0]
     width = w_buf.shape[2]
 
-    def w_copy(s):
-        return pltpu.make_async_copy(columns_of(weight_ref, me, s, width), w_buf.at[s], sem.at[s])
+    def copy(ref, buf, lane, s):
+        return pltpu.make_async_copy(columns_of(ref, me, s, width), buf.at[s], sem.at[lane, s])
 
     order = list(range(1, size, 2)) + list(range(0, size, 2))
+    cot_copy = pltpu.make_async_copy(cot_ref, cot_buf, cot_sem)
+    cot_copy.start()
     for s in order:
-        w_copy(s).start()
-    cot = cot_ref[...]
+        copy(weight_ref, w_buf, 0, s).start()
+    for s in range(size):
+        copy(keys_ref, k_out, 1, s).start()
+        copy(values_ref, v_out, 2, s).start()
+    cot_copy.wait()
+    cot = cot_buf[...]
     for s in order:
-        w_copy(s).wait()
+        copy(weight_ref, w_buf, 0, s).wait()
         (odd_ref if s % 2 else even_ref)[s // 2] = dot(cot, w_buf[s], NN).astype(jnp.bfloat16)
+    for s in range(size):
+        copy(keys_ref, k_out, 1, s).wait()
+        copy(values_ref, v_out, 2, s).wait()
 
 
 def layer_out_kernel(size, me_ref, *refs):
     weight_ref, out_ref, w_buf, sem = refs[size:]
     me = me_ref[0]
     width = w_buf.shape[2]
+    answers = out_ref.shape[0]
 
     def w_copy(s):
         return pltpu.make_async_copy(columns_of(weight_ref, me, s, width), w_buf.at[s], sem.at[s])
@@ -291,39 +289,43 @@
     total = None
     for s in range(size):
         w_copy(s).wait()
-        part = dot(refs[s][...], w_buf[s], NT)
+        part = dot(refs[s][:answers, :], w_buf[s], NT)
         total = part if total is None else total + part
     out_ref[...] = total.astype(jnp.bfloat16)
 
 
-def weight_grad_kernel(size, groups, me_ref, *refs):
+def weight_grad_kernel(size, groups, answers, me_ref, *refs):
     half = size // 2
-    cots = refs[:groups]
-    own_even, own_odd = refs[groups : groups + half], refs[groups + half : groups + size]
-    rest = refs[groups + size :]
-    evens, odds = rest[: groups - 1], rest[groups - 1 : 2 * (groups - 1)]
-    out_ref, cot_buf, out_buf, sem = rest[2 * (groups - 1) :]
+    packs, packs_odd, own = refs[:groups], refs[groups : 2 * groups - 1], refs[2 * groups - 1 : 2 * groups - 1 + half]
+    out_ref, cot_buf, out_buf, sem = refs[2 * groups - 1 + half :]
     me = me_ref[0]
     width = out_buf.shape[2]
-    rows = cots[0].shape[0]
     for g in range(groups):
-        cot_buf[:, g * rows : (g + 1) * rows] = cots[g][...].T
+        for r in range(cot_buf.shape[0] // width):
+            cot_buf[r * width : (r + 1) * width, g * answers : (g + 1) * answers] = packs[g][half + r].T
 
     def out_copy(s):
         return pltpu.make_async_copy(out_buf.at[s], columns_of(out_ref, me, s, width), sem.at[s])
 
     for s in range(size):
-        own, others = (own_odd, odds) if s % 2 else (own_even, evens)
-        context = jnp.concatenate([own[s // 2][...]] + [o[s // 2] for o in others], axis=0)
-        out_buf[s] = dot(cot_buf[...], context, NN)
+        k = s // 2
+        if s % 2:
+            blocks = [own[k][:answers, :]] + [o[k] for o in packs_odd]
+        else:
+            blocks = [o[k] for o in packs]
+        out_buf[s] = dot(cot_buf[...], jnp.concatenate(blocks, axis=0), NN)
         out_copy(s).start()
     for s in range(size):
         out_copy(s).wait()
 
 
-def stack_kernel(*refs):
-    for k, r in enumerate(refs[:-1]):
-        refs[-1][k] = r[...]
+def pack_kernel(half, cot_ref, *refs):
+    out_ref = refs[half]
+    answers, width = out_ref.shape[1:]
+    for k in range(half):
+        out_ref[k] = refs[k][:answers, :]
+    for r in range(cot_ref.shape[1] // width):
+        out_ref[half + r] = cot_ref[:, r * width : (r + 1) * width]
 
 
 def shaped(shape, dtype):
@@ -349,17 +351,25 @@
 
     q_even = spread(query, size)
     slots = interleaved(q_even, across(q_even, size))
-    cots = [cot] + [swap(cot, "dp", dp, d) for d in range(1, dp)]
-
-    g_even, g_odd = call(
+
+    resident = shaped((size, key_count, width), bf16)
+    g_even, g_odd, slot_keys, slot_values = call(
         functools.partial(grad_partial_kernel, size),
         me,
         cot,
         out_weight,
-        out=[shaped((half, answers, width), bf16)] * 2,
-        ins=[SMEM, VMEM, ANY],
-        outs=[VMEM, VMEM],
-        scratch=[pltpu.VMEM((size, model, width), bf16), pltpu.SemaphoreType.DMA((size,))],
+        key_rows,
+        value_rows,
+        out=[shaped((half, answers, width), bf16)] * 2 + [resident] * 2,
+        ins=[SMEM] + [HBM] * 4,
+        outs=[VMEM] * 4,
+        scratch=[
+            pltpu.VMEM((answers, model), bf16),
+            pltpu.VMEM((size, model, width), bf16),
+            pltpu.SemaphoreType.DMA((3, size)),
+            pltpu.SemaphoreType.DMA(()),
+        ],
+        vmem=12,
     )
     g_other = swap(g_odd, "psg", size, 1)
     block = shaped((answers, width), bf16)
@@ -369,21 +379,14 @@
     packed = shaped((width + EXTRA, answers), bf16)
     o_even, o_odd = call(
         functools.partial(forward_kernel, size, passages),
-        me,
         lengths,
         *slots,
-        key_rows,
-        value_rows,
+        slot_keys,
+        slot_values,
         out=[shaped((half, width + EXTRA, answers), bf16)] * 2,
-        ins=[SMEM, SMEM] + [VMEM] * size + [ANY, ANY],
+        ins=[SMEM] + [VMEM] * (size + 2),
         outs=[VMEM] * 2,
-        scratch=[
-            pltpu.VMEM((size, answers, width), bf16),
-            pltpu.VMEM((size, key_count, width), bf16),
-            pltpu.VMEM((size, key_count, width), bf16),
-            pltpu.VMEM((key_count, PAIR), f32),
-            pltpu.SemaphoreType.DMA((2, size)),
-        ],
+        scratch=[pltpu.VMEM((size, answers, width), bf16), pltpu.VMEM((key_count, PAIR), f32)],
         vmem=16,
     )
 
@@ -392,19 +395,19 @@
     arrived = [swap(o_pairs[d // 2], "psg", size, d) for d in far_first(size)]
     context_grad = call(add_all_kernel, g_sums[0], *g_parts, out=block, ins=[VMEM] * half, outs=VMEM)
     cg_even = spread(context_grad, size)
-    context, stats = call(
+    context = call(
         functools.partial(merge_final_kernel, half),
         o_pairs[0],
         *arrived,
         context_grad,
-        out=[block, shaped((2 * heads, answers), f32)],
+        out=shaped((answers + 4 * heads, width), bf16),
         ins=[VMEM] * (half + 1),
-        outs=[VMEM] * 2,
-    )
-    s_even = spread(stats, size)
+        outs=VMEM,
+    )
     c_even = spread(context, size)
+    c_odd = across(c_even, size)
+    c_slots = interleaved(c_even, c_odd)
     g_slots = interleaved(cg_even, across(cg_even, size))
-    s_slots = interleaved(s_even, across(s_even, size))
 
     def backward(chosen, carried):
         count = len(chosen)
@@ -416,20 +419,20 @@
             lengths,
             *slots[pick],
             *g_slots[pick],
-            *s_slots[pick],
-            key_rows,
-            value_rows,
+            *c_slots[pick],
+            slot_keys,
+            slot_values,
             *carried,
             out=[shaped((key_count, inner), bf16)] * 2 + [shaped((count // 2, width, answers), bf16)] * 2,
-            ins=[SMEM, SMEM] + [VMEM] * (3 * count) + [ANY] * (2 + len(carried)),
+            ins=[SMEM, SMEM] + [VMEM] * (3 * count + 2) + [ANY] * len(carried),
             outs=[ANY, ANY, VMEM, VMEM],
             scratch=[
                 pltpu.VMEM((count, answers, width), bf16),
                 pltpu.VMEM((count, answers, width), bf16),
                 pltpu.VMEM((count, 2 * heads, answers), f32),
             ]
-            + [pltpu.VMEM((count, key_count, width), bf16)] * 4
-            + [pltpu.VMEM((key_count, PAIR), f32), pltpu.SemaphoreType.DMA((4, count))],
+            + [pltpu.VMEM((count, key_count, width), bf16)] * 2
+            + [pltpu.VMEM((key_count, PAIR), f32), pltpu.SemaphoreType.DMA((2, count))],
             vmem=16,
             alias={fixed + i: i for i in range(len(carried))},
         )
@@ -453,14 +456,20 @@
     dq_parts = [swap(sums[d // 2], "psg", size, d) for d in far_first(size)]
     query_grad = call(add_all_transposed_kernel, sums[0], *dq_parts, out=block, ins=[VMEM] * half, outs=VMEM)
 
-    c_odd = across(c_even, size)
-    stacked = call(stack_kernel, *c_even, out=shaped((half, answers, width), bf16), ins=[VMEM] * half, outs=VMEM)
-    evens = [swap(stacked, "dp", dp, d) for d in range(1, dp)]
-    odds = [swap(e, "psg", size, 1) for e in evens]
+    pack = call(
+        functools.partial(pack_kernel, half),
+        cot,
+        *c_even,
+        out=shaped((half + model // width, answers, width), bf16),
+        ins=[VMEM] * (half + 1),
+        outs=VMEM,
+    )
+    packs = [pack] + [swap(pack, "dp", dp, d) for d in range(1, dp)]
+    packs_odd = [swap(packs[d], "psg", size, 1) for d in range(1, dp)]
     layer_out = call(
         functools.partial(layer_out_kernel, size),
         me,
-        *interleaved(c_even, c_odd),
+        *c_slots,
         out_weight,
         out=shaped((answers, model), bf16),
         ins=[SMEM] + [VMEM] * size + [ANY],
@@ -468,15 +477,13 @@
         scratch=[pltpu.VMEM((size, model, width), bf16), pltpu.SemaphoreType.DMA((size,))],
     )
     weight_grad = call(
-        functools.partial(weight_grad_kernel, size, dp),
+        functools.partial(weight_grad_kernel, size, dp, answers),
         me,
-        *cots,
-        *c_even,
+        *packs,
+        *packs_odd,
         *c_odd,
-        *evens,
-        *odds,
         out=shaped((model, inner), f32),
-        ins=[SMEM] + [VMEM] * (dp + size + 2 * (dp - 1)),
+        ins=[SMEM] + [VMEM] * (2 * dp - 1 + half),
         outs=ANY,
         scratch=[
             pltpu.VMEM((model, dp * answers), bf16),
@@ -561,7 +568,7 @@
             and 2 * (width // HEAD_SIZE) % 8 == 0
             and queries.shape[1] % 128 == 0
             and keys.shape[2] % 16 == 0
-            and (out_weight.shape[0] // size) % 128 == 0
+            and (out_weight.shape[0] // size) % width == 0
         )
         body = jax.shard_map(
             per_device if direct else general_device,

time: 111 us -> 101 us (0.910)
  starting transfers between devices: 43.1 us -> 32.3 us
  Pallas kernels: 27.1 us -> 25.3 us
  local copies, waits for them, and re-layouts: 4.1 us -> 5.69 us
    ppermute x50 -> x40, starting transfers between devices: 43.1 us -> 32.3 us  [swap(): return lax.ppermute(x, axis, [(j, j ^ distance) for j in range(size)])]
    pallas_call x14, Pallas kernels: 27.1 us -> 25.3 us  [call(): pl.pallas_call(kernel, out_shape=out, in_specs=ins, out_specs=outs, scrat...]
    unnamed x16, local copies, waits for them, and re-layouts: 4.1 us -> 5.69 us
    ppermute x50 -> x40, waiting for transfers between devices: 36.1 us -> 36.8 us  [swap(): return lax.ppermute(x, axis, [(j, j ^ distance) for j in range(size)])]
  transfers between devices with their start and end apart: 50 -> 40, of which waited for: 17 -> 13; matrix products, arithmetic and copies ran while one was open for 0% -> 0% of each run, Pallas kernels for 22% -> 22%
where the time goes in v1:
time: 101 us
  waiting for transfers between devices  36.8 us (36%)
  starting transfers between devices  32.3 us (32%)
  Pallas kernels  25.3 us (25%)
  local copies, waits for them, and re-layouts  5.69 us (6%)
    ppermute x40, waiting for transfers between devices, swap(): return lax.ppermute(x, axis, [(j, j ^ distance) for j in range(size)])  36.8 us
    ppermute x40, starting transfers between devices, swap(): return lax.ppermute(x, axis, [(j, j ^ distance) for j in range(size)])  32.3 us
    pallas_call x14, Pallas kernels, call(): pl.pallas_call(kernel, out_shape=out, in_specs=ins, out_specs=outs, scrat...  25.3 us
    unnamed x16, local copies, waits for them, and re-layouts  5.69 us
  transfers between devices with their start and end apart: 40, of which 13 were waited for; matrix products, arithmetic and copies ran while one was open for 0% of the time, Pallas kernels for 22%

profile of v1, /device:TPU:0, one launch (start us, length us, event | category | flops | bytes accessed | tf_op | source)
XLA Modules:
  0.0 100.9 jit_solution(8025600271822705024)
XLA Ops:
  0.6 3.1 %collective-permute-start.1 = (bf16[128,256]{1,0:T(8,128)(2,1)}, bf16[128,256]{1,0:T(8,128)(2,1)S(1)}, u32[]{:S(2)}, u32[]{:S(2)}) collective-permute-start(bf16[128,256]{1,0:T(8,128)(2,1)} %bitcast.13), channel_id=1, source_target_pairs={{0,2},{1,3},{2,0},{3,1},{4,6},{5,7},{6,4},{7,5},{8,10},{9,11},{10,... | collective-permute-start | bytes 196616 | tf_op jit(solution)/shard_map/ppermute | solution.py:30
  3.7 2.6 %collective-permute-start.3 = (bf16[128,256]{1,0:T(8,128)(2,1)}, bf16[128,256]{1,0:T(8,128)(2,1)S(1)}, u32[]{:S(2)}, u32[]{:S(2)}) collective-permute-start(bf16[128,256]{1,0:T(8,128)(2,1)} %bitcast.14), channel_id=1, source_target_pairs={{0,4},{1,5},{2,6},{3,7},{4,0},{5,1},{6,2},{7,3},{8,12},{9,13},{10,... | collective-permute-start | bytes 196616 | tf_op jit(solution)/shard_map/ppermute | solution.py:30
  6.9 4.4 %collective-permute-done.3.refs_4_.refs_0_ = bf16[128,256]{1,0:T(8,128)(2,1)S(1)} collective-permute-done((bf16[128,256]{1,0:T(8,128)(2,1)}, bf16[128,256]{1,0:T(8,128)(2,1)S(1)}, u32[]{:S(2)}, u32[]{:S(2)}) %collective-permute-start.3) | collective-permute-done | bytes 65568 | tf_op jit(solution)/shard_map/ppermute | solution.py:30
  11.2 1.4 %collective-permute-done.5.refs_6_.refs_2_ = bf16[128,256]{1,0:T(8,128)(2,1)S(1)} collective-permute-done((bf16[128,256]{1,0:T(8,128)(2,1)}, bf16[128,256]{1,0:T(8,128)(2,1)S(1)}, u32[]{:S(2)}, u32[]{:S(2)}) %collective-permute-start.5) | collective-permute-done | bytes 65568 | tf_op jit(solution)/shard_map/ppermute | solution.py:30
  12.6 1.6 %copy-done = bf16[512,2048]{1,0:T(8,128)(2,1)S(1)} copy-done((bf16[512,2048]{1,0:T(8,128)(2,1)S(1)}, bf16[512,2048]{1,0:T(8,128)(2,1)}, u32[]{:S(2)}) %copy-start) | copy-done | bytes 2097176
  14.2 1.6 %copy-done.2 = bf16[1,2,256,2048]{3,2,1,0:T(8,128)(2,1)S(1)} copy-done((bf16[1,2,256,2048]{3,2,1,0:T(8,128)(2,1)S(1)}, bf16[1,2,256,2048]{3,2,1,0:T(8,128)(2,1)}, u32[]{:S(2)}) %copy-start.2) | copy-done | bytes 2097176
  15.8 1.6 %copy-done.3 = bf16[1,2,256,2048]{3,2,1,0:T(8,128)(2,1)S(1)} copy-done((bf16[1,2,256,2048]{3,2,1,0:T(8,128)(2,1)S(1)}, bf16[1,2,256,2048]{3,2,1,0:T(8,128)(2,1)}, u32[]{:S(2)}) %copy-start.3) | copy-done | bytes 2097176
  18.3 3.1 %shard_map.101 = (bf16[4,128,256]{2,1,0:T(8,128)(2,1)S(1)}, bf16[4,128,256]{2,1,0:T(8,128)(2,1)S(1)}, bf16[8,512,256]{2,1,0:T(8,128)(2,1)S(1)}, bf16[8,512,256]{2,1,0:T(8,128)(2,1)S(1)}) custom-call(s32[1]{0:T(128)} %bitcast.me_ref, bf16[128,512]{1,0:T(8,128)(2,1)S(1)} %bitcast.11, bf16[512,2048]{1,0:T(8,128)(2,1)S(1)} %copy-done, ...), custom_call_target="tpu_custom_call" | custom-call | tf_op jit(solution)/shard_map/pallas_call | solution.py:34
  22.0 7.7 %shard_map.102 = (bf16[4,272,128]{2,1,0:T(8,128)(2,1)S(1)}, bf16[4,272,128]{2,1,0:T(8,128)(2,1)S(1)}) custom-call(s32[1,2]{1,0:T(1,128)S(1)} %copy-done.7, bf16[128,256]{1,0:T(8,128)(2,1)S(1)} %bitcast.17, bf16[128,256]{1,0:T(8,128)(2,1)S(1)} %collective-permute-done.refs_1_, bf16[128,256]{1,0:T(8,128)(2,1)S(1)} %collective-permute-done.1.refs_2_, ...), custom_call_target="tpu_custom_call" | custom-call | tf_op jit(solution)/shard_map/pallas_call | solution.py:34
  29.9 2.3 %collective-permute-start.12 = (bf16[128,256]{1,0:T(8,128)(2,1)S(1)}, bf16[128,256]{1,0:T(8,128)(2,1)S(1)}, u32[]{:S(2)}, u32[]{:S(2)}) collective-permute-start(bf16[128,256]{1,0:T(8,128)(2,1)S(1)} %get-tuple-element.42), channel_id=1, source_target_pairs={{0,6},{1,7},{2,4},{3,5},{4,2},{5,3},{6,0},{7,1},{8,14},{9,15},{10,... | collective-permute-start | bytes 196616 | tf_op jit(solution)/shard_map/ppermute | solution.py:30
  32.4 2.2 %collective-permute-start.8 = (bf16[272,128]{1,0:T(8,128)(2,1)S(1)}, bf16[272,128]{1,0:T(8,128)(2,1)S(1)}, u32[]{:S(2)}, u32[]{:S(2)}) collective-permute-start(bf16[272,128]{1,0:T(8,128)(2,1)S(1)} %get-tuple-element.36), channel_id=1, source_target_pairs={{0,6},{1,7},{2,4},{3,5},{4,2},{5,3},{6,0},{7,1},{8,14},{9,15},{10,... | collective-permute-start | bytes 208904 | tf_op jit(solution)/shard_map/ppermute | solution.py:30
  34.6 1.3 %collective-permute-start.9 = (bf16[272,128]{1,0:T(8,128)(2,1)S(1)}, bf16[272,128]{1,0:T(8,128)(2,1)S(1)}, u32[]{:S(2)}, u32[]{:S(2)}) collective-permute-start(bf16[272,128]{1,0:T(8,128)(2,1)S(1)} %get-tuple-element.37), channel_id=1, source_target_pairs={{0,4},{1,5},{2,6},{3,7},{4,0},{5,1},{6,2},{7,3},{8,12},{9,13},{10,... | collective-permute-start | bytes 208904 | tf_op jit(solution)/shard_map/ppermute | solution.py:30
  35.9 1.6 %collective-permute-start.13 = (bf16[128,256]{1,0:T(8,128)(2,1)S(1)}, bf16[128,256]{1,0:T(8,128)(2,1)S(1)}, u32[]{:S(2)}, u32[]{:S(2)}) collective-permute-start(bf16[128,256]{1,0:T(8,128)(2,1)S(1)} %get-tuple-element.43), channel_id=1, source_target_pairs={{0,4},{1,5},{2,6},{3,7},{4,0},{5,1},{6,2},{7,3},{8,12},{9,13},{10,... | collective-permute-start | bytes 196616 | tf_op jit(solution)/shard_map/ppermute | solution.py:30
  38.1 7.3 %collective-permute-done.13.refs_2_ = bf16[128,256]{1,0:T(8,128)(2,1)S(1)} collective-permute-done((bf16[128,256]{1,0:T(8,128)(2,1)S(1)}, bf16[128,256]{1,0:T(8,128)(2,1)S(1)}, u32[]{:S(2)}, u32[]{:S(2)}) %collective-permute-start.13) | collective-permute-done | bytes 65568 | tf_op jit(solution)/shard_map/ppermute | solution.py:30
  45.8 1.9 %collective-permute-start.20 = (bf16[144,256]{1,0:T(8,128)(2,1)S(1)}, bf16[144,256]{1,0:T(8,128)(2,1)S(1)}, u32[]{:S(2)}, u32[]{:S(2)}) collective-permute-start(bf16[144,256]{1,0:T(8,128)(2,1)S(1)} %shard_map.106.refs_0_.refs_8_), channel_id=1, source_target_pairs={{0,6},{1,7},{2,4},{3,5},{4,2},{5,3},{6,0},{7,1},{8,14},{9,15},{10,... | collective-permute-start | bytes 221192 | tf_op jit(solution)/shard_map/ppermute | solution.py:30
  47.7 1.5 %collective-permute-start.16 = (bf16[144,256]{1,0:T(8,128)(2,1)S(1)}, bf16[144,256]{1,0:T(8,128)(2,1)S(1)}, u32[]{:S(2)}, u32[]{:S(2)}) collective-permute-start(bf16[144,256]{1,0:T(8,128)(2,1)S(1)} %shard_map.106.refs_0_.refs_8_), channel_id=1, source_target_pairs={{0,2},{1,3},{2,0},{3,1},{4,6},{5,7},{6,4},{7,5},{8,10},{9,11},{10,... | collective-permute-start | bytes 221192 | tf_op jit(solution)/shard_map/ppermute | solution.py:30
  49.2 3.9 %collective-permute-done.18.refs_4_.refs_2_.refs_8_ = bf16[144,256]{1,0:T(8,128)(2,1)S(1)} collective-permute-done((bf16[144,256]{1,0:T(8,128)(2,1)S(1)}, bf16[144,256]{1,0:T(8,128)(2,1)S(1)}, u32[]{:S(2)}, u32[]{:S(2)}) %collective-permute-start.18) | collective-permute-done | bytes 73760 | tf_op jit(solution)/shard_map/ppermute | solution.py:30
  54.2 1.6 %collective-permute-start.22 = (bf16[6,128,256]{2,1,0:T(8,128)(2,1)S(1)}, bf16[6,128,256]{2,1,0:T(8,128)(2,1)S(1)}, u32[]{:S(2)}, u32[]{:S(2)}) collective-permute-start(bf16[6,128,256]{2,1,0:T(8,128)(2,1)S(1)} %shard_map.108.refs_0_), channel_id=1, source_target_pairs={{0,8},{8,0},{16,24},{24,16},{1,9},{9,1},{17,25},{25,17},{2,10},{10... | collective-permute-start | bytes 1179656 | tf_op jit(solution)/shard_map/ppermute | solution.py:30
  55.7 1.5 %collective-permute-start.23 = (bf16[6,128,256]{2,1,0:T(8,128)(2,1)S(1)}, bf16[6,128,256]{2,1,0:T(8,128)(2,1)S(1)}, u32[]{:S(2)}, u32[]{:S(2)}) collective-permute-start(bf16[6,128,256]{2,1,0:T(8,128)(2,1)S(1)} %shard_map.108.refs_0_), channel_id=1, source_target_pairs={{0,16},{8,24},{16,0},{24,8},{1,17},{9,25},{17,1},{25,9},{2,18},{10... | collective-permute-start | bytes 1179656 | tf_op jit(solution)/shard_map/ppermute | solution.py:30
  57.7 1.3 %collective-permute-start.31 = (bf16[128,256]{1,0:T(8,128)(2,1)S(1)}, bf16[128,256]{1,0:T(8,128)(2,1)S(1)}, u32[]{:S(2)}, u32[]{:S(2)}) collective-permute-start(bf16[128,256]{1,0:T(8,128)(2,1)S(1)} %shard_map.105.refs_4_), channel_id=1, source_target_pairs={{0,4},{1,5},{2,6},{3,7},{4,0},{5,1},{6,2},{7,3},{8,12},{9,13},{10,... | collective-permute-start | bytes 196616 | tf_op jit(solution)/shard_map/ppermute | solution.py:30
  59.0 2.0 %collective-permute-start.33 = (bf16[128,256]{1,0:T(8,128)(2,1)S(1)}, bf16[128,256]{1,0:T(8,128)(2,1)S(1)}, u32[]{:S(2)}, u32[]{:S(2)}) collective-permute-start(bf16[128,256]{1,0:T(8,128)(2,1)S(1)} %shard_map.105.refs_4_), channel_id=1, source_target_pairs={{0,6},{1,7},{2,4},{3,5},{4,2},{5,3},{6,0},{7,1},{8,14},{9,15},{10,... | collective-permute-start | bytes 196616 | tf_op jit(solution)/shard_map/ppermute | solution.py:30
  61.0 3.3 %collective-permute-done.31.refs_4_ = bf16[128,256]{1,0:T(8,128)(2,1)S(1)} collective-permute-done((bf16[128,256]{1,0:T(8,128)(2,1)S(1)}, bf16[128,256]{1,0:T(8,128)(2,1)S(1)}, u32[]{:S(2)}, u32[]{:S(2)}) %collective-permute-start.31) | collective-permute-done | bytes 65568 | tf_op jit(solution)/shard_map/ppermute | solution.py:30
  65.4 3.2 %collective-permute-done.29.refs_6_ = bf16[128,256]{1,0:T(8,128)(2,1)S(1)} collective-permute-done((bf16[128,256]{1,0:T(8,128)(2,1)S(1)}, bf16[128,256]{1,0:T(8,128)(2,1)S(1)}, u32[]{:S(2)}, u32[]{:S(2)}) %collective-permute-start.29) | collective-permute-done | bytes 65568 | tf_op jit(solution)/shard_map/ppermute | solution.py:30
  70.6 4.1 %collective-permute-done.23.refs_2_ = bf16[6,128,256]{2,1,0:T(8,128)(2,1)S(1)} collective-permute-done((bf16[6,128,256]{2,1,0:T(8,128)(2,1)S(1)}, bf16[6,128,256]{2,1,0:T(8,128)(2,1)S(1)}, u32[]{:S(2)}, u32[]{:S(2)}) %collective-permute-start.23) | collective-permute-done | bytes 393248 | tf_op jit(solution)/shard_map/ppermute | solution.py:30
  75.7 1.4 %collective-permute-done.21.refs_7_.refs_10_.refs_11_ = bf16[144,256]{1,0:T(8,128)(2,1)S(1)} collective-permute-done((bf16[144,256]{1,0:T(8,128)(2,1)S(1)}, bf16[144,256]{1,0:T(8,128)(2,1)S(1)}, u32[]{:S(2)}, u32[]{:S(2)}) %collective-permute-start.21) | collective-permute-done | bytes 73760 | tf_op jit(solution)/shard_map/ppermute | solution.py:30
  77.1 4.3 %shard_map.110 = (bf16[512,2048]{1,0:T(8,128)(2,1)}, bf16[512,2048]{1,0:T(8,128)(2,1)}, bf16[2,256,128]{2,1,0:T(8,128)(2,1)S(1)}, bf16[2,256,128]{2,1,0:T(8,128)(2,1)S(1)}) custom-call(s32[1]{0:T(128)} %bitcast.me_ref, s32[1,2]{1,0:T(1,128)S(1)} %copy-done.7, bf16[128,256]{1,0:T(8,128)(2,1)S(1)} %collective-permute-done.3.refs_4_.refs_0_, ...), custom_call_target="tpu_custom_call" | custom-call | tf_op jit(solution)/shard_map/pallas_call | solution.py:34
  81.9 4.3 %shard_map.111 = (bf16[512,2048]{1,0:T(8,128)(2,1)}, bf16[512,2048]{1,0:T(8,128)(2,1)}, bf16[2,256,128]{2,1,0:T(8,128)(2,1)S(1)}, bf16[2,256,128]{2,1,0:T(8,128)(2,1)S(1)}) custom-call(s32[1]{0:T(128)} %bitcast.me_ref, s32[1,2]{1,0:T(1,128)S(1)} %copy-done.7, bf16[128,256]{1,0:T(8,128)(2,1)S(1)} %bitcast.18, ...), custom_call_target="tpu_custom_call", output_to_operand_aliasing={{0}: (16, {}), {1}: (17, {})} | custom-call | tf_op jit(solution)/shard_map/pallas_call | solution.py:34
  87.7 1.4 %collective-permute-start.38 = (bf16[256,128]{1,0:T(8,128)(2,1)S(1)}, bf16[256,128]{1,0:T(8,128)(2,1)S(1)}, u32[]{:S(2)}, u32[]{:S(2)}) collective-permute-start(bf16[256,128]{1,0:T(8,128)(2,1)S(1)} %get-tuple-element.53), channel_id=1, source_target_pairs={{0,4},{1,5},{2,6},{3,7},{4,0},{5,1},{6,2},{7,3},{8,12},{9,13},{10,... | collective-permute-start | bytes 196616 | tf_op jit(solution)/shard_map/ppermute | solution.py:30
  89.1 4.3 %collective-permute-done.37.refs_1_ = bf16[256,128]{1,0:T(8,128)(2,1)S(1)} collective-permute-done((bf16[256,128]{1,0:T(8,128)(2,1)S(1)}, bf16[256,128]{1,0:T(8,128)(2,1)S(1)}, u32[]{:S(2)}, u32[]{:S(2)}) %collective-permute-start.37) | collective-permute-done | bytes 65568 | tf_op jit(solution)/shard_map/ppermute | solution.py:30
  93.4 1.5 %collective-permute-start.39 = (bf16[256,128]{1,0:T(8,128)(2,1)S(1)}, bf16[256,128]{1,0:T(8,128)(2,1)S(1)}, u32[]{:S(2)}, u32[]{:S(2)}) collective-permute-start(bf16[256,128]{1,0:T(8,128)(2,1)S(1)} %get-tuple-element.54), channel_id=1, source_target_pairs={{0,2},{1,3},{2,0},{3,1},{4,6},{5,7},{6,4},{7,5},{8,10},{9,11},{10,... | collective-permute-start | bytes 196616 | tf_op jit(solution)/shard_map/ppermute | solution.py:30
  94.8 2.0 %shard_map.107 = bf16[128,512]{1,0:T(8,128)(2,1)} custom-call(s32[1]{0:T(128)} %bitcast.me_ref, bf16[144,256]{1,0:T(8,128)(2,1)S(1)} %shard_map.106.refs_0_.refs_8_, bf16[144,256]{1,0:T(8,128)(2,1)S(1)} %collective-permute-done.15.refs_1_.refs_7_.refs_9_, bf16[144,256]{1,0:T(8,128)(2,1)S(1)} %collective-permute-done.16.refs_2_.refs_1_.refs_10_, ...), custom_call_target="tpu_custom_call" | custom-call | tf_op jit(solution)/shard_map/pallas_call | solution.py:34
  98.4 2.6 %shard_map.109 = f32[512,2048]{1,0:T(8,128)} custom-call(s32[1]{0:T(128)} %bitcast.me_ref, bf16[6,128,256]{2,1,0:T(8,128)(2,1)S(1)} %shard_map.108.refs_0_, bf16[6,128,256]{2,1,0:T(8,128)(2,1)S(1)} %collective-permute-done.22.refs_1_, bf16[6,128,256]{2,1,0:T(8,128)(2,1)S(1)} %collective-permute-done.23.refs_2_, ...), custom_call_target="tpu_custom_call" | custom-call | tf_op jit(solution)/shard_map/pallas_call | solution.py:34
  (78 shorter events, 12.4 us)
Async XLA Ops:
  0.6 5.7 %collective-permute-start.1 = (bf16[128,256]{1,0:T(8,128)(2,1)}, bf16[128,256]{1,0:T(8,128)(2,1)S(1)}, u32[]{:S(2)}, u32[]{:S(2)}) collective-permute-start(bf16[128,256]{1,0:T(8,128)(2,1)} %bitcast.13), channel_id=1, source_target_pairs={{0,2},{1,3},{2,0},{3,1},{4,6},{5,7},{6,4},{7,5},{8,10},{9,11},{10,... | collective-permute-start | bytes 196616 | tf_op jit(solution)/shard_map/ppermute | solution.py:30
  3.7 7.5 %collective-permute-start.3 = (bf16[128,256]{1,0:T(8,128)(2,1)}, bf16[128,256]{1,0:T(8,128)(2,1)S(1)}, u32[]{:S(2)}, u32[]{:S(2)}) collective-permute-start(bf16[128,256]{1,0:T(8,128)(2,1)} %bitcast.14), channel_id=1, source_target_pairs={{0,4},{1,5},{2,6},{3,7},{4,0},{5,1},{6,2},{7,3},{8,12},{9,13},{10,... | collective-permute-start | bytes 196616 | tf_op jit(solution)/shard_map/ppermute | solution.py:30
  6.3 6.3 %collective-permute-start.5 = (bf16[128,256]{1,0:T(8,128)(2,1)}, bf16[128,256]{1,0:T(8,128)(2,1)S(1)}, u32[]{:S(2)}, u32[]{:S(2)}) collective-permute-start(bf16[128,256]{1,0:T(8,128)(2,1)} %bitcast.15), channel_id=1, source_target_pairs={{0,6},{1,7},{2,4},{3,5},{4,2},{5,3},{6,0},{7,1},{8,14},{9,15},{10,... | collective-permute-start | bytes 196616 | tf_op jit(solution)/shard_map/ppermute | solution.py:30
  6.3 15.6 %collective-permute-start = (bf16[128,256]{1,0:T(8,128)(2,1)}, bf16[128,256]{1,0:T(8,128)(2,1)S(1)}, u32[]{:S(2)}, u32[]{:S(2)}) collective-permute-start(bf16[128,256]{1,0:T(8,128)(2,1)} %bitcast.16), channel_id=1, source_target_pairs={{0,1},{1,0},{2,3},{3,2},{4,5},{5,4},{6,7},{7,6},{8,9},{9,8},{10,11... | collective-permute-start | bytes 196616 | tf_op jit(solution)/shard_map/ppermute | solution.py:30
  6.4 15.6 %collective-permute-start.2 = (bf16[128,256]{1,0:T(8,128)(2,1)S(1)}, bf16[128,256]{1,0:T(8,128)(2,1)S(1)}, u32[]{:S(2)}, u32[]{:S(2)}) collective-permute-start(bf16[128,256]{1,0:T(8,128)(2,1)S(1)} %collective-permute-done.1.refs_2_), channel_id=1, source_target_pairs={{0,1},{1,0},{2,3},{3,2},{4,5},{5,4},{6,7},{7,6},{8,9},{9,8},{10,11... | collective-permute-start | bytes 196616 | tf_op jit(solution)/shard_map/ppermute | solution.py:30
  11.2 10.7 %collective-permute-start.4 = (bf16[128,256]{1,0:T(8,128)(2,1)S(1)}, bf16[128,256]{1,0:T(8,128)(2,1)S(1)}, u32[]{:S(2)}, u32[]{:S(2)}) collective-permute-start(bf16[128,256]{1,0:T(8,128)(2,1)S(1)} %collective-permute-done.3.refs_4_.refs_0_), channel_id=1, source_target_pairs={{0,1},{1,0},{2,3},{3,2},{4,5},{5,4},{6,7},{7,6},{8,9},{9,8},{10,11... | collective-permute-start | bytes 196616 | tf_op jit(solution)/shard_map/ppermute | solution.py:30
  12.6 9.3 %collective-permute-start.6 = (bf16[128,256]{1,0:T(8,128)(2,1)S(1)}, bf16[128,256]{1,0:T(8,128)(2,1)S(1)}, u32[]{:S(2)}, u32[]{:S(2)}) collective-permute-start(bf16[128,256]{1,0:T(8,128)(2,1)S(1)} %collective-permute-done.5.refs_6_.refs_2_), channel_id=1, source_target_pairs={{0,1},{1,0},{2,3},{3,2},{4,5},{5,4},{6,7},{7,6},{8,9},{9,8},{10,11... | collective-permute-start | bytes 196616 | tf_op jit(solution)/shard_map/ppermute | solution.py:30
  21.4 8.4 %collective-permute-start.11 = (bf16[4,128,256]{2,1,0:T(8,128)(2,1)S(1)}, bf16[4,128,256]{2,1,0:T(8,128)(2,1)S(1)}, u32[]{:S(2)}, u32[]{:S(2)}) collective-permute-start(bf16[4,128,256]{2,1,0:T(8,128)(2,1)S(1)} %get-tuple-element.40), channel_id=1, source_target_pairs={{0,1},{1,0},{2,3},{3,2},{4,5},{5,4},{6,7},{7,6},{8,9},{9,8},{10,11... | collective-permute-start | bytes 786440 | tf_op jit(solution)/shard_map/ppermute | solution.py:30
  29.9 7.6 %collective-permute-start.12 = (bf16[128,256]{1,0:T(8,128)(2,1)S(1)}, bf16[128,256]{1,0:T(8,128)(2,1)S(1)}, u32[]{:S(2)}, u32[]{:S(2)}) collective-permute-start(bf16[128,256]{1,0:T(8,128)(2,1)S(1)} %get-tuple-element.42), channel_id=1, source_target_pairs={{0,6},{1,7},{2,4},{3,5},{4,2},{5,3},{6,0},{7,1},{8,14},{9,15},{10,... | collective-permute-start | bytes 196616 | tf_op jit(solution)/shard_map/ppermute | solution.py:30
  32.4 13.1 %collective-permute-start.10 = (bf16[272,128]{1,0:T(8,128)(2,1)S(1)}, bf16[272,128]{1,0:T(8,128)(2,1)S(1)}, u32[]{:S(2)}, u32[]{:S(2)}) collective-permute-start(bf16[272,128]{1,0:T(8,128)(2,1)S(1)} %get-tuple-element.38), channel_id=1, source_target_pairs={{0,2},{1,3},{2,0},{3,1},{4,6},{5,7},{6,4},{7,5},{8,10},{9,11},{10,... | collective-permute-start | bytes 208904 | tf_op jit(solution)/shard_map/ppermute | solution.py:30
  32.4 13.0 %collective-permute-start.8 = (bf16[272,128]{1,0:T(8,128)(2,1)S(1)}, bf16[272,128]{1,0:T(8,128)(2,1)S(1)}, u32[]{:S(2)}, u32[]{:S(2)}) collective-permute-start(bf16[272,128]{1,0:T(8,128)(2,1)S(1)} %get-tuple-element.36), channel_id=1, source_target_pairs={{0,6},{1,7},{2,4},{3,5},{4,2},{5,3},{6,0},{7,1},{8,14},{9,15},{10,... | collective-permute-start | bytes 208904 | tf_op jit(solution)/shard_map/ppermute | solution.py:30
  34.6 10.8 %collective-permute-start.9 = (bf16[272,128]{1,0:T(8,128)(2,1)S(1)}, bf16[272,128]{1,0:T(8,128)(2,1)S(1)}, u32[]{:S(2)}, u32[]{:S(2)}) collective-permute-start(bf16[272,128]{1,0:T(8,128)(2,1)S(1)} %get-tuple-element.37), channel_id=1, source_target_pairs={{0,4},{1,5},{2,6},{3,7},{4,0},{5,1},{6,2},{7,3},{8,12},{9,13},{10,... | collective-permute-start | bytes 208904 | tf_op jit(solution)/shard_map/ppermute | solution.py:30
  35.9 9.5 %collective-permute-start.13 = (bf16[128,256]{1,0:T(8,128)(2,1)S(1)}, bf16[128,256]{1,0:T(8,128)(2,1)S(1)}, u32[]{:S(2)}, u32[]{:S(2)}) collective-permute-start(bf16[128,256]{1,0:T(8,128)(2,1)S(1)} %get-tuple-element.43), channel_id=1, source_target_pairs={{0,4},{1,5},{2,6},{3,7},{4,0},{5,1},{6,2},{7,3},{8,12},{9,13},{10,... | collective-permute-start | bytes 196616 | tf_op jit(solution)/shard_map/ppermute | solution.py:30
  37.5 7.8 %collective-permute-start.14 = (bf16[128,256]{1,0:T(8,128)(2,1)S(1)}, bf16[128,256]{1,0:T(8,128)(2,1)S(1)}, u32[]{:S(2)}, u32[]{:S(2)}) collective-permute-start(bf16[128,256]{1,0:T(8,128)(2,1)S(1)} %get-tuple-element.44), channel_id=1, source_target_pairs={{0,2},{1,3},{2,0},{3,1},{4,6},{5,7},{6,4},{7,5},{8,10},{9,11},{10,... | collective-permute-start | bytes 196616 | tf_op jit(solution)/shard_map/ppermute | solution.py:30
  45.7 7.5 %collective-permute-start.18 = (bf16[144,256]{1,0:T(8,128)(2,1)S(1)}, bf16[144,256]{1,0:T(8,128)(2,1)S(1)}, u32[]{:S(2)}, u32[]{:S(2)}) collective-permute-start(bf16[144,256]{1,0:T(8,128)(2,1)S(1)} %shard_map.106.refs_0_.refs_8_), channel_id=1, source_target_pairs={{0,4},{1,5},{2,6},{3,7},{4,0},{5,1},{6,2},{7,3},{8,12},{9,13},{10,... | collective-permute-start | bytes 221192 | tf_op jit(solution)/shard_map/ppermute | solution.py:30
  45.8 7.4 %collective-permute-start.20 = (bf16[144,256]{1,0:T(8,128)(2,1)S(1)}, bf16[144,256]{1,0:T(8,128)(2,1)S(1)}, u32[]{:S(2)}, u32[]{:S(2)}) collective-permute-start(bf16[144,256]{1,0:T(8,128)(2,1)S(1)} %shard_map.106.refs_0_.refs_8_), channel_id=1, source_target_pairs={{0,6},{1,7},{2,4},{3,5},{4,2},{5,3},{6,0},{7,1},{8,14},{9,15},{10,... | collective-permute-start | bytes 221192 | tf_op jit(solution)/shard_map/ppermute | solution.py:30
  47.7 6.4 %collective-permute-start.16 = (bf16[144,256]{1,0:T(8,128)(2,1)S(1)}, bf16[144,256]{1,0:T(8,128)(2,1)S(1)}, u32[]{:S(2)}, u32[]{:S(2)}) collective-permute-start(bf16[144,256]{1,0:T(8,128)(2,1)S(1)} %shard_map.106.refs_0_.refs_8_), channel_id=1, source_target_pairs={{0,2},{1,3},{2,0},{3,1},{4,6},{5,7},{6,4},{7,5},{8,10},{9,11},{10,... | collective-permute-start | bytes 221192 | tf_op jit(solution)/shard_map/ppermute | solution.py:30
  54.2 16.2 %collective-permute-start.22 = (bf16[6,128,256]{2,1,0:T(8,128)(2,1)S(1)}, bf16[6,128,256]{2,1,0:T(8,128)(2,1)S(1)}, u32[]{:S(2)}, u32[]{:S(2)}) collective-permute-start(bf16[6,128,256]{2,1,0:T(8,128)(2,1)S(1)} %shard_map.108.refs_0_), channel_id=1, source_target_pairs={{0,8},{8,0},{16,24},{24,16},{1,9},{9,1},{17,25},{25,17},{2,10},{10... | collective-permute-start | bytes 1179656 | tf_op jit(solution)/shard_map/ppermute | solution.py:30
  55.7 18.9 %collective-permute-start.23 = (bf16[6,128,256]{2,1,0:T(8,128)(2,1)S(1)}, bf16[6,128,256]{2,1,0:T(8,128)(2,1)S(1)}, u32[]{:S(2)}, u32[]{:S(2)}) collective-permute-start(bf16[6,128,256]{2,1,0:T(8,128)(2,1)S(1)} %shard_map.108.refs_0_), channel_id=1, source_target_pairs={{0,16},{8,24},{16,0},{24,8},{1,17},{9,25},{17,1},{25,9},{2,18},{10... | collective-permute-start | bytes 1179656 | tf_op jit(solution)/shard_map/ppermute | solution.py:30
  57.2 17.4 %collective-permute-start.24 = (bf16[6,128,256]{2,1,0:T(8,128)(2,1)S(1)}, bf16[6,128,256]{2,1,0:T(8,128)(2,1)S(1)}, u32[]{:S(2)}, u32[]{:S(2)}) collective-permute-start(bf16[6,128,256]{2,1,0:T(8,128)(2,1)S(1)} %shard_map.108.refs_0_), channel_id=1, source_target_pairs={{0,24},{8,16},{16,8},{24,0},{1,25},{9,17},{17,9},{25,1},{2,26},{10... | collective-permute-start | bytes 1179656 | tf_op jit(solution)/shard_map/ppermute | solution.py:30
  57.7 6.6 %collective-permute-start.31 = (bf16[128,256]{1,0:T(8,128)(2,1)S(1)}, bf16[128,256]{1,0:T(8,128)(2,1)S(1)}, u32[]{:S(2)}, u32[]{:S(2)}) collective-permute-start(bf16[128,256]{1,0:T(8,128)(2,1)S(1)} %shard_map.105.refs_4_), channel_id=1, source_target_pairs={{0,4},{1,5},{2,6},{3,7},{4,0},{5,1},{6,2},{7,3},{8,12},{9,13},{10,... | collective-permute-start | bytes 196616 | tf_op jit(solution)/shard_map/ppermute | solution.py:30
  59.0 6.4 %collective-permute-start.33 = (bf16[128,256]{1,0:T(8,128)(2,1)S(1)}, bf16[128,256]{1,0:T(8,128)(2,1)S(1)}, u32[]{:S(2)}, u32[]{:S(2)}) collective-permute-start(bf16[128,256]{1,0:T(8,128)(2,1)S(1)} %shard_map.105.refs_4_), channel_id=1, source_target_pairs={{0,6},{1,7},{2,4},{3,5},{4,2},{5,3},{6,0},{7,1},{8,14},{9,15},{10,... | collective-permute-start | bytes 196616 | tf_op jit(solution)/shard_map/ppermute | solution.py:30
  69.9 5.3 %collective-permute-start.30 = (bf16[128,256]{1,0:T(8,128)(2,1)S(1)}, bf16[128,256]{1,0:T(8,128)(2,1)S(1)}, u32[]{:S(2)}, u32[]{:S(2)}) collective-permute-start(bf16[128,256]{1,0:T(8,128)(2,1)S(1)} %collective-permute-done.29.refs_6_), channel_id=1, source_target_pairs={{0,1},{1,0},{2,3},{3,2},{4,5},{5,4},{6,7},{7,6},{8,9},{9,8},{10,11... | collective-permute-start | bytes 196616 | tf_op jit(solution)/shard_map/ppermute | solution.py:30
  70.0 5.2 %collective-permute-start.19 = (bf16[144,256]{1,0:T(8,128)(2,1)S(1)}, bf16[144,256]{1,0:T(8,128)(2,1)S(1)}, u32[]{:S(2)}, u32[]{:S(2)}) collective-permute-start(bf16[144,256]{1,0:T(8,128)(2,1)S(1)} %collective-permute-done.18.refs_4_.refs_2_.refs_8_), channel_id=1, source_target_pairs={{0,1},{1,0},{2,3},{3,2},{4,5},{5,4},{6,7},{7,6},{8,9},{9,8},{10,11... | collective-permute-start | bytes 221192 | tf_op jit(solution)/shard_map/ppermute | solution.py:30
  70.4 28.0 %collective-permute-start.25 = (bf16[6,128,256]{2,1,0:T(8,128)(2,1)S(1)}, bf16[6,128,256]{2,1,0:T(8,128)(2,1)S(1)}, u32[]{:S(2)}, u32[]{:S(2)}) collective-permute-start(bf16[6,128,256]{2,1,0:T(8,128)(2,1)S(1)} %collective-permute-done.22.refs_1_), channel_id=1, source_target_pairs={{0,1},{1,0},{2,3},{3,2},{4,5},{5,4},{6,7},{7,6},{8,9},{9,8},{10,11... | collective-permute-start | bytes 1179656 | tf_op jit(solution)/shard_map/ppermute | solution.py:30
  74.6 23.8 %collective-permute-start.26 = (bf16[6,128,256]{2,1,0:T(8,128)(2,1)S(1)}, bf16[6,128,256]{2,1,0:T(8,128)(2,1)S(1)}, u32[]{:S(2)}, u32[]{:S(2)}) collective-permute-start(bf16[6,128,256]{2,1,0:T(8,128)(2,1)S(1)} %collective-permute-done.23.refs_2_), channel_id=1, source_target_pairs={{0,1},{1,0},{2,3},{3,2},{4,5},{5,4},{6,7},{7,6},{8,9},{9,8},{10,11... | collective-permute-start | bytes 1179656 | tf_op jit(solution)/shard_map/ppermute | solution.py:30
  74.6 23.8 %collective-permute-start.27 = (bf16[6,128,256]{2,1,0:T(8,128)(2,1)S(1)}, bf16[6,128,256]{2,1,0:T(8,128)(2,1)S(1)}, u32[]{:S(2)}, u32[]{:S(2)}) collective-permute-start(bf16[6,128,256]{2,1,0:T(8,128)(2,1)S(1)} %collective-permute-done.24.refs_3_), channel_id=1, source_target_pairs={{0,1},{1,0},{2,3},{3,2},{4,5},{5,4},{6,7},{7,6},{8,9},{9,8},{10,11... | collective-permute-start | bytes 1179656 | tf_op jit(solution)/shard_map/ppermute | solution.py:30
  75.2 6.2 %collective-permute-start.15 = (bf16[144,256]{1,0:T(8,128)(2,1)S(1)}, bf16[144,256]{1,0:T(8,128)(2,1)S(1)}, u32[]{:S(2)}, u32[]{:S(2)}) collective-permute-start(bf16[144,256]{1,0:T(8,128)(2,1)S(1)} %shard_map.106.refs_0_.refs_8_), channel_id=1, source_target_pairs={{0,1},{1,0},{2,3},{3,2},{4,5},{5,4},{6,7},{7,6},{8,9},{9,8},{10,11... | collective-permute-start | bytes 221192 | tf_op jit(solution)/shard_map/ppermute | solution.py:30
  77.0 4.9 %collective-permute-start.17 = (bf16[144,256]{1,0:T(8,128)(2,1)S(1)}, bf16[144,256]{1,0:T(8,128)(2,1)S(1)}, u32[]{:S(2)}, u32[]{:S(2)}) collective-permute-start(bf16[144,256]{1,0:T(8,128)(2,1)S(1)} %collective-permute-done.16.refs_2_.refs_1_.refs_10_), channel_id=1, source_target_pairs={{0,1},{1,0},{2,3},{3,2},{4,5},{5,4},{6,7},{7,6},{8,9},{9,8},{10,11... | collective-permute-start | bytes 221192 | tf_op jit(solution)/shard_map/ppermute | solution.py:30
  81.4 4.9 %collective-permute-start.36 = (bf16[2,256,128]{2,1,0:T(8,128)(2,1)S(1)}, bf16[2,256,128]{2,1,0:T(8,128)(2,1)S(1)}, u32[]{:S(2)}, u32[]{:S(2)}) collective-permute-start(bf16[2,256,128]{2,1,0:T(8,128)(2,1)S(1)} %get-tuple-element.51), channel_id=1, source_target_pairs={{0,1},{1,0},{2,3},{3,2},{4,5},{5,4},{6,7},{7,6},{8,9},{9,8},{10,11... | collective-permute-start | bytes 393224 | tf_op jit(solution)/shard_map/ppermute | solution.py:30
  86.4 6.9 %collective-permute-start.37 = (bf16[256,128]{1,0:T(8,128)(2,1)S(1)}, bf16[256,128]{1,0:T(8,128)(2,1)S(1)}, u32[]{:S(2)}, u32[]{:S(2)}) collective-permute-start(bf16[256,128]{1,0:T(8,128)(2,1)S(1)} %get-tuple-element.52), channel_id=1, source_target_pairs={{0,6},{1,7},{2,4},{3,5},{4,2},{5,3},{6,0},{7,1},{8,14},{9,15},{10,... | collective-permute-start | bytes 196616 | tf_op jit(solution)/shard_map/ppermute | solution.py:30
  87.7 9.3 %collective-permute-start.38 = (bf16[256,128]{1,0:T(8,128)(2,1)S(1)}, bf16[256,128]{1,0:T(8,128)(2,1)S(1)}, u32[]{:S(2)}, u32[]{:S(2)}) collective-permute-start(bf16[256,128]{1,0:T(8,128)(2,1)S(1)} %get-tuple-element.53), channel_id=1, source_target_pairs={{0,4},{1,5},{2,6},{3,7},{4,0},{5,1},{6,2},{7,3},{8,12},{9,13},{10,... | collective-permute-start | bytes 196616 | tf_op jit(solution)/shard_map/ppermute | solution.py:30
  (16 other events, 78.3 us)

commit v2 on v1

--- a/solution.py
+++ b/solution.py
@@ -296,13 +296,13 @@
 
 def weight_grad_kernel(size, groups, answers, me_ref, *refs):
     half = size // 2
+    cots, refs = refs[:groups], refs[groups:]
     packs, packs_odd, own = refs[:groups], refs[groups : 2 * groups - 1], refs[2 * groups - 1 : 2 * groups - 1 + half]
     out_ref, cot_buf, out_buf, sem = refs[2 * groups - 1 + half :]
     me = me_ref[0]
     width = out_buf.shape[2]
     for g in range(groups):
-        for r in range(cot_buf.shape[0] // width):
-            cot_buf[r * width : (r + 1) * width, g * answers : (g + 1) * answers] = packs[g][half + r].T
+        cot_buf[:, g * answers : (g + 1) * answers] = cots[g][...].T
 
     def out_copy(s):
         return pltpu.make_async_copy(out_buf.at[s], columns_of(out_ref, me, s, width), sem.at[s])
@@ -319,13 +319,10 @@
         out_copy(s).wait()
 
 
-def pack_kernel(half, cot_ref, *refs):
-    out_ref = refs[half]
-    answers, width = out_ref.shape[1:]
-    for k in range(half):
-        out_ref[k] = refs[k][:answers, :]
-    for r in range(cot_ref.shape[1] // width):
-        out_ref[half + r] = cot_ref[:, r * width : (r + 1) * width]
+def pack_kernel(*refs):
+    out_ref = refs[-1]
+    for k in range(out_ref.shape[0]):
+        out_ref[k] = refs[k][: out_ref.shape[1], :]
 
 
 def shaped(shape, dtype):
@@ -369,7 +366,7 @@
             pltpu.SemaphoreType.DMA((3, size)),
             pltpu.SemaphoreType.DMA(()),
         ],
-        vmem=12,
+        vmem=49,
     )
     g_other = swap(g_odd, "psg", size, 1)
     block = shaped((answers, width), bf16)
@@ -456,14 +453,8 @@
     dq_parts = [swap(sums[d // 2], "psg", size, d) for d in far_first(size)]
     query_grad = call(add_all_transposed_kernel, sums[0], *dq_parts, out=block, ins=[VMEM] * half, outs=VMEM)
 
-    pack = call(
-        functools.partial(pack_kernel, half),
-        cot,
-        *c_even,
-        out=shaped((half + model // width, answers, width), bf16),
-        ins=[VMEM] * (half + 1),
-        outs=VMEM,
-    )
+    pack = call(pack_kernel, *c_even, out=shaped((half, answers, width), bf16), ins=[VMEM] * half, outs=VMEM)
+    cots = [cot] + [swap(cot, "dp", dp, d) for d in range(1, dp)]
     packs = [pack] + [swap(pack, "dp", dp, d) for d in range(1, dp)]
     packs_odd = [swap(packs[d], "psg", size, 1) for d in range(1, dp)]
     layer_out = call(
@@ -479,11 +470,12 @@
     weight_grad = call(
         functools.partial(weight_grad_kernel, size, dp, answers),
         me,
+        *cots,
         *packs,
         *packs_odd,
         *c_odd,
         out=shaped((model, inner), f32),
-        ins=[SMEM] + [VMEM] * (2 * dp - 1 + half),
+        ins=[SMEM] + [VMEM] * (3 * dp - 1 + half),
         outs=ANY,
         scratch=[
             pltpu.VMEM((model, dp * answers), bf16),

time: 101 us -> 87.9 us (0.87)
  waiting for transfers between devices: 36.8 us -> 24.8 us
  local copies, waits for them, and re-layouts: 5.69 us -> 0.92 us
  starting transfers between devices: 32.3 us -> 35.8 us
    ppermute x40 -> x43, waiting for transfers between devices: 36.8 us -> 24.8 us  [swap(): return lax.ppermute(x, axis, [(j, j ^ distance) for j in range(size)])]
    unnamed x16 -> x8, local copies, waits for them, and re-layouts: 5.69 us -> 0.92 us
    ppermute x40 -> x43, starting transfers between devices: 32.3 us -> 35.8 us  [swap(): return lax.ppermute(x, axis, [(j, j ^ distance) for j in range(size)])]
  transfers between devices with their start and end apart: 40 -> 43, of which waited for: 13 -> 13; matrix products, arithmetic and copies ran while one was open for 0% -> 0% of each run, Pallas kernels for 22% -> 26%
where the time goes in v2:
time: 87.9 us; the launch traced here: 87.7 us
  starting transfers between devices  35.8 us (41%)
  Pallas kernels  25.4 us (29%)
  waiting for transfers between devices  24.8 us (28%)
  local copies, waits for them, and re-layouts  0.92 us (1%)
    ppermute x43, starting transfers between devices, swap(): return lax.ppermute(x, axis, [(j, j ^ distance) for j in range(size)])  35.8 us
    pallas_call x14, Pallas kernels, call(): pl.pallas_call(kernel, out_shape=out, in_specs=ins, out_specs=outs, scrat...  25.4 us
    ppermute x43, waiting for transfers between devices, swap(): return lax.ppermute(x, axis, [(j, j ^ distance) for j in range(size)])  24.8 us
  transfers between devices with their start and end apart: 43, of which 13 were waited for; matrix products, arithmetic and copies ran while one was open for 0% of the time, Pallas kernels for 26%

profile of v2, /device:TPU:0, one launch (start us, length us, event | category | flops | bytes accessed | tf_op | source)
XLA Modules:
  0.0 87.7 jit_solution(9314481905166164964)
XLA Ops:
  0.6 3.1 %collective-permute-start.1 = (bf16[128,256]{1,0:T(8,128)(2,1)}, bf16[128,256]{1,0:T(8,128)(2,1)S(1)}, u32[]{:S(2)}, u32[]{:S(2)}) collective-permute-start(bf16[128,256]{1,0:T(8,128)(2,1)} %bitcast.14), channel_id=1, source_target_pairs={{0,2},{1,3},{2,0},{3,1},{4,6},{5,7},{6,4},{7,5},{8,10},{9,11},{10,... | collective-permute-start | bytes 196616 | tf_op jit(solution)/shard_map/ppermute | solution.py:30
  3.8 2.6 %collective-permute-start.3 = (bf16[128,256]{1,0:T(8,128)(2,1)}, bf16[128,256]{1,0:T(8,128)(2,1)S(1)}, u32[]{:S(2)}, u32[]{:S(2)}) collective-permute-start(bf16[128,256]{1,0:T(8,128)(2,1)} %bitcast.15), channel_id=1, source_target_pairs={{0,4},{1,5},{2,6},{3,7},{4,0},{5,1},{6,2},{7,3},{8,12},{9,13},{10,... | collective-permute-start | bytes 196616 | tf_op jit(solution)/shard_map/ppermute | solution.py:30
  6.9 4.4 %collective-permute-done.3.refs_4_.refs_0_ = bf16[128,256]{1,0:T(8,128)(2,1)S(1)} collective-permute-done((bf16[128,256]{1,0:T(8,128)(2,1)}, bf16[128,256]{1,0:T(8,128)(2,1)S(1)}, u32[]{:S(2)}, u32[]{:S(2)}) %collective-permute-start.3) | collective-permute-done | bytes 65568 | tf_op jit(solution)/shard_map/ppermute | solution.py:30
  11.2 1.4 %collective-permute-done.5.refs_6_.refs_2_ = bf16[128,256]{1,0:T(8,128)(2,1)S(1)} collective-permute-done((bf16[128,256]{1,0:T(8,128)(2,1)}, bf16[128,256]{1,0:T(8,128)(2,1)S(1)}, u32[]{:S(2)}, u32[]{:S(2)}) %collective-permute-start.5) | collective-permute-done | bytes 65568 | tf_op jit(solution)/shard_map/ppermute | solution.py:30
  13.6 3.2 %shard_map.101 = (bf16[4,128,256]{2,1,0:T(8,128)(2,1)S(1)}, bf16[4,128,256]{2,1,0:T(8,128)(2,1)S(1)}, bf16[8,512,256]{2,1,0:T(8,128)(2,1)S(1)}, bf16[8,512,256]{2,1,0:T(8,128)(2,1)S(1)}) custom-call(s32[1]{0:T(128)} %bitcast.me_ref, bf16[128,512]{1,0:T(8,128)(2,1)S(1)} %bitcast.9, bf16[512,2048]{1,0:T(8,128)(2,1)} %refs_8_.1, bf16[512,2048]{1,0:T(8,128)(2,1)} %bitcast.20, ...), custom_call_target="tpu_custom_call" | custom-call | tf_op jit(solution)/shard_map/pallas_call | solution.py:34
  17.4 7.7 %shard_map.102 = (bf16[4,272,128]{2,1,0:T(8,128)(2,1)S(1)}, bf16[4,272,128]{2,1,0:T(8,128)(2,1)S(1)}) custom-call(s32[1,2]{1,0:T(1,128)S(1)} %copy-done.3, bf16[128,256]{1,0:T(8,128)(2,1)S(1)} %bitcast.18, bf16[128,256]{1,0:T(8,128)(2,1)S(1)} %collective-permute-done.refs_1_, bf16[128,256]{1,0:T(8,128)(2,1)S(1)} %collective-permute-done.1.refs_2_, ...), custom_call_target="tpu_custom_call" | custom-call | tf_op jit(solution)/shard_map/pallas_call | solution.py:34
  25.3 2.3 %collective-permute-start.12 = (bf16[128,256]{1,0:T(8,128)(2,1)S(1)}, bf16[128,256]{1,0:T(8,128)(2,1)S(1)}, u32[]{:S(2)}, u32[]{:S(2)}) collective-permute-start(bf16[128,256]{1,0:T(8,128)(2,1)S(1)} %get-tuple-element.42), channel_id=1, source_target_pairs={{0,6},{1,7},{2,4},{3,5},{4,2},{5,3},{6,0},{7,1},{8,14},{9,15},{10,... | collective-permute-start | bytes 196616 | tf_op jit(solution)/shard_map/ppermute | solution.py:30
  27.6 2.1 %collective-permute-start.14 = (bf16[128,256]{1,0:T(8,128)(2,1)S(1)}, bf16[128,256]{1,0:T(8,128)(2,1)S(1)}, u32[]{:S(2)}, u32[]{:S(2)}) collective-permute-start(bf16[128,256]{1,0:T(8,128)(2,1)S(1)} %get-tuple-element.44), channel_id=1, source_target_pairs={{0,2},{1,3},{2,0},{3,1},{4,6},{5,7},{6,4},{7,5},{8,10},{9,11},{10,... | collective-permute-start | bytes 196616 | tf_op jit(solution)/shard_map/ppermute | solution.py:30
  30.0 2.3 %collective-permute-start.8 = (bf16[272,128]{1,0:T(8,128)(2,1)S(1)}, bf16[272,128]{1,0:T(8,128)(2,1)S(1)}, u32[]{:S(2)}, u32[]{:S(2)}) collective-permute-start(bf16[272,128]{1,0:T(8,128)(2,1)S(1)} %get-tuple-element.36), channel_id=1, source_target_pairs={{0,6},{1,7},{2,4},{3,5},{4,2},{5,3},{6,0},{7,1},{8,14},{9,15},{10,... | collective-permute-start | bytes 208904 | tf_op jit(solution)/shard_map/ppermute | solution.py:30
  32.3 1.6 %collective-permute-start.9 = (bf16[272,128]{1,0:T(8,128)(2,1)S(1)}, bf16[272,128]{1,0:T(8,128)(2,1)S(1)}, u32[]{:S(2)}, u32[]{:S(2)}) collective-permute-start(bf16[272,128]{1,0:T(8,128)(2,1)S(1)} %get-tuple-element.37), channel_id=1, source_target_pairs={{0,4},{1,5},{2,6},{3,7},{4,0},{5,1},{6,2},{7,3},{8,12},{9,13},{10,... | collective-permute-start | bytes 208904 | tf_op jit(solution)/shard_map/ppermute | solution.py:30
  34.6 1.0 %collective-permute-start.34 = (bf16[128,256]{1,0:T(8,128)(2,1)S(1)}, bf16[128,256]{1,0:T(8,128)(2,1)S(1)}, u32[]{:S(2)}, u32[]{:S(2)}) collective-permute-start(bf16[128,256]{1,0:T(8,128)(2,1)S(1)} %shard_map.105.refs_4_), channel_id=1, source_target_pairs={{0,4},{1,5},{2,6},{3,7},{4,0},{5,1},{6,2},{7,3},{8,12},{9,13},{10,... | collective-permute-start | bytes 196616 | tf_op jit(solution)/shard_map/ppermute | solution.py:30
  35.6 2.1 %collective-permute-start.36 = (bf16[128,256]{1,0:T(8,128)(2,1)S(1)}, bf16[128,256]{1,0:T(8,128)(2,1)S(1)}, u32[]{:S(2)}, u32[]{:S(2)}) collective-permute-start(bf16[128,256]{1,0:T(8,128)(2,1)S(1)} %shard_map.105.refs_4_), channel_id=1, source_target_pairs={{0,6},{1,7},{2,4},{3,5},{4,2},{5,3},{6,0},{7,1},{8,14},{9,15},{10,... | collective-permute-start | bytes 196616 | tf_op jit(solution)/shard_map/ppermute | solution.py:30
  38.1 5.6 %collective-permute-done.9.refs_2_ = bf16[272,128]{1,0:T(8,128)(2,1)S(1)} collective-permute-done((bf16[272,128]{1,0:T(8,128)(2,1)S(1)}, bf16[272,128]{1,0:T(8,128)(2,1)S(1)}, u32[]{:S(2)}, u32[]{:S(2)}) %collective-permute-start.9) | collective-permute-done | bytes 69664 | tf_op jit(solution)/shard_map/ppermute | solution.py:30
  44.1 1.0 %collective-permute-done.34.refs_4_ = bf16[128,256]{1,0:T(8,128)(2,1)S(1)} collective-permute-done((bf16[128,256]{1,0:T(8,128)(2,1)S(1)}, bf16[128,256]{1,0:T(8,128)(2,1)S(1)}, u32[]{:S(2)}, u32[]{:S(2)}) %collective-permute-start.34) | collective-permute-done | bytes 65568 | tf_op jit(solution)/shard_map/ppermute | solution.py:30
  45.2 2.1 %collective-permute-start.20 = (bf16[144,256]{1,0:T(8,128)(2,1)S(1)}, bf16[144,256]{1,0:T(8,128)(2,1)S(1)}, u32[]{:S(2)}, u32[]{:S(2)}) collective-permute-start(bf16[144,256]{1,0:T(8,128)(2,1)S(1)} %shard_map.106.refs_0_.refs_8_), channel_id=1, source_target_pairs={{0,6},{1,7},{2,4},{3,5},{4,2},{5,3},{6,0},{7,1},{8,14},{9,15},{10,... | collective-permute-start | bytes 221192 | tf_op jit(solution)/shard_map/ppermute | solution.py:30
  47.3 1.5 %collective-permute-start.16 = (bf16[144,256]{1,0:T(8,128)(2,1)S(1)}, bf16[144,256]{1,0:T(8,128)(2,1)S(1)}, u32[]{:S(2)}, u32[]{:S(2)}) collective-permute-start(bf16[144,256]{1,0:T(8,128)(2,1)S(1)} %shard_map.106.refs_0_.refs_8_), channel_id=1, source_target_pairs={{0,2},{1,3},{2,0},{3,1},{4,6},{5,7},{6,4},{7,5},{8,10},{9,11},{10,... | collective-permute-start | bytes 221192 | tf_op jit(solution)/shard_map/ppermute | solution.py:30
  49.9 2.2 %collective-permute-done.20.refs_6_.refs_3_.refs_10_ = bf16[144,256]{1,0:T(8,128)(2,1)S(1)} collective-permute-done((bf16[144,256]{1,0:T(8,128)(2,1)S(1)}, bf16[144,256]{1,0:T(8,128)(2,1)S(1)}, u32[]{:S(2)}, u32[]{:S(2)}) %collective-permute-start.20) | collective-permute-done | bytes 73760 | tf_op jit(solution)/shard_map/ppermute | solution.py:30
  52.1 1.1 %collective-permute-done.16.refs_2_.refs_1_.refs_10_ = bf16[144,256]{1,0:T(8,128)(2,1)S(1)} collective-permute-done((bf16[144,256]{1,0:T(8,128)(2,1)S(1)}, bf16[144,256]{1,0:T(8,128)(2,1)S(1)}, u32[]{:S(2)}, u32[]{:S(2)}) %collective-permute-start.16) | collective-permute-done | bytes 73760 | tf_op jit(solution)/shard_map/ppermute | solution.py:30
  53.3 1.6 %collective-permute-start.25 = (bf16[4,128,256]{2,1,0:T(8,128)(2,1)S(1)}, bf16[4,128,256]{2,1,0:T(8,128)(2,1)S(1)}, u32[]{:S(2)}, u32[]{:S(2)}) collective-permute-start(bf16[4,128,256]{2,1,0:T(8,128)(2,1)S(1)} %shard_map.108.refs_4_), channel_id=1, source_target_pairs={{0,8},{8,0},{16,24},{24,16},{1,9},{9,1},{17,25},{25,17},{2,10},{10... | collective-permute-start | bytes 786440 | tf_op jit(solution)/shard_map/ppermute | solution.py:30
  54.8 1.5 %collective-permute-start.26 = (bf16[4,128,256]{2,1,0:T(8,128)(2,1)S(1)}, bf16[4,128,256]{2,1,0:T(8,128)(2,1)S(1)}, u32[]{:S(2)}, u32[]{:S(2)}) collective-permute-start(bf16[4,128,256]{2,1,0:T(8,128)(2,1)S(1)} %shard_map.108.refs_4_), channel_id=1, source_target_pairs={{0,16},{8,24},{16,0},{24,8},{1,17},{9,25},{17,1},{25,9},{2,18},{10... | collective-permute-start | bytes 786440 | tf_op jit(solution)/shard_map/ppermute | solution.py:30
  56.8 4.3 %shard_map.110 = (bf16[512,2048]{1,0:T(8,128)(2,1)}, bf16[512,2048]{1,0:T(8,128)(2,1)}, bf16[2,256,128]{2,1,0:T(8,128)(2,1)S(1)}, bf16[2,256,128]{2,1,0:T(8,128)(2,1)S(1)}) custom-call(s32[1]{0:T(128)} %bitcast.me_ref, s32[1,2]{1,0:T(1,128)S(1)} %copy-done.3, bf16[128,256]{1,0:T(8,128)(2,1)S(1)} %collective-permute-done.3.refs_4_.refs_0_, ...), custom_call_target="tpu_custom_call" | custom-call | tf_op jit(solution)/shard_map/pallas_call | solution.py:34
  61.7 4.3 %shard_map.111 = (bf16[512,2048]{1,0:T(8,128)(2,1)}, bf16[512,2048]{1,0:T(8,128)(2,1)}, bf16[2,256,128]{2,1,0:T(8,128)(2,1)S(1)}, bf16[2,256,128]{2,1,0:T(8,128)(2,1)S(1)}) custom-call(s32[1]{0:T(128)} %bitcast.me_ref, s32[1,2]{1,0:T(1,128)S(1)} %copy-done.3, bf16[128,256]{1,0:T(8,128)(2,1)S(1)} %bitcast.19, ...), custom_call_target="tpu_custom_call", output_to_operand_aliasing={{0}: (16, {}), {1}: (17, {})} | custom-call | tf_op jit(solution)/shard_map/pallas_call | solution.py:34
  66.1 1.5 %collective-permute-start.22 = (bf16[128,512]{1,0:T(8,128)(2,1)S(1)}, bf16[128,512]{1,0:T(8,128)(2,1)S(1)}, u32[]{:S(2)}, u32[]{:S(2)}) collective-permute-start(bf16[128,512]{1,0:T(8,128)(2,1)S(1)} %bitcast.10), channel_id=1, source_target_pairs={{0,8},{8,0},{16,24},{24,16},{1,9},{9,1},{17,25},{25,17},{2,10},{10... | collective-permute-start | bytes 393224 | tf_op jit(solution)/shard_map/ppermute | solution.py:30
  67.7 1.8 %collective-permute-start.40 = (bf16[256,128]{1,0:T(8,128)(2,1)S(1)}, bf16[256,128]{1,0:T(8,128)(2,1)S(1)}, u32[]{:S(2)}, u32[]{:S(2)}) collective-permute-start(bf16[256,128]{1,0:T(8,128)(2,1)S(1)} %get-tuple-element.52), channel_id=1, source_target_pairs={{0,6},{1,7},{2,4},{3,5},{4,2},{5,3},{6,0},{7,1},{8,14},{9,15},{10,... | collective-permute-start | bytes 196616 | tf_op jit(solution)/shard_map/ppermute | solution.py:30
  70.1 1.8 %collective-permute-done.22.refs_1_ = bf16[128,512]{1,0:T(8,128)(2,1)S(1)} collective-permute-done((bf16[128,512]{1,0:T(8,128)(2,1)S(1)}, bf16[128,512]{1,0:T(8,128)(2,1)S(1)}, u32[]{:S(2)}, u32[]{:S(2)}) %collective-permute-start.22) | collective-permute-done | bytes 131104 | tf_op jit(solution)/shard_map/ppermute | solution.py:30
  72.0 0.9 %collective-permute-start.41 = (bf16[256,128]{1,0:T(8,128)(2,1)S(1)}, bf16[256,128]{1,0:T(8,128)(2,1)S(1)}, u32[]{:S(2)}, u32[]{:S(2)}) collective-permute-start(bf16[256,128]{1,0:T(8,128)(2,1)S(1)} %get-tuple-element.53), channel_id=1, source_target_pairs={{0,4},{1,5},{2,6},{3,7},{4,0},{5,1},{6,2},{7,3},{8,12},{9,13},{10,... | collective-permute-start | bytes 196616 | tf_op jit(solution)/shard_map/ppermute | solution.py:30
  74.3 3.4 %collective-permute-done.41.refs_2_ = bf16[256,128]{1,0:T(8,128)(2,1)S(1)} collective-permute-done((bf16[256,128]{1,0:T(8,128)(2,1)S(1)}, bf16[256,128]{1,0:T(8,128)(2,1)S(1)}, u32[]{:S(2)}, u32[]{:S(2)}) %collective-permute-start.41) | collective-permute-done | bytes 65568 | tf_op jit(solution)/shard_map/ppermute | solution.py:30
  77.7 1.5 %collective-permute-start.23 = (bf16[128,512]{1,0:T(8,128)(2,1)S(1)}, bf16[128,512]{1,0:T(8,128)(2,1)S(1)}, u32[]{:S(2)}, u32[]{:S(2)}) collective-permute-start(bf16[128,512]{1,0:T(8,128)(2,1)S(1)} %bitcast.11), channel_id=1, source_target_pairs={{0,16},{8,24},{16,0},{24,8},{1,17},{9,25},{17,1},{25,9},{2,18},{10... | collective-permute-start | bytes 393224 | tf_op jit(solution)/shard_map/ppermute | solution.py:30
  79.3 1.4 %collective-permute-start.24 = (bf16[128,512]{1,0:T(8,128)(2,1)S(1)}, bf16[128,512]{1,0:T(8,128)(2,1)S(1)}, u32[]{:S(2)}, u32[]{:S(2)}) collective-permute-start(bf16[128,512]{1,0:T(8,128)(2,1)S(1)} %bitcast.12), channel_id=1, source_target_pairs={{0,24},{8,16},{16,8},{24,0},{1,25},{9,17},{17,9},{25,1},{2,26},{10... | collective-permute-start | bytes 393224 | tf_op jit(solution)/shard_map/ppermute | solution.py:30
  80.7 2.1 %shard_map.107 = bf16[128,512]{1,0:T(8,128)(2,1)} custom-call(s32[1]{0:T(128)} %bitcast.me_ref, bf16[144,256]{1,0:T(8,128)(2,1)S(1)} %shard_map.106.refs_0_.refs_8_, bf16[144,256]{1,0:T(8,128)(2,1)S(1)} %collective-permute-done.15.refs_1_.refs_11_.refs_9_, bf16[144,256]{1,0:T(8,128)(2,1)S(1)} %collective-permute-done.16.refs_2_.refs_1_.refs_10_, ...), custom_call_target="tpu_custom_call" | custom-call | tf_op jit(solution)/shard_map/pallas_call | solution.py:34
  84.0 1.1 %collective-permute-done.24.refs_3_ = bf16[128,512]{1,0:T(8,128)(2,1)S(1)} collective-permute-done((bf16[128,512]{1,0:T(8,128)(2,1)S(1)}, bf16[128,512]{1,0:T(8,128)(2,1)S(1)}, u32[]{:S(2)}, u32[]{:S(2)}) %collective-permute-start.24) | collective-permute-done | bytes 131104 | tf_op jit(solution)/shard_map/ppermute | solution.py:30
  85.1 2.6 %shard_map.109 = f32[512,2048]{1,0:T(8,128)} custom-call(s32[1]{0:T(128)} %bitcast.me_ref, bf16[128,512]{1,0:T(8,128)(2,1)S(1)} %bitcast.13, bf16[128,512]{1,0:T(8,128)(2,1)S(1)} %collective-permute-done.22.refs_1_, bf16[128,512]{1,0:T(8,128)(2,1)S(1)} %collective-permute-done.23.refs_2_, bf16[128,512]{1,0:T(8,128)(2,1)S(1)} %collective-permute-done.24.refs_3_, ...), custom_call_target="tpu_custom_call" | custom-call | tf_op jit(solution)/shard_map/pallas_call | solution.py:34
  (76 shorter events, 9.4 us)
Async XLA Ops:
  0.6 5.7 %collective-permute-start.1 = (bf16[128,256]{1,0:T(8,128)(2,1)}, bf16[128,256]{1,0:T(8,128)(2,1)S(1)}, u32[]{:S(2)}, u32[]{:S(2)}) collective-permute-start(bf16[128,256]{1,0:T(8,128)(2,1)} %bitcast.14), channel_id=1, source_target_pairs={{0,2},{1,3},{2,0},{3,1},{4,6},{5,7},{6,4},{7,5},{8,10},{9,11},{10,... | collective-permute-start | bytes 196616 | tf_op jit(solution)/shard_map/ppermute | solution.py:30
  3.8 7.5 %collective-permute-start.3 = (bf16[128,256]{1,0:T(8,128)(2,1)}, bf16[128,256]{1,0:T(8,128)(2,1)S(1)}, u32[]{:S(2)}, u32[]{:S(2)}) collective-permute-start(bf16[128,256]{1,0:T(8,128)(2,1)} %bitcast.15), channel_id=1, source_target_pairs={{0,4},{1,5},{2,6},{3,7},{4,0},{5,1},{6,2},{7,3},{8,12},{9,13},{10,... | collective-permute-start | bytes 196616 | tf_op jit(solution)/shard_map/ppermute | solution.py:30
  6.3 6.3 %collective-permute-start.5 = (bf16[128,256]{1,0:T(8,128)(2,1)}, bf16[128,256]{1,0:T(8,128)(2,1)S(1)}, u32[]{:S(2)}, u32[]{:S(2)}) collective-permute-start(bf16[128,256]{1,0:T(8,128)(2,1)} %bitcast.16), channel_id=1, source_target_pairs={{0,6},{1,7},{2,4},{3,5},{4,2},{5,3},{6,0},{7,1},{8,14},{9,15},{10,... | collective-permute-start | bytes 196616 | tf_op jit(solution)/shard_map/ppermute | solution.py:30
  6.3 11.0 %collective-permute-start = (bf16[128,256]{1,0:T(8,128)(2,1)}, bf16[128,256]{1,0:T(8,128)(2,1)S(1)}, u32[]{:S(2)}, u32[]{:S(2)}) collective-permute-start(bf16[128,256]{1,0:T(8,128)(2,1)} %bitcast.17), channel_id=1, source_target_pairs={{0,1},{1,0},{2,3},{3,2},{4,5},{5,4},{6,7},{7,6},{8,9},{9,8},{10,11... | collective-permute-start | bytes 196616 | tf_op jit(solution)/shard_map/ppermute | solution.py:30
  6.4 11.0 %collective-permute-start.2 = (bf16[128,256]{1,0:T(8,128)(2,1)S(1)}, bf16[128,256]{1,0:T(8,128)(2,1)S(1)}, u32[]{:S(2)}, u32[]{:S(2)}) collective-permute-start(bf16[128,256]{1,0:T(8,128)(2,1)S(1)} %collective-permute-done.1.refs_2_), channel_id=1, source_target_pairs={{0,1},{1,0},{2,3},{3,2},{4,5},{5,4},{6,7},{7,6},{8,9},{9,8},{10,11... | collective-permute-start | bytes 196616 | tf_op jit(solution)/shard_map/ppermute | solution.py:30
  11.2 6.1 %collective-permute-start.4 = (bf16[128,256]{1,0:T(8,128)(2,1)S(1)}, bf16[128,256]{1,0:T(8,128)(2,1)S(1)}, u32[]{:S(2)}, u32[]{:S(2)}) collective-permute-start(bf16[128,256]{1,0:T(8,128)(2,1)S(1)} %collective-permute-done.3.refs_4_.refs_0_), channel_id=1, source_target_pairs={{0,1},{1,0},{2,3},{3,2},{4,5},{5,4},{6,7},{7,6},{8,9},{9,8},{10,11... | collective-permute-start | bytes 196616 | tf_op jit(solution)/shard_map/ppermute | solution.py:30
  16.8 8.4 %collective-permute-start.11 = (bf16[4,128,256]{2,1,0:T(8,128)(2,1)S(1)}, bf16[4,128,256]{2,1,0:T(8,128)(2,1)S(1)}, u32[]{:S(2)}, u32[]{:S(2)}) collective-permute-start(bf16[4,128,256]{2,1,0:T(8,128)(2,1)S(1)} %get-tuple-element.40), channel_id=1, source_target_pairs={{0,1},{1,0},{2,3},{3,2},{4,5},{5,4},{6,7},{7,6},{8,9},{9,8},{10,11... | collective-permute-start | bytes 786440 | tf_op jit(solution)/shard_map/ppermute | solution.py:30
  25.3 7.0 %collective-permute-start.12 = (bf16[128,256]{1,0:T(8,128)(2,1)S(1)}, bf16[128,256]{1,0:T(8,128)(2,1)S(1)}, u32[]{:S(2)}, u32[]{:S(2)}) collective-permute-start(bf16[128,256]{1,0:T(8,128)(2,1)S(1)} %get-tuple-element.42), channel_id=1, source_target_pairs={{0,6},{1,7},{2,4},{3,5},{4,2},{5,3},{6,0},{7,1},{8,14},{9,15},{10,... | collective-permute-start | bytes 196616 | tf_op jit(solution)/shard_map/ppermute | solution.py:30
  27.6 6.9 %collective-permute-start.13 = (bf16[128,256]{1,0:T(8,128)(2,1)S(1)}, bf16[128,256]{1,0:T(8,128)(2,1)S(1)}, u32[]{:S(2)}, u32[]{:S(2)}) collective-permute-start(bf16[128,256]{1,0:T(8,128)(2,1)S(1)} %get-tuple-element.43), channel_id=1, source_target_pairs={{0,4},{1,5},{2,6},{3,7},{4,0},{5,1},{6,2},{7,3},{8,12},{9,13},{10,... | collective-permute-start | bytes 196616 | tf_op jit(solution)/shard_map/ppermute | solution.py:30
  27.6 6.9 %collective-permute-start.14 = (bf16[128,256]{1,0:T(8,128)(2,1)S(1)}, bf16[128,256]{1,0:T(8,128)(2,1)S(1)}, u32[]{:S(2)}, u32[]{:S(2)}) collective-permute-start(bf16[128,256]{1,0:T(8,128)(2,1)S(1)} %get-tuple-element.44), channel_id=1, source_target_pairs={{0,2},{1,3},{2,0},{3,1},{4,6},{5,7},{6,4},{7,5},{8,10},{9,11},{10,... | collective-permute-start | bytes 196616 | tf_op jit(solution)/shard_map/ppermute | solution.py:30
  29.9 7.9 %collective-permute-start.10 = (bf16[272,128]{1,0:T(8,128)(2,1)S(1)}, bf16[272,128]{1,0:T(8,128)(2,1)S(1)}, u32[]{:S(2)}, u32[]{:S(2)}) collective-permute-start(bf16[272,128]{1,0:T(8,128)(2,1)S(1)} %get-tuple-element.38), channel_id=1, source_target_pairs={{0,2},{1,3},{2,0},{3,1},{4,6},{5,7},{6,4},{7,5},{8,10},{9,11},{10,... | collective-permute-start | bytes 208904 | tf_op jit(solution)/shard_map/ppermute | solution.py:30
  30.0 8.2 %collective-permute-start.8 = (bf16[272,128]{1,0:T(8,128)(2,1)S(1)}, bf16[272,128]{1,0:T(8,128)(2,1)S(1)}, u32[]{:S(2)}, u32[]{:S(2)}) collective-permute-start(bf16[272,128]{1,0:T(8,128)(2,1)S(1)} %get-tuple-element.36), channel_id=1, source_target_pairs={{0,6},{1,7},{2,4},{3,5},{4,2},{5,3},{6,0},{7,1},{8,14},{9,15},{10,... | collective-permute-start | bytes 208904 | tf_op jit(solution)/shard_map/ppermute | solution.py:30
  32.3 11.5 %collective-permute-start.9 = (bf16[272,128]{1,0:T(8,128)(2,1)S(1)}, bf16[272,128]{1,0:T(8,128)(2,1)S(1)}, u32[]{:S(2)}, u32[]{:S(2)}) collective-permute-start(bf16[272,128]{1,0:T(8,128)(2,1)S(1)} %get-tuple-element.37), channel_id=1, source_target_pairs={{0,4},{1,5},{2,6},{3,7},{4,0},{5,1},{6,2},{7,3},{8,12},{9,13},{10,... | collective-permute-start | bytes 208904 | tf_op jit(solution)/shard_map/ppermute | solution.py:30
  34.6 10.6 %collective-permute-start.34 = (bf16[128,256]{1,0:T(8,128)(2,1)S(1)}, bf16[128,256]{1,0:T(8,128)(2,1)S(1)}, u32[]{:S(2)}, u32[]{:S(2)}) collective-permute-start(bf16[128,256]{1,0:T(8,128)(2,1)S(1)} %shard_map.105.refs_4_), channel_id=1, source_target_pairs={{0,4},{1,5},{2,6},{3,7},{4,0},{5,1},{6,2},{7,3},{8,12},{9,13},{10,... | collective-permute-start | bytes 196616 | tf_op jit(solution)/shard_map/ppermute | solution.py:30
  35.6 9.6 %collective-permute-start.36 = (bf16[128,256]{1,0:T(8,128)(2,1)S(1)}, bf16[128,256]{1,0:T(8,128)(2,1)S(1)}, u32[]{:S(2)}, u32[]{:S(2)}) collective-permute-start(bf16[128,256]{1,0:T(8,128)(2,1)S(1)} %shard_map.105.refs_4_), channel_id=1, source_target_pairs={{0,6},{1,7},{2,4},{3,5},{4,2},{5,3},{6,0},{7,1},{8,14},{9,15},{10,... | collective-permute-start | bytes 196616 | tf_op jit(solution)/shard_map/ppermute | solution.py:30
  37.7 9.5 %collective-permute-start.32 = (bf16[128,256]{1,0:T(8,128)(2,1)S(1)}, bf16[128,256]{1,0:T(8,128)(2,1)S(1)}, u32[]{:S(2)}, u32[]{:S(2)}) collective-permute-start(bf16[128,256]{1,0:T(8,128)(2,1)S(1)} %shard_map.105.refs_4_), channel_id=1, source_target_pairs={{0,2},{1,3},{2,0},{3,1},{4,6},{5,7},{6,4},{7,5},{8,10},{9,11},{10,... | collective-permute-start | bytes 196616 | tf_op jit(solution)/shard_map/ppermute | solution.py:30
  45.2 6.9 %collective-permute-start.20 = (bf16[144,256]{1,0:T(8,128)(2,1)S(1)}, bf16[144,256]{1,0:T(8,128)(2,1)S(1)}, u32[]{:S(2)}, u32[]{:S(2)}) collective-permute-start(bf16[144,256]{1,0:T(8,128)(2,1)S(1)} %shard_map.106.refs_0_.refs_8_), channel_id=1, source_target_pairs={{0,6},{1,7},{2,4},{3,5},{4,2},{5,3},{6,0},{7,1},{8,14},{9,15},{10,... | collective-permute-start | bytes 221192 | tf_op jit(solution)/shard_map/ppermute | solution.py:30
  47.3 6.0 %collective-permute-start.16 = (bf16[144,256]{1,0:T(8,128)(2,1)S(1)}, bf16[144,256]{1,0:T(8,128)(2,1)S(1)}, u32[]{:S(2)}, u32[]{:S(2)}) collective-permute-start(bf16[144,256]{1,0:T(8,128)(2,1)S(1)} %shard_map.106.refs_0_.refs_8_), channel_id=1, source_target_pairs={{0,2},{1,3},{2,0},{3,1},{4,6},{5,7},{6,4},{7,5},{8,10},{9,11},{10,... | collective-permute-start | bytes 221192 | tf_op jit(solution)/shard_map/ppermute | solution.py:30
  49.3 7.0 %collective-permute-start.19 = (bf16[144,256]{1,0:T(8,128)(2,1)S(1)}, bf16[144,256]{1,0:T(8,128)(2,1)S(1)}, u32[]{:S(2)}, u32[]{:S(2)}) collective-permute-start(bf16[144,256]{1,0:T(8,128)(2,1)S(1)} %collective-permute-done.18.refs_4_.refs_2_.refs_8_), channel_id=1, source_target_pairs={{0,1},{1,0},{2,3},{3,2},{4,5},{5,4},{6,7},{7,6},{8,9},{9,8},{10,11... | collective-permute-start | bytes 221192 | tf_op jit(solution)/shard_map/ppermute | solution.py:30
  53.2 7.9 %collective-permute-start.15 = (bf16[144,256]{1,0:T(8,128)(2,1)S(1)}, bf16[144,256]{1,0:T(8,128)(2,1)S(1)}, u32[]{:S(2)}, u32[]{:S(2)}) collective-permute-start(bf16[144,256]{1,0:T(8,128)(2,1)S(1)} %shard_map.106.refs_0_.refs_8_), channel_id=1, source_target_pairs={{0,1},{1,0},{2,3},{3,2},{4,5},{5,4},{6,7},{7,6},{8,9},{9,8},{10,11... | collective-permute-start | bytes 221192 | tf_op jit(solution)/shard_map/ppermute | solution.py:30
  53.3 16.2 %collective-permute-start.25 = (bf16[4,128,256]{2,1,0:T(8,128)(2,1)S(1)}, bf16[4,128,256]{2,1,0:T(8,128)(2,1)S(1)}, u32[]{:S(2)}, u32[]{:S(2)}) collective-permute-start(bf16[4,128,256]{2,1,0:T(8,128)(2,1)S(1)} %shard_map.108.refs_4_), channel_id=1, source_target_pairs={{0,8},{8,0},{16,24},{24,16},{1,9},{9,1},{17,25},{25,17},{2,10},{10... | collective-permute-start | bytes 786440 | tf_op jit(solution)/shard_map/ppermute | solution.py:30
  54.8 14.7 %collective-permute-start.26 = (bf16[4,128,256]{2,1,0:T(8,128)(2,1)S(1)}, bf16[4,128,256]{2,1,0:T(8,128)(2,1)S(1)}, u32[]{:S(2)}, u32[]{:S(2)}) collective-permute-start(bf16[4,128,256]{2,1,0:T(8,128)(2,1)S(1)} %shard_map.108.refs_4_), channel_id=1, source_target_pairs={{0,16},{8,24},{16,0},{24,8},{1,17},{9,25},{17,1},{25,9},{2,18},{10... | collective-permute-start | bytes 786440 | tf_op jit(solution)/shard_map/ppermute | solution.py:30
  56.3 13.7 %collective-permute-start.27 = (bf16[4,128,256]{2,1,0:T(8,128)(2,1)S(1)}, bf16[4,128,256]{2,1,0:T(8,128)(2,1)S(1)}, u32[]{:S(2)}, u32[]{:S(2)}) collective-permute-start(bf16[4,128,256]{2,1,0:T(8,128)(2,1)S(1)} %shard_map.108.refs_4_), channel_id=1, source_target_pairs={{0,24},{8,16},{16,8},{24,0},{1,25},{9,17},{17,9},{25,1},{2,26},{10... | collective-permute-start | bytes 786440 | tf_op jit(solution)/shard_map/ppermute | solution.py:30
  66.1 5.9 %collective-permute-start.22 = (bf16[128,512]{1,0:T(8,128)(2,1)S(1)}, bf16[128,512]{1,0:T(8,128)(2,1)S(1)}, u32[]{:S(2)}, u32[]{:S(2)}) collective-permute-start(bf16[128,512]{1,0:T(8,128)(2,1)S(1)} %bitcast.10), channel_id=1, source_target_pairs={{0,8},{8,0},{16,24},{24,16},{1,9},{9,1},{17,25},{25,17},{2,10},{10... | collective-permute-start | bytes 393224 | tf_op jit(solution)/shard_map/ppermute | solution.py:30
  67.7 6.1 %collective-permute-start.40 = (bf16[256,128]{1,0:T(8,128)(2,1)S(1)}, bf16[256,128]{1,0:T(8,128)(2,1)S(1)}, u32[]{:S(2)}, u32[]{:S(2)}) collective-permute-start(bf16[256,128]{1,0:T(8,128)(2,1)S(1)} %get-tuple-element.52), channel_id=1, source_target_pairs={{0,6},{1,7},{2,4},{3,5},{4,2},{5,3},{6,0},{7,1},{8,14},{9,15},{10,... | collective-permute-start | bytes 196616 | tf_op jit(solution)/shard_map/ppermute | solution.py:30
  69.5 15.6 %collective-permute-start.28 = (bf16[4,128,256]{2,1,0:T(8,128)(2,1)S(1)}, bf16[4,128,256]{2,1,0:T(8,128)(2,1)S(1)}, u32[]{:S(2)}, u32[]{:S(2)}) collective-permute-start(bf16[4,128,256]{2,1,0:T(8,128)(2,1)S(1)} %collective-permute-done.25.refs_5_), channel_id=1, source_target_pairs={{0,1},{1,0},{2,3},{3,2},{4,5},{5,4},{6,7},{7,6},{8,9},{9,8},{10,11... | collective-permute-start | bytes 786440 | tf_op jit(solution)/shard_map/ppermute | solution.py:30
  69.5 15.6 %collective-permute-start.29 = (bf16[4,128,256]{2,1,0:T(8,128)(2,1)S(1)}, bf16[4,128,256]{2,1,0:T(8,128)(2,1)S(1)}, u32[]{:S(2)}, u32[]{:S(2)}) collective-permute-start(bf16[4,128,256]{2,1,0:T(8,128)(2,1)S(1)} %collective-permute-done.26.refs_6_), channel_id=1, source_target_pairs={{0,1},{1,0},{2,3},{3,2},{4,5},{5,4},{6,7},{7,6},{8,9},{9,8},{10,11... | collective-permute-start | bytes 786440 | tf_op jit(solution)/shard_map/ppermute | solution.py:30
  70.0 15.1 %collective-permute-start.30 = (bf16[4,128,256]{2,1,0:T(8,128)(2,1)S(1)}, bf16[4,128,256]{2,1,0:T(8,128)(2,1)S(1)}, u32[]{:S(2)}, u32[]{:S(2)}) collective-permute-start(bf16[4,128,256]{2,1,0:T(8,128)(2,1)S(1)} %collective-permute-done.27.refs_7_), channel_id=1, source_target_pairs={{0,1},{1,0},{2,3},{3,2},{4,5},{5,4},{6,7},{7,6},{8,9},{9,8},{10,11... | collective-permute-start | bytes 786440 | tf_op jit(solution)/shard_map/ppermute | solution.py:30
  72.0 5.8 %collective-permute-start.41 = (bf16[256,128]{1,0:T(8,128)(2,1)S(1)}, bf16[256,128]{1,0:T(8,128)(2,1)S(1)}, u32[]{:S(2)}, u32[]{:S(2)}) collective-permute-start(bf16[256,128]{1,0:T(8,128)(2,1)S(1)} %get-tuple-element.53), channel_id=1, source_target_pairs={{0,4},{1,5},{2,6},{3,7},{4,0},{5,1},{6,2},{7,3},{8,12},{9,13},{10,... | collective-permute-start | bytes 196616 | tf_op jit(solution)/shard_map/ppermute | solution.py:30
  73.8 5.4 %collective-permute-start.42 = (bf16[256,128]{1,0:T(8,128)(2,1)S(1)}, bf16[256,128]{1,0:T(8,128)(2,1)S(1)}, u32[]{:S(2)}, u32[]{:S(2)}) collective-permute-start(bf16[256,128]{1,0:T(8,128)(2,1)S(1)} %get-tuple-element.54), channel_id=1, source_target_pairs={{0,2},{1,3},{2,0},{3,1},{4,6},{5,7},{6,4},{7,5},{8,10},{9,11},{10,... | collective-permute-start | bytes 196616 | tf_op jit(solution)/shard_map/ppermute | solution.py:30
  77.7 6.2 %collective-permute-start.23 = (bf16[128,512]{1,0:T(8,128)(2,1)S(1)}, bf16[128,512]{1,0:T(8,128)(2,1)S(1)}, u32[]{:S(2)}, u32[]{:S(2)}) collective-permute-start(bf16[128,512]{1,0:T(8,128)(2,1)S(1)} %bitcast.11), channel_id=1, source_target_pairs={{0,16},{8,24},{16,0},{24,8},{1,17},{9,25},{17,1},{25,9},{2,18},{10... | collective-permute-start | bytes 393224 | tf_op jit(solution)/shard_map/ppermute | solution.py:30
  79.3 5.9 %collective-permute-start.24 = (bf16[128,512]{1,0:T(8,128)(2,1)S(1)}, bf16[128,512]{1,0:T(8,128)(2,1)S(1)}, u32[]{:S(2)}, u32[]{:S(2)}) collective-permute-start(bf16[128,512]{1,0:T(8,128)(2,1)S(1)} %bitcast.12), channel_id=1, source_target_pairs={{0,24},{8,16},{16,8},{24,0},{1,25},{9,17},{17,9},{25,1},{2,26},{10... | collective-permute-start | bytes 393224 | tf_op jit(solution)/shard_map/ppermute | solution.py:30
  (15 other events, 77.4 us)

commit v3 on v2

--- a/solution.py
+++ b/solution.py
@@ -95,36 +95,53 @@
 
 def forward_kernel(size, passages, lengths_ref, *refs):
     q_refs = refs[:size]
-    keys_ref, values_ref, even_ref, odd_ref, q_buf, bias_ref = refs[size:]
+    keys_ref, values_ref, even_ref, odd_ref, weights_ref, tops_ref, q_buf, s_buf, bias_ref = refs[size:]
     width = q_buf.shape[2]
+    pairs = width // PAIR
     for s in range(size):
         q_buf[s] = q_refs[s][...]
     bias_ref[...] = mask_bias(lengths_ref, passages, keys_ref.shape[1] // passages)
     lane_low = lax.broadcasted_iota(jnp.int32, (1, PAIR), 1) < HEAD_SIZE
 
-    def one_slot(s, out_ref, k):
-        rows = []
-        for p in range(width // PAIR):
-            lanes = slice(p * PAIR, (p + 1) * PAIR)
-            queries = block_stack(q_buf[s, :, lanes], lane_low)
-            bias = bias_ref[...]
-            scores = dot(keys_ref[s, :, lanes], queries, NT) + jnp.concatenate([bias, bias], axis=1)
-            top = jnp.max(scores, axis=0, keepdims=True)
-            weights = jnp.exp(scores - top)
-            total = jnp.sum(weights, axis=0, keepdims=True)
-            mixed = dot(values_ref[s, :, lanes], weights.astype(jnp.bfloat16), TN) / total
-            out_ref[k, lanes, :] = diagonal(mixed).astype(jnp.bfloat16)
-            lse = top + jnp.log(total)
-            n = lse.shape[1] // 2
-            rows += [lse[:, :n], lse[:, n:]]
-        out_ref[k, width:, :] = thirds(jnp.concatenate(rows, axis=0))
-
-    def body(k, carry):
-        one_slot(2 * k, even_ref, k)
-        one_slot(2 * k + 1, odd_ref, k)
-        return carry
-
-    lax.fori_loop(0, size // 2, body, 0)
+    def score(s, p):
+        lanes = slice(p * PAIR, (p + 1) * PAIR)
+        queries = block_stack(q_buf[s, :, lanes], lane_low)
+        bias = bias_ref[...]
+        scores = dot(keys_ref[s, :, lanes], queries, NT) + jnp.concatenate([bias, bias], axis=1)
+        s_buf[p] = scores
+        return jnp.max(scores, axis=0, keepdims=True)
+
+    def mix(s, p, top, out_ref, k):
+        lanes = slice(p * PAIR, (p + 1) * PAIR)
+        weights = jnp.exp(s_buf[p] - top)
+        total = jnp.sum(weights, axis=0, keepdims=True)
+        rounded = weights.astype(jnp.bfloat16)
+        weights_ref[s * pairs + p] = rounded
+        mixed = dot(values_ref[s, :, lanes], rounded, TN) / total
+        out_ref[k, lanes, :] = diagonal(mixed).astype(jnp.bfloat16)
+        return top + jnp.log(total)
+
+    def one_slot(s, out_ref, k, first_top):
+        tops, lses = [first_top], []
+        for p in range(pairs):
+            if p + 1 < pairs:
+                tops.append(score(s, p + 1))
+            else:
+                following = score(jnp.minimum(s + 1, size - 1), 0) if pairs > 1 else None
+            lses.append(mix(s, p, tops[p], out_ref, k))
+        if following is None:
+            following = score(jnp.minimum(s + 1, size - 1), 0)
+        n = first_top.shape[1] // 2
+        tops_ref[s] = jnp.concatenate([x[:, h * n : (h + 1) * n] for x in tops for h in range(2)], axis=0)
+        rows = jnp.concatenate([x[:, h * n : (h + 1) * n] for x in lses for h in range(2)], axis=0)
+        out_ref[k, width:, :] = thirds(rows)
+        return following
+
+    def body(k, top):
+        top = one_slot(2 * k, even_ref, k, top)
+        return one_slot(2 * k + 1, odd_ref, k, top)
+
+    lax.fori_loop(0, size // 2, body, score(0, 0))
 
 
 def merge(blocks):
@@ -172,16 +189,16 @@
     return rows[:n, :answers] + rows[:n, answers:] + rows[n:, :answers]
 
 
-def backward_kernel(slots, carried, passages, me_ref, lengths_ref, *refs):
+def backward_kernel(slots, carried, me_ref, *refs):
     count = len(slots)
     q_refs, g_refs, c_refs = refs[:count], refs[count : 2 * count], refs[2 * count : 3 * count]
-    keys_ref, values_ref = refs[3 * count : 3 * count + 2]
-    dk_ref, dv_ref, even_ref, odd_ref, q_buf, g_buf, st_buf, dk_buf, dv_buf, bias_ref, sem = refs[
-        3 * count + 2 + carried :
-    ]
+    keys_ref, values_ref, weights_ref, tops_ref = refs[3 * count : 3 * count + 4]
+    dk_ref, dv_ref, even_ref, odd_ref, q_buf, g_buf, st_buf, p_buf, dk_buf, dv_buf, sem = refs[3 * count + 4 + carried :]
     me = me_ref[0]
     answers, width = q_buf.shape[1:]
+    pairs = width // PAIR
     first = slots[0]
+    heads = width // HEAD_SIZE
 
     def dk_copy(i):
         return pltpu.make_async_copy(dk_buf.at[i], columns_of(dk_ref, me, first + i, width), sem.at[0, i])
@@ -189,33 +206,42 @@
     def dv_copy(i):
         return pltpu.make_async_copy(dv_buf.at[i], columns_of(dv_ref, me, first + i, width), sem.at[1, i])
 
+    lane_low = lax.broadcasted_iota(jnp.int32, (1, PAIR), 1) < HEAD_SIZE
     for i in range(count):
+        stats = stats_of(c_refs[i], answers)
+        share = jnp.exp(tops_ref[first + i] - stats[:heads])
+        st_buf[i] = jnp.concatenate([share, stats[heads:]], axis=0)
         q_buf[i] = q_refs[i][...]
         g_buf[i] = g_refs[i][...]
-        st_buf[i] = stats_of(c_refs[i], answers)
-    bias_ref[...] = mask_bias(lengths_ref, passages, keys_ref.shape[1] // passages)
-    lane_low = lax.broadcasted_iota(jnp.int32, (1, PAIR), 1) < HEAD_SIZE
-    heads = width // HEAD_SIZE
+
+    def grads_of(i, p):
+        return block_stack(g_buf[i, :, p * PAIR : (p + 1) * PAIR], lane_low)
+
+    def prob_grad(i, p):
+        p_buf[p] = dot(values_ref[first + i, :, p * PAIR : (p + 1) * PAIR], grads_of(i, p), NT)
+
+    def row_pair(rows, at):
+        return jnp.concatenate([rows[at : at + 1], rows[at + 1 : at + 2]], axis=1)
+
+    def rest(i, p, out_ref, k):
+        lanes = slice(p * PAIR, (p + 1) * PAIR)
+        queries = block_stack(q_buf[i, :, lanes], lane_low)
+        stats = st_buf[i]
+        probs = weights_ref[(first + i) * pairs + p].astype(jnp.float32) * row_pair(stats, 2 * p)
+        score_grad = (probs * (p_buf[p] - row_pair(stats, heads + 2 * p))).astype(jnp.bfloat16)
+        dv_buf[i, :, lanes] = dot(probs.astype(jnp.bfloat16), grads_of(i, p), NN).astype(jnp.bfloat16)
+        dk_buf[i, :, lanes] = dot(score_grad, queries, NN).astype(jnp.bfloat16)
+        out_ref[k, lanes, :] = diagonal(dot(keys_ref[first + i, :, lanes], score_grad, TN)).astype(jnp.bfloat16)
 
     def one_slot(i, out_ref, k):
-        for p in range(width // PAIR):
-            lanes = slice(p * PAIR, (p + 1) * PAIR)
-            queries = block_stack(q_buf[i, :, lanes], lane_low)
-            grads = block_stack(g_buf[i, :, lanes], lane_low)
-            stats = st_buf[i]
-            lse = jnp.concatenate([stats[2 * p : 2 * p + 1], stats[2 * p + 1 : 2 * p + 2]], axis=1)
-            dots = jnp.concatenate(
-                [stats[heads + 2 * p : heads + 2 * p + 1], stats[heads + 2 * p + 1 : heads + 2 * p + 2]], axis=1
-            )
-            key_block = keys_ref[first + i, :, lanes]
-            bias = bias_ref[...]
-            scores = dot(key_block, queries, NT) + jnp.concatenate([bias, bias], axis=1)
-            probs = jnp.exp(scores - lse)
-            prob_grad = dot(values_ref[first + i, :, lanes], grads, NT)
-            score_grad = (probs * (prob_grad - dots)).astype(jnp.bfloat16)
-            dv_buf[i, :, lanes] = dot(probs.astype(jnp.bfloat16), grads, NN).astype(jnp.bfloat16)
-            dk_buf[i, :, lanes] = dot(score_grad, queries, NN).astype(jnp.bfloat16)
-            out_ref[k, lanes, :] = diagonal(dot(key_block, score_grad, TN)).astype(jnp.bfloat16)
+        for p in range(pairs):
+            if p + 1 < pairs:
+                prob_grad(i, p + 1)
+                rest(i, p, out_ref, k)
+            else:
+                rest(i, p, out_ref, k) if pairs == 1 else None
+                prob_grad(jnp.minimum(i + 1, count - 1), 0)
+                rest(i, p, out_ref, k) if pairs > 1 else None
         dk_copy(i).start()
         dv_copy(i).start()
 
@@ -224,6 +250,7 @@
         one_slot(2 * k + 1, odd_ref, k)
         return carry
 
+    prob_grad(0, 0)
     lax.fori_loop(0, count // 2, body, 0)
     for i in range(count):
         dk_copy(i).wait()
@@ -276,20 +303,12 @@
 
 
 def layer_out_kernel(size, me_ref, *refs):
-    weight_ref, out_ref, w_buf, sem = refs[size:]
+    weight_ref, out_ref = refs[size:]
     me = me_ref[0]
-    width = w_buf.shape[2]
-    answers = out_ref.shape[0]
-
-    def w_copy(s):
-        return pltpu.make_async_copy(columns_of(weight_ref, me, s, width), w_buf.at[s], sem.at[s])
-
-    for s in range(size):
-        w_copy(s).start()
+    answers, width = out_ref.shape[0], refs[0].shape[1]
     total = None
     for s in range(size):
-        w_copy(s).wait()
-        part = dot(refs[s][:answers, :], w_buf[s], NT)
+        part = dot(refs[s][:answers, :], columns_of(weight_ref, me, s, width)[...], NT)
         total = part if total is None else total + part
     out_ref[...] = total.astype(jnp.bfloat16)
 
@@ -374,16 +393,22 @@
     g_parts = [swap(g_sums[d // 2], "psg", size, d) for d in far_first(size)]
 
     packed = shaped((width + EXTRA, answers), bf16)
-    o_even, o_odd = call(
+    pairs = width // PAIR
+    o_even, o_odd, weights, tops = call(
         functools.partial(forward_kernel, size, passages),
         lengths,
         *slots,
         slot_keys,
         slot_values,
-        out=[shaped((half, width + EXTRA, answers), bf16)] * 2,
+        out=[shaped((half, width + EXTRA, answers), bf16)] * 2
+        + [shaped((size * pairs, key_count, 2 * answers), bf16), shaped((size, heads, answers), f32)],
         ins=[SMEM] + [VMEM] * (size + 2),
-        outs=[VMEM] * 2,
-        scratch=[pltpu.VMEM((size, answers, width), bf16), pltpu.VMEM((key_count, PAIR), f32)],
+        outs=[VMEM] * 4,
+        scratch=[
+            pltpu.VMEM((size, answers, width), bf16),
+            pltpu.VMEM((pairs, key_count, 2 * answers), f32),
+            pltpu.VMEM((key_count, PAIR), f32),
+        ],
         vmem=16,
     )
 
@@ -409,27 +434,29 @@
     def backward(chosen, carried):
         count = len(chosen)
         pick = slice(chosen[0], chosen[0] + count)
-        fixed = 2 + 3 * count + 2
+        fixed = 1 + 3 * count + 4
         return call(
-            functools.partial(backward_kernel, chosen, len(carried), passages),
+            functools.partial(backward_kernel, chosen, len(carried)),
             me,
-            lengths,
             *slots[pick],
             *g_slots[pick],
             *c_slots[pick],
             slot_keys,
             slot_values,
+            weights,
+            tops,
             *carried,
             out=[shaped((key_count, inner), bf16)] * 2 + [shaped((count // 2, width, answers), bf16)] * 2,
-            ins=[SMEM, SMEM] + [VMEM] * (3 * count + 2) + [ANY] * len(carried),
+            ins=[SMEM] + [VMEM] * (3 * count + 4) + [ANY] * len(carried),
             outs=[ANY, ANY, VMEM, VMEM],
             scratch=[
                 pltpu.VMEM((count, answers, width), bf16),
                 pltpu.VMEM((count, answers, width), bf16),
                 pltpu.VMEM((count, 2 * heads, answers), f32),
             ]
+            + [pltpu.VMEM((pairs, key_count, 2 * answers), f32)]
             + [pltpu.VMEM((count, key_count, width), bf16)] * 2
-            + [pltpu.VMEM((key_count, PAIR), f32), pltpu.SemaphoreType.DMA((2, count))],
+            + [pltpu.SemaphoreType.DMA((2, count))],
             vmem=16,
             alias={fixed + i: i for i in range(len(carried))},
         )
@@ -463,9 +490,8 @@
         *c_slots,
         out_weight,
         out=shaped((answers, model), bf16),
-        ins=[SMEM] + [VMEM] * size + [ANY],
+        ins=[SMEM] + [VMEM] * (size + 1),
         outs=VMEM,
-        scratch=[pltpu.VMEM((size, model, width), bf16), pltpu.SemaphoreType.DMA((size,))],
     )
     weight_grad = call(
         functools.partial(weight_grad_kernel, size, dp, answers),

time: 87.9 us -> 83.4 us (0.949)
  Pallas kernels: 25.4 us -> 20.3 us
    pallas_call x14, Pallas kernels: 25.4 us -> 20.3 us  [call(): pl.pallas_call(kernel, out_shape=out, in_specs=ins, out_specs=outs, scrat...]
  transfers between devices with their start and end apart: 43 -> 43, of which waited for: 13 -> 14; matrix products, arithmetic and copies ran while one was open for 0% -> 0% of each run, Pallas kernels for 26% -> 21%
where the time goes in v3:
time: 83.4 us; the launch traced here: 83.3 us
  starting transfers between devices  35.8 us (43%)
  waiting for transfers between devices  25.5 us (31%)
  Pallas kernels  20.3 us (24%)
  local copies, waits for them, and re-layouts  0.92 us (1%)
    ppermute x43, starting transfers between devices, swap(): return lax.ppermute(x, axis, [(j, j ^ distance) for j in range(size)])  35.8 us
    ppermute x43, waiting for transfers between devices, swap(): return lax.ppermute(x, axis, [(j, j ^ distance) for j in range(size)])  25.5 us
    pallas_call x14, Pallas kernels, call(): pl.pallas_call(kernel, out_shape=out, in_specs=ins, out_specs=outs, scrat...  20.3 us
  transfers between devices with their start and end apart: 43, of which 14 were waited for; matrix products, arithmetic and copies ran while one was open for 0% of the time, Pallas kernels for 21%

profile of v3, /device:TPU:0, one launch (start us, length us, event | category | flops | bytes accessed | tf_op | source)
XLA Modules:
  0.0 83.3 jit_solution(15993030639975229563)
XLA Ops:
  0.6 3.1 %collective-permute-start.1 = (bf16[128,256]{1,0:T(8,128)(2,1)}, bf16[128,256]{1,0:T(8,128)(2,1)S(1)}, u32[]{:S(2)}, u32[]{:S(2)}) collective-permute-start(bf16[128,256]{1,0:T(8,128)(2,1)} %bitcast.14), channel_id=1, source_target_pairs={{0,2},{1,3},{2,0},{3,1},{4,6},{5,7},{6,4},{7,5},{8,10},{9,11},{10,... | collective-permute-start | bytes 196616 | tf_op jit(solution)/shard_map/ppermute | solution.py:30
  3.8 2.6 %collective-permute-start.3 = (bf16[128,256]{1,0:T(8,128)(2,1)}, bf16[128,256]{1,0:T(8,128)(2,1)S(1)}, u32[]{:S(2)}, u32[]{:S(2)}) collective-permute-start(bf16[128,256]{1,0:T(8,128)(2,1)} %bitcast.15), channel_id=1, source_target_pairs={{0,4},{1,5},{2,6},{3,7},{4,0},{5,1},{6,2},{7,3},{8,12},{9,13},{10,... | collective-permute-start | bytes 196616 | tf_op jit(solution)/shard_map/ppermute | solution.py:30
  6.9 4.4 %collective-permute-done.3.refs_4_.refs_0_ = bf16[128,256]{1,0:T(8,128)(2,1)S(1)} collective-permute-done((bf16[128,256]{1,0:T(8,128)(2,1)}, bf16[128,256]{1,0:T(8,128)(2,1)S(1)}, u32[]{:S(2)}, u32[]{:S(2)}) %collective-permute-start.3) | collective-permute-done | bytes 65568 | tf_op jit(solution)/shard_map/ppermute | solution.py:30
  11.2 1.4 %collective-permute-done.5.refs_6_.refs_2_ = bf16[128,256]{1,0:T(8,128)(2,1)S(1)} collective-permute-done((bf16[128,256]{1,0:T(8,128)(2,1)}, bf16[128,256]{1,0:T(8,128)(2,1)S(1)}, u32[]{:S(2)}, u32[]{:S(2)}) %collective-permute-start.5) | collective-permute-done | bytes 65568 | tf_op jit(solution)/shard_map/ppermute | solution.py:30
  13.6 3.2 %shard_map.101 = (bf16[4,128,256]{2,1,0:T(8,128)(2,1)S(1)}, bf16[4,128,256]{2,1,0:T(8,128)(2,1)S(1)}, bf16[8,512,256]{2,1,0:T(8,128)(2,1)S(1)}, bf16[8,512,256]{2,1,0:T(8,128)(2,1)S(1)}) custom-call(s32[1]{0:T(128)} %bitcast.me_ref, bf16[128,512]{1,0:T(8,128)(2,1)S(1)} %bitcast.9, bf16[512,2048]{1,0:T(8,128)(2,1)} %refs_8_.1, bf16[512,2048]{1,0:T(8,128)(2,1)} %bitcast.20, ...), custom_call_target="tpu_custom_call" | custom-call | tf_op jit(solution)/shard_map/pallas_call | solution.py:34
  17.4 4.7 %shard_map.102 = (bf16[4,272,128]{2,1,0:T(8,128)(2,1)S(1)}, bf16[4,272,128]{2,1,0:T(8,128)(2,1)S(1)}, bf16[16,512,256]{2,1,0:T(8,128)(2,1)S(1)}, f32[8,4,128]{2,1,0:T(4,128)S(1)}) custom-call(s32[1,2]{1,0:T(1,128)S(1)} %copy-done.3, bf16[128,256]{1,0:T(8,128)(2,1)S(1)} %bitcast.18, bf16[128,256]{1,0:T(8,128)(2,1)S(1)} %collective-permute-done.refs_1_, ...), custom_call_target="tpu_custom_call" | custom-call | tf_op jit(solution)/shard_map/pallas_call | solution.py:34
  22.3 2.3 %collective-permute-start.12 = (bf16[128,256]{1,0:T(8,128)(2,1)S(1)}, bf16[128,256]{1,0:T(8,128)(2,1)S(1)}, u32[]{:S(2)}, u32[]{:S(2)}) collective-permute-start(bf16[128,256]{1,0:T(8,128)(2,1)S(1)} %get-tuple-element.44), channel_id=1, source_target_pairs={{0,6},{1,7},{2,4},{3,5},{4,2},{5,3},{6,0},{7,1},{8,14},{9,15},{10,... | collective-permute-start | bytes 196616 | tf_op jit(solution)/shard_map/ppermute | solution.py:30
  24.6 2.2 %collective-permute-start.14 = (bf16[128,256]{1,0:T(8,128)(2,1)S(1)}, bf16[128,256]{1,0:T(8,128)(2,1)S(1)}, u32[]{:S(2)}, u32[]{:S(2)}) collective-permute-start(bf16[128,256]{1,0:T(8,128)(2,1)S(1)} %get-tuple-element.46), channel_id=1, source_target_pairs={{0,2},{1,3},{2,0},{3,1},{4,6},{5,7},{6,4},{7,5},{8,10},{9,11},{10,... | collective-permute-start | bytes 196616 | tf_op jit(solution)/shard_map/ppermute | solution.py:30
  27.0 2.3 %collective-permute-start.8 = (bf16[272,128]{1,0:T(8,128)(2,1)S(1)}, bf16[272,128]{1,0:T(8,128)(2,1)S(1)}, u32[]{:S(2)}, u32[]{:S(2)}) collective-permute-start(bf16[272,128]{1,0:T(8,128)(2,1)S(1)} %get-tuple-element.38), channel_id=1, source_target_pairs={{0,6},{1,7},{2,4},{3,5},{4,2},{5,3},{6,0},{7,1},{8,14},{9,15},{10,... | collective-permute-start | bytes 208904 | tf_op jit(solution)/shard_map/ppermute | solution.py:30
  29.3 1.7 %collective-permute-start.9 = (bf16[272,128]{1,0:T(8,128)(2,1)S(1)}, bf16[272,128]{1,0:T(8,128)(2,1)S(1)}, u32[]{:S(2)}, u32[]{:S(2)}) collective-permute-start(bf16[272,128]{1,0:T(8,128)(2,1)S(1)} %get-tuple-element.39), channel_id=1, source_target_pairs={{0,4},{1,5},{2,6},{3,7},{4,0},{5,1},{6,2},{7,3},{8,12},{9,13},{10,... | collective-permute-start | bytes 208904 | tf_op jit(solution)/shard_map/ppermute | solution.py:30
  31.6 1.0 %collective-permute-start.34 = (bf16[128,256]{1,0:T(8,128)(2,1)S(1)}, bf16[128,256]{1,0:T(8,128)(2,1)S(1)}, u32[]{:S(2)}, u32[]{:S(2)}) collective-permute-start(bf16[128,256]{1,0:T(8,128)(2,1)S(1)} %shard_map.105.refs_4_), channel_id=1, source_target_pairs={{0,4},{1,5},{2,6},{3,7},{4,0},{5,1},{6,2},{7,3},{8,12},{9,13},{10,... | collective-permute-start | bytes 196616 | tf_op jit(solution)/shard_map/ppermute | solution.py:30
  32.6 2.1 %collective-permute-start.36 = (bf16[128,256]{1,0:T(8,128)(2,1)S(1)}, bf16[128,256]{1,0:T(8,128)(2,1)S(1)}, u32[]{:S(2)}, u32[]{:S(2)}) collective-permute-start(bf16[128,256]{1,0:T(8,128)(2,1)S(1)} %shard_map.105.refs_4_), channel_id=1, source_target_pairs={{0,6},{1,7},{2,4},{3,5},{4,2},{5,3},{6,0},{7,1},{8,14},{9,15},{10,... | collective-permute-start | bytes 196616 | tf_op jit(solution)/shard_map/ppermute | solution.py:30
  35.2 5.6 %collective-permute-done.9.refs_2_ = bf16[272,128]{1,0:T(8,128)(2,1)S(1)} collective-permute-done((bf16[272,128]{1,0:T(8,128)(2,1)S(1)}, bf16[272,128]{1,0:T(8,128)(2,1)S(1)}, u32[]{:S(2)}, u32[]{:S(2)}) %collective-permute-start.9) | collective-permute-done | bytes 69664 | tf_op jit(solution)/shard_map/ppermute | solution.py:30
  41.2 1.0 %collective-permute-done.34.refs_4_ = bf16[128,256]{1,0:T(8,128)(2,1)S(1)} collective-permute-done((bf16[128,256]{1,0:T(8,128)(2,1)S(1)}, bf16[128,256]{1,0:T(8,128)(2,1)S(1)}, u32[]{:S(2)}, u32[]{:S(2)}) %collective-permute-start.34) | collective-permute-done | bytes 65568 | tf_op jit(solution)/shard_map/ppermute | solution.py:30
  42.2 2.1 %collective-permute-start.20 = (bf16[144,256]{1,0:T(8,128)(2,1)S(1)}, bf16[144,256]{1,0:T(8,128)(2,1)S(1)}, u32[]{:S(2)}, u32[]{:S(2)}) collective-permute-start(bf16[144,256]{1,0:T(8,128)(2,1)S(1)} %shard_map.106.refs_0_.refs_8_), channel_id=1, source_target_pairs={{0,6},{1,7},{2,4},{3,5},{4,2},{5,3},{6,0},{7,1},{8,14},{9,15},{10,... | collective-permute-start | bytes 221192 | tf_op jit(solution)/shard_map/ppermute | solution.py:30
  44.3 1.5 %collective-permute-start.16 = (bf16[144,256]{1,0:T(8,128)(2,1)S(1)}, bf16[144,256]{1,0:T(8,128)(2,1)S(1)}, u32[]{:S(2)}, u32[]{:S(2)}) collective-permute-start(bf16[144,256]{1,0:T(8,128)(2,1)S(1)} %shard_map.106.refs_0_.refs_8_), channel_id=1, source_target_pairs={{0,2},{1,3},{2,0},{3,1},{4,6},{5,7},{6,4},{7,5},{8,10},{9,11},{10,... | collective-permute-start | bytes 221192 | tf_op jit(solution)/shard_map/ppermute | solution.py:30
  46.9 2.2 %collective-permute-done.20.refs_6_.refs_3_.refs_10_ = bf16[144,256]{1,0:T(8,128)(2,1)S(1)} collective-permute-done((bf16[144,256]{1,0:T(8,128)(2,1)S(1)}, bf16[144,256]{1,0:T(8,128)(2,1)S(1)}, u32[]{:S(2)}, u32[]{:S(2)}) %collective-permute-start.20) | collective-permute-done | bytes 73760 | tf_op jit(solution)/shard_map/ppermute | solution.py:30
  49.1 1.1 %collective-permute-done.16.refs_2_.refs_1_.refs_10_ = bf16[144,256]{1,0:T(8,128)(2,1)S(1)} collective-permute-done((bf16[144,256]{1,0:T(8,128)(2,1)S(1)}, bf16[144,256]{1,0:T(8,128)(2,1)S(1)}, u32[]{:S(2)}, u32[]{:S(2)}) %collective-permute-start.16) | collective-permute-done | bytes 73760 | tf_op jit(solution)/shard_map/ppermute | solution.py:30
  50.3 1.6 %collective-permute-start.25 = (bf16[4,128,256]{2,1,0:T(8,128)(2,1)S(1)}, bf16[4,128,256]{2,1,0:T(8,128)(2,1)S(1)}, u32[]{:S(2)}, u32[]{:S(2)}) collective-permute-start(bf16[4,128,256]{2,1,0:T(8,128)(2,1)S(1)} %shard_map.108.refs_4_), channel_id=1, source_target_pairs={{0,8},{8,0},{16,24},{24,16},{1,9},{9,1},{17,25},{25,17},{2,10},{10... | collective-permute-start | bytes 786440 | tf_op jit(solution)/shard_map/ppermute | solution.py:30
  51.9 1.5 %collective-permute-start.26 = (bf16[4,128,256]{2,1,0:T(8,128)(2,1)S(1)}, bf16[4,128,256]{2,1,0:T(8,128)(2,1)S(1)}, u32[]{:S(2)}, u32[]{:S(2)}) collective-permute-start(bf16[4,128,256]{2,1,0:T(8,128)(2,1)S(1)} %shard_map.108.refs_4_), channel_id=1, source_target_pairs={{0,16},{8,24},{16,0},{24,8},{1,17},{9,25},{17,1},{25,9},{2,18},{10... | collective-permute-start | bytes 786440 | tf_op jit(solution)/shard_map/ppermute | solution.py:30
  53.9 3.5 %shard_map.110 = (bf16[512,2048]{1,0:T(8,128)(2,1)}, bf16[512,2048]{1,0:T(8,128)(2,1)}, bf16[2,256,128]{2,1,0:T(8,128)(2,1)S(1)}, bf16[2,256,128]{2,1,0:T(8,128)(2,1)S(1)}) custom-call(s32[1]{0:T(128)} %bitcast.me_ref, bf16[128,256]{1,0:T(8,128)(2,1)S(1)} %collective-permute-done.3.refs_4_.refs_0_, ...), custom_call_target="tpu_custom_call" | custom-call | tf_op jit(solution)/shard_map/pallas_call | solution.py:34
  58.0 3.5 %shard_map.111 = (bf16[512,2048]{1,0:T(8,128)(2,1)}, bf16[512,2048]{1,0:T(8,128)(2,1)}, bf16[2,256,128]{2,1,0:T(8,128)(2,1)S(1)}, bf16[2,256,128]{2,1,0:T(8,128)(2,1)S(1)}) custom-call(s32[1]{0:T(128)} %bitcast.me_ref, bf16[128,256]{1,0:T(8,128)(2,1)S(1)} %bitcast.19, ...), custom_call_target="tpu_custom_call", output_to_operand_aliasing={{0}: (17, {}), {1}: (18, {})} | custom-call | tf_op jit(solution)/shard_map/pallas_call | solution.py:34
  61.6 1.6 %collective-permute-start.22 = (bf16[128,512]{1,0:T(8,128)(2,1)S(1)}, bf16[128,512]{1,0:T(8,128)(2,1)S(1)}, u32[]{:S(2)}, u32[]{:S(2)}) collective-permute-start(bf16[128,512]{1,0:T(8,128)(2,1)S(1)} %bitcast.10), channel_id=1, source_target_pairs={{0,8},{8,0},{16,24},{24,16},{1,9},{9,1},{17,25},{25,17},{2,10},{10... | collective-permute-start | bytes 393224 | tf_op jit(solution)/shard_map/ppermute | solution.py:30
  63.1 1.8 %collective-permute-start.40 = (bf16[256,128]{1,0:T(8,128)(2,1)S(1)}, bf16[256,128]{1,0:T(8,128)(2,1)S(1)}, u32[]{:S(2)}, u32[]{:S(2)}) collective-permute-start(bf16[256,128]{1,0:T(8,128)(2,1)S(1)} %get-tuple-element.56), channel_id=1, source_target_pairs={{0,6},{1,7},{2,4},{3,5},{4,2},{5,3},{6,0},{7,1},{8,14},{9,15},{10,... | collective-permute-start | bytes 196616 | tf_op jit(solution)/shard_map/ppermute | solution.py:30
  65.0 1.0 %collective-permute-done.26.refs_6_ = bf16[4,128,256]{2,1,0:T(8,128)(2,1)S(1)} collective-permute-done((bf16[4,128,256]{2,1,0:T(8,128)(2,1)S(1)}, bf16[4,128,256]{2,1,0:T(8,128)(2,1)S(1)}, u32[]{:S(2)}, u32[]{:S(2)}) %collective-permute-start.26) | collective-permute-done | bytes 262176 | tf_op jit(solution)/shard_map/ppermute | solution.py:30
  66.5 1.1 %collective-permute-done.22.refs_1_ = bf16[128,512]{1,0:T(8,128)(2,1)S(1)} collective-permute-done((bf16[128,512]{1,0:T(8,128)(2,1)S(1)}, bf16[128,512]{1,0:T(8,128)(2,1)S(1)}, u32[]{:S(2)}, u32[]{:S(2)}) %collective-permute-start.22) | collective-permute-done | bytes 131104 | tf_op jit(solution)/shard_map/ppermute | solution.py:30
  69.9 3.3 %collective-permute-done.41.refs_2_ = bf16[256,128]{1,0:T(8,128)(2,1)S(1)} collective-permute-done((bf16[256,128]{1,0:T(8,128)(2,1)S(1)}, bf16[256,128]{1,0:T(8,128)(2,1)S(1)}, u32[]{:S(2)}, u32[]{:S(2)}) %collective-permute-start.41) | collective-permute-done | bytes 65568 | tf_op jit(solution)/shard_map/ppermute | solution.py:30
  73.2 1.5 %collective-permute-start.23 = (bf16[128,512]{1,0:T(8,128)(2,1)S(1)}, bf16[128,512]{1,0:T(8,128)(2,1)S(1)}, u32[]{:S(2)}, u32[]{:S(2)}) collective-permute-start(bf16[128,512]{1,0:T(8,128)(2,1)S(1)} %bitcast.11), channel_id=1, source_target_pairs={{0,16},{8,24},{16,0},{24,8},{1,17},{9,25},{17,1},{25,9},{2,18},{10... | collective-permute-start | bytes 393224 | tf_op jit(solution)/shard_map/ppermute | solution.py:30
  74.8 1.4 %collective-permute-start.24 = (bf16[128,512]{1,0:T(8,128)(2,1)S(1)}, bf16[128,512]{1,0:T(8,128)(2,1)S(1)}, u32[]{:S(2)}, u32[]{:S(2)}) collective-permute-start(bf16[128,512]{1,0:T(8,128)(2,1)S(1)} %bitcast.12), channel_id=1, source_target_pairs={{0,24},{8,16},{16,8},{24,0},{1,25},{9,17},{17,9},{25,1},{2,26},{10... | collective-permute-start | bytes 393224 | tf_op jit(solution)/shard_map/ppermute | solution.py:30
  76.2 1.5 %shard_map.107 = bf16[128,512]{1,0:T(8,128)(2,1)} custom-call(s32[1]{0:T(128)} %bitcast.me_ref, bf16[144,256]{1,0:T(8,128)(2,1)S(1)} %shard_map.106.refs_0_.refs_8_, bf16[144,256]{1,0:T(8,128)(2,1)S(1)} %collective-permute-done.15.refs_1_.refs_11_.refs_9_, bf16[144,256]{1,0:T(8,128)(2,1)S(1)} %collective-permute-done.16.refs_2_.refs_1_.refs_10_, ...), custom_call_target="tpu_custom_call" | custom-call | tf_op jit(solution)/shard_map/pallas_call | solution.py:34
  79.3 1.3 %collective-permute-done.24.refs_3_ = bf16[128,512]{1,0:T(8,128)(2,1)S(1)} collective-permute-done((bf16[128,512]{1,0:T(8,128)(2,1)S(1)}, bf16[128,512]{1,0:T(8,128)(2,1)S(1)}, u32[]{:S(2)}, u32[]{:S(2)}) %collective-permute-start.24) | collective-permute-done | bytes 131104 | tf_op jit(solution)/shard_map/ppermute | solution.py:30
  80.7 2.6 %shard_map.109 = f32[512,2048]{1,0:T(8,128)} custom-call(s32[1]{0:T(128)} %bitcast.me_ref, bf16[128,512]{1,0:T(8,128)(2,1)S(1)} %bitcast.13, bf16[128,512]{1,0:T(8,128)(2,1)S(1)} %collective-permute-done.22.refs_1_, bf16[128,512]{1,0:T(8,128)(2,1)S(1)} %collective-permute-done.23.refs_2_, bf16[128,512]{1,0:T(8,128)(2,1)S(1)} %collective-permute-done.24.refs_3_, ...), custom_call_target="tpu_custom_call" | custom-call | tf_op jit(solution)/shard_map/pallas_call | solution.py:34
  (76 shorter events, 10.7 us)
Async XLA Ops:
  0.6 5.7 %collective-permute-start.1 = (bf16[128,256]{1,0:T(8,128)(2,1)}, bf16[128,256]{1,0:T(8,128)(2,1)S(1)}, u32[]{:S(2)}, u32[]{:S(2)}) collective-permute-start(bf16[128,256]{1,0:T(8,128)(2,1)} %bitcast.14), channel_id=1, source_target_pairs={{0,2},{1,3},{2,0},{3,1},{4,6},{5,7},{6,4},{7,5},{8,10},{9,11},{10,... | collective-permute-start | bytes 196616 | tf_op jit(solution)/shard_map/ppermute | solution.py:30
  3.8 7.5 %collective-permute-start.3 = (bf16[128,256]{1,0:T(8,128)(2,1)}, bf16[128,256]{1,0:T(8,128)(2,1)S(1)}, u32[]{:S(2)}, u32[]{:S(2)}) collective-permute-start(bf16[128,256]{1,0:T(8,128)(2,1)} %bitcast.15), channel_id=1, source_target_pairs={{0,4},{1,5},{2,6},{3,7},{4,0},{5,1},{6,2},{7,3},{8,12},{9,13},{10,... | collective-permute-start | bytes 196616 | tf_op jit(solution)/shard_map/ppermute | solution.py:30
  6.3 6.3 %collective-permute-start.5 = (bf16[128,256]{1,0:T(8,128)(2,1)}, bf16[128,256]{1,0:T(8,128)(2,1)S(1)}, u32[]{:S(2)}, u32[]{:S(2)}) collective-permute-start(bf16[128,256]{1,0:T(8,128)(2,1)} %bitcast.16), channel_id=1, source_target_pairs={{0,6},{1,7},{2,4},{3,5},{4,2},{5,3},{6,0},{7,1},{8,14},{9,15},{10,... | collective-permute-start | bytes 196616 | tf_op jit(solution)/shard_map/ppermute | solution.py:30
  6.3 11.0 %collective-permute-start = (bf16[128,256]{1,0:T(8,128)(2,1)}, bf16[128,256]{1,0:T(8,128)(2,1)S(1)}, u32[]{:S(2)}, u32[]{:S(2)}) collective-permute-start(bf16[128,256]{1,0:T(8,128)(2,1)} %bitcast.17), channel_id=1, source_target_pairs={{0,1},{1,0},{2,3},{3,2},{4,5},{5,4},{6,7},{7,6},{8,9},{9,8},{10,11... | collective-permute-start | bytes 196616 | tf_op jit(solution)/shard_map/ppermute | solution.py:30
  6.4 11.0 %collective-permute-start.2 = (bf16[128,256]{1,0:T(8,128)(2,1)S(1)}, bf16[128,256]{1,0:T(8,128)(2,1)S(1)}, u32[]{:S(2)}, u32[]{:S(2)}) collective-permute-start(bf16[128,256]{1,0:T(8,128)(2,1)S(1)} %collective-permute-done.1.refs_2_), channel_id=1, source_target_pairs={{0,1},{1,0},{2,3},{3,2},{4,5},{5,4},{6,7},{7,6},{8,9},{9,8},{10,11... | collective-permute-start | bytes 196616 | tf_op jit(solution)/shard_map/ppermute | solution.py:30
  11.2 6.1 %collective-permute-start.4 = (bf16[128,256]{1,0:T(8,128)(2,1)S(1)}, bf16[128,256]{1,0:T(8,128)(2,1)S(1)}, u32[]{:S(2)}, u32[]{:S(2)}) collective-permute-start(bf16[128,256]{1,0:T(8,128)(2,1)S(1)} %collective-permute-done.3.refs_4_.refs_0_), channel_id=1, source_target_pairs={{0,1},{1,0},{2,3},{3,2},{4,5},{5,4},{6,7},{7,6},{8,9},{9,8},{10,11... | collective-permute-start | bytes 196616 | tf_op jit(solution)/shard_map/ppermute | solution.py:30
  16.8 5.5 %collective-permute-start.11 = (bf16[4,128,256]{2,1,0:T(8,128)(2,1)S(1)}, bf16[4,128,256]{2,1,0:T(8,128)(2,1)S(1)}, u32[]{:S(2)}, u32[]{:S(2)}) collective-permute-start(bf16[4,128,256]{2,1,0:T(8,128)(2,1)S(1)} %get-tuple-element.42), channel_id=1, source_target_pairs={{0,1},{1,0},{2,3},{3,2},{4,5},{5,4},{6,7},{7,6},{8,9},{9,8},{10,11... | collective-permute-start | bytes 786440 | tf_op jit(solution)/shard_map/ppermute | solution.py:30
  22.3 7.0 %collective-permute-start.12 = (bf16[128,256]{1,0:T(8,128)(2,1)S(1)}, bf16[128,256]{1,0:T(8,128)(2,1)S(1)}, u32[]{:S(2)}, u32[]{:S(2)}) collective-permute-start(bf16[128,256]{1,0:T(8,128)(2,1)S(1)} %get-tuple-element.44), channel_id=1, source_target_pairs={{0,6},{1,7},{2,4},{3,5},{4,2},{5,3},{6,0},{7,1},{8,14},{9,15},{10,... | collective-permute-start | bytes 196616 | tf_op jit(solution)/shard_map/ppermute | solution.py:30
  24.6 7.0 %collective-permute-start.13 = (bf16[128,256]{1,0:T(8,128)(2,1)S(1)}, bf16[128,256]{1,0:T(8,128)(2,1)S(1)}, u32[]{:S(2)}, u32[]{:S(2)}) collective-permute-start(bf16[128,256]{1,0:T(8,128)(2,1)S(1)} %get-tuple-element.45), channel_id=1, source_target_pairs={{0,4},{1,5},{2,6},{3,7},{4,0},{5,1},{6,2},{7,3},{8,12},{9,13},{10,... | collective-permute-start | bytes 196616 | tf_op jit(solution)/shard_map/ppermute | solution.py:30
  24.6 7.0 %collective-permute-start.14 = (bf16[128,256]{1,0:T(8,128)(2,1)S(1)}, bf16[128,256]{1,0:T(8,128)(2,1)S(1)}, u32[]{:S(2)}, u32[]{:S(2)}) collective-permute-start(bf16[128,256]{1,0:T(8,128)(2,1)S(1)} %get-tuple-element.46), channel_id=1, source_target_pairs={{0,2},{1,3},{2,0},{3,1},{4,6},{5,7},{6,4},{7,5},{8,10},{9,11},{10,... | collective-permute-start | bytes 196616 | tf_op jit(solution)/shard_map/ppermute | solution.py:30
  26.9 7.8 %collective-permute-start.10 = (bf16[272,128]{1,0:T(8,128)(2,1)S(1)}, bf16[272,128]{1,0:T(8,128)(2,1)S(1)}, u32[]{:S(2)}, u32[]{:S(2)}) collective-permute-start(bf16[272,128]{1,0:T(8,128)(2,1)S(1)} %get-tuple-element.40), channel_id=1, source_target_pairs={{0,2},{1,3},{2,0},{3,1},{4,6},{5,7},{6,4},{7,5},{8,10},{9,11},{10,... | collective-permute-start | bytes 208904 | tf_op jit(solution)/shard_map/ppermute | solution.py:30
  27.0 8.2 %collective-permute-start.8 = (bf16[272,128]{1,0:T(8,128)(2,1)S(1)}, bf16[272,128]{1,0:T(8,128)(2,1)S(1)}, u32[]{:S(2)}, u32[]{:S(2)}) collective-permute-start(bf16[272,128]{1,0:T(8,128)(2,1)S(1)} %get-tuple-element.38), channel_id=1, source_target_pairs={{0,6},{1,7},{2,4},{3,5},{4,2},{5,3},{6,0},{7,1},{8,14},{9,15},{10,... | collective-permute-start | bytes 208904 | tf_op jit(solution)/shard_map/ppermute | solution.py:30
  29.3 11.5 %collective-permute-start.9 = (bf16[272,128]{1,0:T(8,128)(2,1)S(1)}, bf16[272,128]{1,0:T(8,128)(2,1)S(1)}, u32[]{:S(2)}, u32[]{:S(2)}) collective-permute-start(bf16[272,128]{1,0:T(8,128)(2,1)S(1)} %get-tuple-element.39), channel_id=1, source_target_pairs={{0,4},{1,5},{2,6},{3,7},{4,0},{5,1},{6,2},{7,3},{8,12},{9,13},{10,... | collective-permute-start | bytes 208904 | tf_op jit(solution)/shard_map/ppermute | solution.py:30
  31.6 10.6 %collective-permute-start.34 = (bf16[128,256]{1,0:T(8,128)(2,1)S(1)}, bf16[128,256]{1,0:T(8,128)(2,1)S(1)}, u32[]{:S(2)}, u32[]{:S(2)}) collective-permute-start(bf16[128,256]{1,0:T(8,128)(2,1)S(1)} %shard_map.105.refs_4_), channel_id=1, source_target_pairs={{0,4},{1,5},{2,6},{3,7},{4,0},{5,1},{6,2},{7,3},{8,12},{9,13},{10,... | collective-permute-start | bytes 196616 | tf_op jit(solution)/shard_map/ppermute | solution.py:30
  32.6 9.6 %collective-permute-start.36 = (bf16[128,256]{1,0:T(8,128)(2,1)S(1)}, bf16[128,256]{1,0:T(8,128)(2,1)S(1)}, u32[]{:S(2)}, u32[]{:S(2)}) collective-permute-start(bf16[128,256]{1,0:T(8,128)(2,1)S(1)} %shard_map.105.refs_4_), channel_id=1, source_target_pairs={{0,6},{1,7},{2,4},{3,5},{4,2},{5,3},{6,0},{7,1},{8,14},{9,15},{10,... | collective-permute-start | bytes 196616 | tf_op jit(solution)/shard_map/ppermute | solution.py:30
  34.8 9.5 %collective-permute-start.32 = (bf16[128,256]{1,0:T(8,128)(2,1)S(1)}, bf16[128,256]{1,0:T(8,128)(2,1)S(1)}, u32[]{:S(2)}, u32[]{:S(2)}) collective-permute-start(bf16[128,256]{1,0:T(8,128)(2,1)S(1)} %shard_map.105.refs_4_), channel_id=1, source_target_pairs={{0,2},{1,3},{2,0},{3,1},{4,6},{5,7},{6,4},{7,5},{8,10},{9,11},{10,... | collective-permute-start | bytes 196616 | tf_op jit(solution)/shard_map/ppermute | solution.py:30
  42.2 6.9 %collective-permute-start.20 = (bf16[144,256]{1,0:T(8,128)(2,1)S(1)}, bf16[144,256]{1,0:T(8,128)(2,1)S(1)}, u32[]{:S(2)}, u32[]{:S(2)}) collective-permute-start(bf16[144,256]{1,0:T(8,128)(2,1)S(1)} %shard_map.106.refs_0_.refs_8_), channel_id=1, source_target_pairs={{0,6},{1,7},{2,4},{3,5},{4,2},{5,3},{6,0},{7,1},{8,14},{9,15},{10,... | collective-permute-start | bytes 221192 | tf_op jit(solution)/shard_map/ppermute | solution.py:30
  44.3 6.0 %collective-permute-start.16 = (bf16[144,256]{1,0:T(8,128)(2,1)S(1)}, bf16[144,256]{1,0:T(8,128)(2,1)S(1)}, u32[]{:S(2)}, u32[]{:S(2)}) collective-permute-start(bf16[144,256]{1,0:T(8,128)(2,1)S(1)} %shard_map.106.refs_0_.refs_8_), channel_id=1, source_target_pairs={{0,2},{1,3},{2,0},{3,1},{4,6},{5,7},{6,4},{7,5},{8,10},{9,11},{10,... | collective-permute-start | bytes 221192 | tf_op jit(solution)/shard_map/ppermute | solution.py:30
  46.3 7.0 %collective-permute-start.19 = (bf16[144,256]{1,0:T(8,128)(2,1)S(1)}, bf16[144,256]{1,0:T(8,128)(2,1)S(1)}, u32[]{:S(2)}, u32[]{:S(2)}) collective-permute-start(bf16[144,256]{1,0:T(8,128)(2,1)S(1)} %collective-permute-done.18.refs_4_.refs_2_.refs_8_), channel_id=1, source_target_pairs={{0,1},{1,0},{2,3},{3,2},{4,5},{5,4},{6,7},{7,6},{8,9},{9,8},{10,11... | collective-permute-start | bytes 221192 | tf_op jit(solution)/shard_map/ppermute | solution.py:30
  50.3 7.1 %collective-permute-start.15 = (bf16[144,256]{1,0:T(8,128)(2,1)S(1)}, bf16[144,256]{1,0:T(8,128)(2,1)S(1)}, u32[]{:S(2)}, u32[]{:S(2)}) collective-permute-start(bf16[144,256]{1,0:T(8,128)(2,1)S(1)} %shard_map.106.refs_0_.refs_8_), channel_id=1, source_target_pairs={{0,1},{1,0},{2,3},{3,2},{4,5},{5,4},{6,7},{7,6},{8,9},{9,8},{10,11... | collective-permute-start | bytes 221192 | tf_op jit(solution)/shard_map/ppermute | solution.py:30
  50.3 14.7 %collective-permute-start.25 = (bf16[4,128,256]{2,1,0:T(8,128)(2,1)S(1)}, bf16[4,128,256]{2,1,0:T(8,128)(2,1)S(1)}, u32[]{:S(2)}, u32[]{:S(2)}) collective-permute-start(bf16[4,128,256]{2,1,0:T(8,128)(2,1)S(1)} %shard_map.108.refs_4_), channel_id=1, source_target_pairs={{0,8},{8,0},{16,24},{24,16},{1,9},{9,1},{17,25},{25,17},{2,10},{10... | collective-permute-start | bytes 786440 | tf_op jit(solution)/shard_map/ppermute | solution.py:30
  51.9 14.1 %collective-permute-start.26 = (bf16[4,128,256]{2,1,0:T(8,128)(2,1)S(1)}, bf16[4,128,256]{2,1,0:T(8,128)(2,1)S(1)}, u32[]{:S(2)}, u32[]{:S(2)}) collective-permute-start(bf16[4,128,256]{2,1,0:T(8,128)(2,1)S(1)} %shard_map.108.refs_4_), channel_id=1, source_target_pairs={{0,16},{8,24},{16,0},{24,8},{1,17},{9,25},{17,1},{25,9},{2,18},{10... | collective-permute-start | bytes 786440 | tf_op jit(solution)/shard_map/ppermute | solution.py:30
  53.4 12.5 %collective-permute-start.27 = (bf16[4,128,256]{2,1,0:T(8,128)(2,1)S(1)}, bf16[4,128,256]{2,1,0:T(8,128)(2,1)S(1)}, u32[]{:S(2)}, u32[]{:S(2)}) collective-permute-start(bf16[4,128,256]{2,1,0:T(8,128)(2,1)S(1)} %shard_map.108.refs_4_), channel_id=1, source_target_pairs={{0,24},{8,16},{16,8},{24,0},{1,25},{9,17},{17,9},{25,1},{2,26},{10... | collective-permute-start | bytes 786440 | tf_op jit(solution)/shard_map/ppermute | solution.py:30
  61.6 6.0 %collective-permute-start.22 = (bf16[128,512]{1,0:T(8,128)(2,1)S(1)}, bf16[128,512]{1,0:T(8,128)(2,1)S(1)}, u32[]{:S(2)}, u32[]{:S(2)}) collective-permute-start(bf16[128,512]{1,0:T(8,128)(2,1)S(1)} %bitcast.10), channel_id=1, source_target_pairs={{0,8},{8,0},{16,24},{24,16},{1,9},{9,1},{17,25},{25,17},{2,10},{10... | collective-permute-start | bytes 393224 | tf_op jit(solution)/shard_map/ppermute | solution.py:30
  63.1 6.1 %collective-permute-start.40 = (bf16[256,128]{1,0:T(8,128)(2,1)S(1)}, bf16[256,128]{1,0:T(8,128)(2,1)S(1)}, u32[]{:S(2)}, u32[]{:S(2)}) collective-permute-start(bf16[256,128]{1,0:T(8,128)(2,1)S(1)} %get-tuple-element.56), channel_id=1, source_target_pairs={{0,6},{1,7},{2,4},{3,5},{4,2},{5,3},{6,0},{7,1},{8,14},{9,15},{10,... | collective-permute-start | bytes 196616 | tf_op jit(solution)/shard_map/ppermute | solution.py:30
  65.0 15.7 %collective-permute-start.28 = (bf16[4,128,256]{2,1,0:T(8,128)(2,1)S(1)}, bf16[4,128,256]{2,1,0:T(8,128)(2,1)S(1)}, u32[]{:S(2)}, u32[]{:S(2)}) collective-permute-start(bf16[4,128,256]{2,1,0:T(8,128)(2,1)S(1)} %collective-permute-done.25.refs_5_), channel_id=1, source_target_pairs={{0,1},{1,0},{2,3},{3,2},{4,5},{5,4},{6,7},{7,6},{8,9},{9,8},{10,11... | collective-permute-start | bytes 786440 | tf_op jit(solution)/shard_map/ppermute | solution.py:30
  65.9 14.8 %collective-permute-start.29 = (bf16[4,128,256]{2,1,0:T(8,128)(2,1)S(1)}, bf16[4,128,256]{2,1,0:T(8,128)(2,1)S(1)}, u32[]{:S(2)}, u32[]{:S(2)}) collective-permute-start(bf16[4,128,256]{2,1,0:T(8,128)(2,1)S(1)} %collective-permute-done.26.refs_6_), channel_id=1, source_target_pairs={{0,1},{1,0},{2,3},{3,2},{4,5},{5,4},{6,7},{7,6},{8,9},{9,8},{10,11... | collective-permute-start | bytes 786440 | tf_op jit(solution)/shard_map/ppermute | solution.py:30
  65.9 14.8 %collective-permute-start.30 = (bf16[4,128,256]{2,1,0:T(8,128)(2,1)S(1)}, bf16[4,128,256]{2,1,0:T(8,128)(2,1)S(1)}, u32[]{:S(2)}, u32[]{:S(2)}) collective-permute-start(bf16[4,128,256]{2,1,0:T(8,128)(2,1)S(1)} %collective-permute-done.27.refs_7_), channel_id=1, source_target_pairs={{0,1},{1,0},{2,3},{3,2},{4,5},{5,4},{6,7},{7,6},{8,9},{9,8},{10,11... | collective-permute-start | bytes 786440 | tf_op jit(solution)/shard_map/ppermute | solution.py:30
  67.6 5.7 %collective-permute-start.41 = (bf16[256,128]{1,0:T(8,128)(2,1)S(1)}, bf16[256,128]{1,0:T(8,128)(2,1)S(1)}, u32[]{:S(2)}, u32[]{:S(2)}) collective-permute-start(bf16[256,128]{1,0:T(8,128)(2,1)S(1)} %get-tuple-element.57), channel_id=1, source_target_pairs={{0,4},{1,5},{2,6},{3,7},{4,0},{5,1},{6,2},{7,3},{8,12},{9,13},{10,... | collective-permute-start | bytes 196616 | tf_op jit(solution)/shard_map/ppermute | solution.py:30
  69.3 5.5 %collective-permute-start.42 = (bf16[256,128]{1,0:T(8,128)(2,1)S(1)}, bf16[256,128]{1,0:T(8,128)(2,1)S(1)}, u32[]{:S(2)}, u32[]{:S(2)}) collective-permute-start(bf16[256,128]{1,0:T(8,128)(2,1)S(1)} %get-tuple-element.58), channel_id=1, source_target_pairs={{0,2},{1,3},{2,0},{3,1},{4,6},{5,7},{6,4},{7,5},{8,10},{9,11},{10,... | collective-permute-start | bytes 196616 | tf_op jit(solution)/shard_map/ppermute | solution.py:30
  73.2 6.1 %collective-permute-start.23 = (bf16[128,512]{1,0:T(8,128)(2,1)S(1)}, bf16[128,512]{1,0:T(8,128)(2,1)S(1)}, u32[]{:S(2)}, u32[]{:S(2)}) collective-permute-start(bf16[128,512]{1,0:T(8,128)(2,1)S(1)} %bitcast.11), channel_id=1, source_target_pairs={{0,16},{8,24},{16,0},{24,8},{1,17},{9,25},{17,1},{25,9},{2,18},{10... | collective-permute-start | bytes 393224 | tf_op jit(solution)/shard_map/ppermute | solution.py:30
  74.8 5.9 %collective-permute-start.24 = (bf16[128,512]{1,0:T(8,128)(2,1)S(1)}, bf16[128,512]{1,0:T(8,128)(2,1)S(1)}, u32[]{:S(2)}, u32[]{:S(2)}) collective-permute-start(bf16[128,512]{1,0:T(8,128)(2,1)S(1)} %bitcast.12), channel_id=1, source_target_pairs={{0,24},{8,16},{16,8},{24,0},{1,25},{9,17},{17,9},{25,1},{2,26},{10... | collective-permute-start | bytes 393224 | tf_op jit(solution)/shard_map/ppermute | solution.py:30
  (15 other events, 75.0 us)

commit v4 on v3

--- a/solution.py
+++ b/solution.py
@@ -12,6 +12,8 @@
 MASKED = -1e30
 EXTRA = 16
 MIB = 1 << 20
+GRAD_VMEM = 55
+ADD_COST = 20
 
 NT = (((1,), (1,)), ((), ()))
 NN = (((1,), (0,)), ((), ()))
@@ -30,7 +32,7 @@
     return lax.ppermute(x, axis, [(j, j ^ distance) for j in range(size)])
 
 
-def call(kernel, *args, out, ins, outs, scratch=(), vmem=8, alias=None):
+def call(kernel, *args, out, ins, outs, scratch=(), vmem=8, alias=None, cost=None):
     return pl.pallas_call(
         kernel,
         out_shape=out,
@@ -38,7 +40,8 @@
         out_specs=outs,
         scratch_shapes=list(scratch),
         input_output_aliases=alias or {},
-        compiler_params=pltpu.CompilerParams(vmem_limit_bytes=vmem * MIB),
+        compiler_params=pltpu.CompilerParams(vmem_limit_bytes=int(vmem * MIB)),
+        cost_estimate=cost,
     )(*args)
 
 
@@ -93,55 +96,59 @@
     return ref.at[:, pl.ds(pl.multiple_of(owner * width, width), width)]
 
 
-def forward_kernel(size, passages, lengths_ref, *refs):
-    q_refs = refs[:size]
-    keys_ref, values_ref, even_ref, odd_ref, weights_ref, tops_ref, q_buf, s_buf, bias_ref = refs[size:]
-    width = q_buf.shape[2]
+def pair_of(ref, me, slot, width, pair):
+    at = jnp.bitwise_xor(me, slot) * width + pair * PAIR
+    return ref.at[:, pl.ds(pl.multiple_of(at, PAIR), PAIR)]
+
+
+def forward_kernel(parity, passages, me_ref, lengths_ref, *refs):
+    out_ref, weights_ref, tops_ref, q_buf, s_buf, bias_ref = refs[-6:]
+    keys_ref, values_ref = refs[-8:-6]
+    me = me_ref[0]
+    count, _, width = q_buf.shape
     pairs = width // PAIR
-    for s in range(size):
-        q_buf[s] = q_refs[s][...]
-    bias_ref[...] = mask_bias(lengths_ref, passages, keys_ref.shape[1] // passages)
+    for k in range(count):
+        q_buf[k] = refs[k][...]
+    bias_ref[...] = mask_bias(lengths_ref, passages, keys_ref.shape[0] // passages)
     lane_low = lax.broadcasted_iota(jnp.int32, (1, PAIR), 1) < HEAD_SIZE
 
-    def score(s, p):
-        lanes = slice(p * PAIR, (p + 1) * PAIR)
-        queries = block_stack(q_buf[s, :, lanes], lane_low)
+    def score(k, p):
+        queries = block_stack(q_buf[k, :, p * PAIR : (p + 1) * PAIR], lane_low)
         bias = bias_ref[...]
-        scores = dot(keys_ref[s, :, lanes], queries, NT) + jnp.concatenate([bias, bias], axis=1)
+        keys = pair_of(keys_ref, me, 2 * k + parity, width, p)[...]
+        scores = dot(keys, queries, NT) + jnp.concatenate([bias, bias], axis=1)
         s_buf[p] = scores
         return jnp.max(scores, axis=0, keepdims=True)
 
-    def mix(s, p, top, out_ref, k):
-        lanes = slice(p * PAIR, (p + 1) * PAIR)
+    def mix(k, p, top):
         weights = jnp.exp(s_buf[p] - top)
         total = jnp.sum(weights, axis=0, keepdims=True)
         rounded = weights.astype(jnp.bfloat16)
-        weights_ref[s * pairs + p] = rounded
-        mixed = dot(values_ref[s, :, lanes], rounded, TN) / total
-        out_ref[k, lanes, :] = diagonal(mixed).astype(jnp.bfloat16)
+        weights_ref[k * pairs + p] = rounded
+        values = pair_of(values_ref, me, 2 * k + parity, width, p)[...]
+        mixed = dot(values, rounded, TN) / total
+        out_ref[k, p * PAIR : (p + 1) * PAIR, :] = diagonal(mixed).astype(jnp.bfloat16)
         return top + jnp.log(total)
 
-    def one_slot(s, out_ref, k, first_top):
-        tops, lses = [first_top], []
+    def by_head(rows):
+        n = rows[0].shape[1] // 2
+        return jnp.concatenate([x[:, h * n : (h + 1) * n] for x in rows for h in range(2)], axis=0)
+
+    def one_slot(k, top):
+        tops, lses = [top], []
         for p in range(pairs):
             if p + 1 < pairs:
-                tops.append(score(s, p + 1))
-            else:
-                following = score(jnp.minimum(s + 1, size - 1), 0) if pairs > 1 else None
-            lses.append(mix(s, p, tops[p], out_ref, k))
-        if following is None:
-            following = score(jnp.minimum(s + 1, size - 1), 0)
-        n = first_top.shape[1] // 2
-        tops_ref[s] = jnp.concatenate([x[:, h * n : (h + 1) * n] for x in tops for h in range(2)], axis=0)
-        rows = jnp.concatenate([x[:, h * n : (h + 1) * n] for x in lses for h in range(2)], axis=0)
-        out_ref[k, width:, :] = thirds(rows)
-        return following
-
-    def body(k, top):
-        top = one_slot(2 * k, even_ref, k, top)
-        return one_slot(2 * k + 1, odd_ref, k, top)
-
-    lax.fori_loop(0, size // 2, body, score(0, 0))
+                tops.append(score(k, p + 1))
+            elif pairs > 1:
+                top = score(jnp.minimum(k + 1, count - 1), 0)
+            lses.append(mix(k, p, tops[p]))
+        if pairs == 1:
+            top = score(jnp.minimum(k + 1, count - 1), 0)
+        tops_ref[k] = by_head(tops)
+        out_ref[k, width:, :] = thirds(by_head(lses))
+        return top
+
+    lax.fori_loop(0, count // 2, lambda k, top: one_slot(2 * k + 1, one_slot(2 * k, top)), score(0, 0))
 
 
 def merge(blocks):
@@ -192,8 +199,9 @@
 def backward_kernel(slots, carried, me_ref, *refs):
     count = len(slots)
     q_refs, g_refs, c_refs = refs[:count], refs[count : 2 * count], refs[2 * count : 3 * count]
-    keys_ref, values_ref, weights_ref, tops_ref = refs[3 * count : 3 * count + 4]
-    dk_ref, dv_ref, even_ref, odd_ref, q_buf, g_buf, st_buf, p_buf, dk_buf, dv_buf, sem = refs[3 * count + 4 + carried :]
+    keys_ref, values_ref, *kept = refs[3 * count : 3 * count + 6]
+    weights_refs, tops_refs = kept[:2], kept[2:]
+    dk_ref, dv_ref, even_ref, odd_ref, q_buf, g_buf, st_buf, p_buf, dk_buf, dv_buf, sem = refs[3 * count + 6 + carried :]
     me = me_ref[0]
     answers, width = q_buf.shape[1:]
     pairs = width // PAIR
@@ -209,7 +217,7 @@
     lane_low = lax.broadcasted_iota(jnp.int32, (1, PAIR), 1) < HEAD_SIZE
     for i in range(count):
         stats = stats_of(c_refs[i], answers)
-        share = jnp.exp(tops_ref[first + i] - stats[:heads])
+        share = jnp.exp(tops_refs[i % 2][first // 2 + i // 2] - stats[:heads])
         st_buf[i] = jnp.concatenate([share, stats[heads:]], axis=0)
         q_buf[i] = q_refs[i][...]
         g_buf[i] = g_refs[i][...]
@@ -218,36 +226,39 @@
         return block_stack(g_buf[i, :, p * PAIR : (p + 1) * PAIR], lane_low)
 
     def prob_grad(i, p):
-        p_buf[p] = dot(values_ref[first + i, :, p * PAIR : (p + 1) * PAIR], grads_of(i, p), NT)
+        p_buf[p] = dot(pair_of(values_ref, me, first + i, width, p)[...], grads_of(i, p), NT)
 
     def row_pair(rows, at):
         return jnp.concatenate([rows[at : at + 1], rows[at + 1 : at + 2]], axis=1)
 
-    def rest(i, p, out_ref, k):
+    def rest(i, p, parity, k):
+        out_ref = (even_ref, odd_ref)[parity]
         lanes = slice(p * PAIR, (p + 1) * PAIR)
         queries = block_stack(q_buf[i, :, lanes], lane_low)
         stats = st_buf[i]
-        probs = weights_ref[(first + i) * pairs + p].astype(jnp.float32) * row_pair(stats, 2 * p)
+        probs = weights_refs[parity][(first // 2 + k) * pairs + p].astype(jnp.float32) * row_pair(stats, 2 * p)
         score_grad = (probs * (p_buf[p] - row_pair(stats, heads + 2 * p))).astype(jnp.bfloat16)
         dv_buf[i, :, lanes] = dot(probs.astype(jnp.bfloat16), grads_of(i, p), NN).astype(jnp.bfloat16)
         dk_buf[i, :, lanes] = dot(score_grad, queries, NN).astype(jnp.bfloat16)
-        out_ref[k, lanes, :] = diagonal(dot(keys_ref[first + i, :, lanes], score_grad, TN)).astype(jnp.bfloat16)
-
-    def one_slot(i, out_ref, k):
+        out_ref[k, lanes, :] = diagonal(dot(pair_of(keys_ref, me, first + i, width, p)[...], score_grad, TN)).astype(
+            jnp.bfloat16
+        )
+
+    def one_slot(i, parity, k):
         for p in range(pairs):
             if p + 1 < pairs:
                 prob_grad(i, p + 1)
-                rest(i, p, out_ref, k)
+                rest(i, p, parity, k)
             else:
-                rest(i, p, out_ref, k) if pairs == 1 else None
+                rest(i, p, parity, k) if pairs == 1 else None
                 prob_grad(jnp.minimum(i + 1, count - 1), 0)
-                rest(i, p, out_ref, k) if pairs > 1 else None
+                rest(i, p, parity, k) if pairs > 1 else None
         dk_copy(i).start()
         dv_copy(i).start()
 
     def body(k, carry):
-        one_slot(2 * k, even_ref, k)
-        one_slot(2 * k + 1, odd_ref, k)
+        one_slot(2 * k, 0, k)
+        one_slot(2 * k + 1, 1, k)
         return carry
 
     prob_grad(0, 0)
@@ -276,30 +287,23 @@
     refs[-1][...] = total.T.astype(jnp.bfloat16)
 
 
-def grad_partial_kernel(size, me_ref, cot_ref, weight_ref, keys_ref, values_ref, *refs):
-    even_ref, odd_ref, k_out, v_out, cot_buf, w_buf, sem, cot_sem = refs
+def grad_partial_kernel(size, me_ref, cot_ref, weight_ref, even_ref, odd_ref, cot_buf, w_buf, sem, cot_sem):
     me = me_ref[0]
     width = w_buf.shape[2]
 
-    def copy(ref, buf, lane, s):
-        return pltpu.make_async_copy(columns_of(ref, me, s, width), buf.at[s], sem.at[lane, s])
-
-    order = list(range(1, size, 2)) + list(range(0, size, 2))
+    def copy(s):
+        return pltpu.make_async_copy(columns_of(weight_ref, me, s, width), w_buf.at[s], sem.at[s])
+
     cot_copy = pltpu.make_async_copy(cot_ref, cot_buf, cot_sem)
     cot_copy.start()
+    order = list(range(1, size, 2)) + list(range(0, size, 2))
     for s in order:
-        copy(weight_ref, w_buf, 0, s).start()
-    for s in range(size):
-        copy(keys_ref, k_out, 1, s).start()
-        copy(values_ref, v_out, 2, s).start()
+        copy(s).start()
     cot_copy.wait()
     cot = cot_buf[...]
     for s in order:
-        copy(weight_ref, w_buf, 0, s).wait()
+        copy(s).wait()
         (odd_ref if s % 2 else even_ref)[s // 2] = dot(cot, w_buf[s], NN).astype(jnp.bfloat16)
-    for s in range(size):
-        copy(keys_ref, k_out, 1, s).wait()
-        copy(values_ref, v_out, 2, s).wait()
 
 
 def layer_out_kernel(size, me_ref, *refs):
@@ -342,6 +346,10 @@
     out_ref = refs[-1]
     for k in range(out_ref.shape[0]):
         out_ref[k] = refs[k][: out_ref.shape[1], :]
+
+
+def cost(products, exps, nbytes):
+    return pl.CostEstimate(flops=2 * products, transcendentals=exps, bytes_accessed=nbytes)
 
 
 def shaped(shape, dtype):
@@ -368,49 +376,65 @@
     q_even = spread(query, size)
     slots = interleaved(q_even, across(q_even, size))
 
-    resident = shaped((size, key_count, width), bf16)
-    g_even, g_odd, slot_keys, slot_values = call(
+    g_even, g_odd = call(
         functools.partial(grad_partial_kernel, size),
         me,
         cot,
         out_weight,
-        key_rows,
-        value_rows,
-        out=[shaped((half, answers, width), bf16)] * 2 + [resident] * 2,
-        ins=[SMEM] + [HBM] * 4,
-        outs=[VMEM] * 4,
+        out=[shaped((half, answers, width), bf16)] * 2,
+        ins=[SMEM, HBM, HBM],
+        outs=[VMEM] * 2,
         scratch=[
             pltpu.VMEM((answers, model), bf16),
             pltpu.VMEM((size, model, width), bf16),
-            pltpu.SemaphoreType.DMA((3, size)),
+            pltpu.SemaphoreType.DMA((size,)),
             pltpu.SemaphoreType.DMA(()),
         ],
-        vmem=49,
+        vmem=GRAD_VMEM,
+        cost=cost(answers * model * inner, 0, 2 * model * inner),
     )
     g_other = swap(g_odd, "psg", size, 1)
     block = shaped((answers, width), bf16)
-    g_sums = call(add_pair_kernel, g_even, g_other, out=[block] * half, ins=[VMEM] * 2, outs=[VMEM] * half)
+    g_sums = call(
+        add_pair_kernel,
+        g_even,
+        g_other,
+        out=[block] * half,
+        ins=[VMEM] * 2,
+        outs=[VMEM] * half,
+        cost=cost(ADD_COST * answers * model * inner, 0, 2 * model * inner),
+    )
     g_parts = [swap(g_sums[d // 2], "psg", size, d) for d in far_first(size)]
 
     packed = shaped((width + EXTRA, answers), bf16)
     pairs = width // PAIR
-    o_even, o_odd, weights, tops = call(
-        functools.partial(forward_kernel, size, passages),
-        lengths,
-        *slots,
-        slot_keys,
-        slot_values,
-        out=[shaped((half, width + EXTRA, answers), bf16)] * 2
-        + [shaped((size * pairs, key_count, 2 * answers), bf16), shaped((size, heads, answers), f32)],
-        ins=[SMEM] + [VMEM] * (size + 2),
-        outs=[VMEM] * 4,
-        scratch=[
-            pltpu.VMEM((size, answers, width), bf16),
-            pltpu.VMEM((pairs, key_count, 2 * answers), f32),
-            pltpu.VMEM((key_count, PAIR), f32),
-        ],
-        vmem=16,
-    )
+
+    def forward(parity):
+        return call(
+            functools.partial(forward_kernel, parity, passages),
+            me,
+            lengths,
+            *slots[parity::2],
+            key_rows,
+            value_rows,
+            out=[
+                shaped((half, width + EXTRA, answers), bf16),
+                shaped((half * pairs, key_count, 2 * answers), bf16),
+                shaped((half, heads, answers), f32),
+            ],
+            ins=[SMEM, SMEM] + [VMEM] * (half + 2),
+            outs=[VMEM] * 3,
+            scratch=[
+                pltpu.VMEM((half, answers, width), bf16),
+                pltpu.VMEM((pairs, key_count, 2 * answers), f32),
+                pltpu.VMEM((key_count, PAIR), f32),
+            ],
+            vmem=12,
+            cost=cost(2 * answers * key_count * inner // 2, answers * key_count * half * heads, 2 * key_count * inner),
+        )
+
+    o_odd, *kept_odd = forward(1)
+    o_even, *kept_even = forward(0)
 
     o_other = swap(o_odd, "psg", size, 1)
     o_pairs = call(merge_pair_kernel, o_even, o_other, out=[packed] * half, ins=[VMEM] * 2, outs=[VMEM] * half)
@@ -434,20 +458,22 @@
     def backward(chosen, carried):
         count = len(chosen)
         pick = slice(chosen[0], chosen[0] + count)
-        fixed = 1 + 3 * count + 4
+        fixed = 1 + 3 * count + 6
         return call(
             functools.partial(backward_kernel, chosen, len(carried)),
             me,
             *slots[pick],
             *g_slots[pick],
             *c_slots[pick],
-            slot_keys,
-            slot_values,
-            weights,
-            tops,
+            key_rows,
+            value_rows,
+            kept_even[0],
+            kept_odd[0],
+            kept_even[1],
+            kept_odd[1],
             *carried,
             out=[shaped((key_count, inner), bf16)] * 2 + [shaped((count // 2, width, answers), bf16)] * 2,
-            ins=[SMEM] + [VMEM] * (3 * count + 4) + [ANY] * len(carried),
+            ins=[SMEM] + [VMEM] * (3 * count + 6) + [ANY] * len(carried),
             outs=[ANY, ANY, VMEM, VMEM],
             scratch=[
                 pltpu.VMEM((count, answers, width), bf16),
@@ -459,6 +485,7 @@
             + [pltpu.SemaphoreType.DMA((2, count))],
             vmem=16,
             alias={fixed + i: i for i in range(len(carried))},
+            cost=cost(4 * answers * key_count * count * width, 0, 8 * key_count * count * width),
         )
 
     def owners_sums(even, odd, count):

time: 83.4 us -> 85.3 us (1.023)
  waiting for transfers between devices: 25.5 us -> 20.6 us
  starting transfers between devices: 35.8 us -> 40 us
  Pallas kernels: 20.3 us -> 22.1 us
    ppermute x43, waiting for transfers between devices: 25.5 us -> 20.6 us  [swap(): return lax.ppermute(x, axis, [(j, j ^ distance) for j in range(size)])]
    ppermute x43, starting transfers between devices: 35.8 us -> 40 us  [swap(): return lax.ppermute(x, axis, [(j, j ^ distance) for j in range(size)])]
    pallas_call x14 -> x15, Pallas kernels: 20.3 us -> 22.1 us  [call(): pl.pallas_call(kernel, out_shape=out, in_specs=ins, out_specs=outs, scrat...]
  transfers between devices with their start and end apart: 43 -> 43, of which waited for: 14 -> 13; matrix products, arithmetic and copies ran while one was open for 0% -> 0% of each run, Pallas kernels for 21% -> 18%
where the time goes in v4:
time: 85.3 us; the launch traced here: 85.1 us
  starting transfers between devices  40 us (47%)
  Pallas kernels  22.1 us (26%)
  waiting for transfers between devices  20.6 us (24%)
  local copies, waits for them, and re-layouts  1.62 us (2%)
    ppermute x43, starting transfers between devices, swap(): return lax.ppermute(x, axis, [(j, j ^ distance) for j in range(size)])  40 us
    pallas_call x15, Pallas kernels, call(): pl.pallas_call(kernel, out_shape=out, in_specs=ins, out_specs=outs, scrat...  22.1 us
    ppermute x43, waiting for transfers between devices, swap(): return lax.ppermute(x, axis, [(j, j ^ distance) for j in range(size)])  20.6 us
  transfers between devices with their start and end apart: 43, of which 13 were waited for; matrix products, arithmetic and copies ran while one was open for 0% of the time, Pallas kernels for 18%

profile of v4, /device:TPU:0, one launch (start us, length us, event | category | flops | bytes accessed | tf_op | source)
XLA Modules:
  0.0 85.1 jit_solution(14983288495298850323)
XLA Ops:
  0.7 4.2 %shard_map.104 = (bf16[4,128,256]{2,1,0:T(8,128)(2,1)}, bf16[4,128,256]{2,1,0:T(8,128)(2,1)}) custom-call(s32[1]{0:T(128)} %bitcast.me_ref, bf16[128,512]{1,0:T(8,128)(2,1)} %bitcast.17, bf16[512,2048]{1,0:T(8,128)(2,1)} %refs_8_.1), custom_call_target="tpu_custom_call" | custom-call | flops 268435456 | bytes 2097152 | tf_op jit(solution)/shard_map/pallas_call | solution.py:36
  5.4 2.6 %collective-permute-start = (bf16[128,256]{1,0:T(8,128)(2,1)S(1)}, bf16[128,256]{1,0:T(8,128)(2,1)S(1)}, u32[]{:S(2)}, u32[]{:S(2)}) collective-permute-start(bf16[128,256]{1,0:T(8,128)(2,1)S(1)} %bitcast.22), channel_id=1, source_target_pairs={{0,2},{1,3},{2,0},{3,1},{4,6},{5,7},{6,4},{7,5},{8,10},{9,11},{10,... | collective-permute-start | bytes 196616 | tf_op jit(solution)/shard_map/ppermute | solution.py:32
  8.1 2.6 %collective-permute-start.1 = (bf16[128,256]{1,0:T(8,128)(2,1)S(1)}, bf16[128,256]{1,0:T(8,128)(2,1)S(1)}, u32[]{:S(2)}, u32[]{:S(2)}) collective-permute-start(bf16[128,256]{1,0:T(8,128)(2,1)S(1)} %bitcast.23), channel_id=1, source_target_pairs={{0,4},{1,5},{2,6},{3,7},{4,0},{5,1},{6,2},{7,3},{8,12},{9,13},{10,... | collective-permute-start | bytes 196616 | tf_op jit(solution)/shard_map/ppermute | solution.py:32
  11.2 4.6 %collective-permute-done.1.refs_2_.refs_0_ = bf16[128,256]{1,0:T(8,128)(2,1)S(1)} collective-permute-done((bf16[128,256]{1,0:T(8,128)(2,1)S(1)}, bf16[128,256]{1,0:T(8,128)(2,1)S(1)}, u32[]{:S(2)}, u32[]{:S(2)}) %collective-permute-start.1) | collective-permute-done | bytes 65568 | tf_op jit(solution)/shard_map/ppermute | solution.py:32
  15.7 1.0 %collective-permute-done.2.refs_3_.refs_2_ = bf16[128,256]{1,0:T(8,128)(2,1)S(1)} collective-permute-done((bf16[128,256]{1,0:T(8,128)(2,1)S(1)}, bf16[128,256]{1,0:T(8,128)(2,1)S(1)}, u32[]{:S(2)}, u32[]{:S(2)}) %collective-permute-start.2) | collective-permute-done | bytes 65568 | tf_op jit(solution)/shard_map/ppermute | solution.py:32
  17.0 1.0 %collective-permute-done.6.refs_3_ = bf16[128,256]{1,0:T(8,128)(2,1)S(1)} collective-permute-done((bf16[128,256]{1,0:T(8,128)(2,1)S(1)}, bf16[128,256]{1,0:T(8,128)(2,1)S(1)}, u32[]{:S(2)}, u32[]{:S(2)}) %collective-permute-start.6) | collective-permute-done | bytes 65568 | tf_op jit(solution)/shard_map/ppermute | solution.py:32
  18.0 1.6 %copy-done.1 = bf16[1,2,256,2048]{3,2,1,0:T(8,128)(2,1)S(1)} copy-done((bf16[1,2,256,2048]{3,2,1,0:T(8,128)(2,1)S(1)}, bf16[1,2,256,2048]{3,2,1,0:T(8,128)(2,1)}, u32[]{:S(2)}) %copy-start.1) | copy-done | bytes 2097176
  19.6 2.8 %shard_map.102 = (bf16[4,272,128]{2,1,0:T(8,128)(2,1)S(1)}, bf16[8,512,256]{2,1,0:T(8,128)(2,1)S(1)}, f32[4,4,128]{2,1,0:T(4,128)S(1)}) custom-call(s32[1]{0:T(128)} %bitcast.me_ref, s32[1,2]{1,0:T(1,128)S(1)} %copy-done.6, bf16[128,256]{1,0:T(8,128)(2,1)S(1)} %collective-permute-done.3.refs_0_.refs_1_, ...), custom_call_target="tpu_custom_call" | custom-call | flops 268435456 | bytes 2097152 | tf_op jit(solution)/shard_map/pallas_call | solution.py:36
  22.6 2.8 %collective-permute-start.12 = (bf16[128,256]{1,0:T(8,128)(2,1)S(1)}, bf16[128,256]{1,0:T(8,128)(2,1)S(1)}, u32[]{:S(2)}, u32[]{:S(2)}) collective-permute-start(bf16[128,256]{1,0:T(8,128)(2,1)S(1)} %get-tuple-element.42), channel_id=1, source_target_pairs={{0,6},{1,7},{2,4},{3,5},{4,2},{5,3},{6,0},{7,1},{8,14},{9,15},{10,... | collective-permute-start | bytes 196616 | tf_op jit(solution)/shard_map/ppermute | solution.py:32
  25.4 1.7 %collective-permute-start.14 = (bf16[128,256]{1,0:T(8,128)(2,1)S(1)}, bf16[128,256]{1,0:T(8,128)(2,1)S(1)}, u32[]{:S(2)}, u32[]{:S(2)}) collective-permute-start(bf16[128,256]{1,0:T(8,128)(2,1)S(1)} %get-tuple-element.44), channel_id=1, source_target_pairs={{0,2},{1,3},{2,0},{3,1},{4,6},{5,7},{6,4},{7,5},{8,10},{9,11},{10,... | collective-permute-start | bytes 196616 | tf_op jit(solution)/shard_map/ppermute | solution.py:32
  27.1 2.8 %shard_map.101 = (bf16[4,272,128]{2,1,0:T(8,128)(2,1)S(1)}, bf16[8,512,256]{2,1,0:T(8,128)(2,1)S(1)}, f32[4,4,128]{2,1,0:T(4,128)S(1)}) custom-call(s32[1]{0:T(128)} %bitcast.me_ref, s32[1,2]{1,0:T(1,128)S(1)} %copy-done.6, bf16[128,256]{1,0:T(8,128)(2,1)S(1)} %bitcast.26, bf16[128,256]{1,0:T(8,128)(2,1)S(1)} %collective-permute-done.refs_1_.refs_2_, ...), custom_call_target="tpu_custom_call" | custom-call | flops 268435456 | bytes 2097152 | tf_op jit(solution)/shard_map/pallas_call | solution.py:36
  30.5 2.4 %collective-permute-start.8 = (bf16[272,128]{1,0:T(8,128)(2,1)S(1)}, bf16[272,128]{1,0:T(8,128)(2,1)S(1)}, u32[]{:S(2)}, u32[]{:S(2)}) collective-permute-start(bf16[272,128]{1,0:T(8,128)(2,1)S(1)} %get-tuple-element.36), channel_id=1, source_target_pairs={{0,6},{1,7},{2,4},{3,5},{4,2},{5,3},{6,0},{7,1},{8,14},{9,15},{10,... | collective-permute-start | bytes 208904 | tf_op jit(solution)/shard_map/ppermute | solution.py:32
  33.6 2.3 %collective-permute-start.34 = (bf16[128,256]{1,0:T(8,128)(2,1)S(1)}, bf16[128,256]{1,0:T(8,128)(2,1)S(1)}, u32[]{:S(2)}, u32[]{:S(2)}) collective-permute-start(bf16[128,256]{1,0:T(8,128)(2,1)S(1)} %shard_map.106.refs_4_), channel_id=1, source_target_pairs={{0,4},{1,5},{2,6},{3,7},{4,0},{5,1},{6,2},{7,3},{8,12},{9,13},{10,... | collective-permute-start | bytes 196616 | tf_op jit(solution)/shard_map/ppermute | solution.py:32
  36.0 1.4 %collective-permute-start.36 = (bf16[128,256]{1,0:T(8,128)(2,1)S(1)}, bf16[128,256]{1,0:T(8,128)(2,1)S(1)}, u32[]{:S(2)}, u32[]{:S(2)}) collective-permute-start(bf16[128,256]{1,0:T(8,128)(2,1)S(1)} %shard_map.106.refs_4_), channel_id=1, source_target_pairs={{0,6},{1,7},{2,4},{3,5},{4,2},{5,3},{6,0},{7,1},{8,14},{9,15},{10,... | collective-permute-start | bytes 196616 | tf_op jit(solution)/shard_map/ppermute | solution.py:32
  37.4 5.7 %collective-permute-done.9.refs_2_ = bf16[272,128]{1,0:T(8,128)(2,1)S(1)} collective-permute-done((bf16[272,128]{1,0:T(8,128)(2,1)S(1)}, bf16[272,128]{1,0:T(8,128)(2,1)S(1)}, u32[]{:S(2)}, u32[]{:S(2)}) %collective-permute-start.9) | collective-permute-done | bytes 69664 | tf_op jit(solution)/shard_map/ppermute | solution.py:32
  43.5 2.4 %collective-permute-start.20 = (bf16[144,256]{1,0:T(8,128)(2,1)S(1)}, bf16[144,256]{1,0:T(8,128)(2,1)S(1)}, u32[]{:S(2)}, u32[]{:S(2)}) collective-permute-start(bf16[144,256]{1,0:T(8,128)(2,1)S(1)} %shard_map.107.refs_0_.refs_8_), channel_id=1, source_target_pairs={{0,6},{1,7},{2,4},{3,5},{4,2},{5,3},{6,0},{7,1},{8,14},{9,15},{10,... | collective-permute-start | bytes 221192 | tf_op jit(solution)/shard_map/ppermute | solution.py:32
  46.4 2.3 %collective-permute-start.16 = (bf16[144,256]{1,0:T(8,128)(2,1)S(1)}, bf16[144,256]{1,0:T(8,128)(2,1)S(1)}, u32[]{:S(2)}, u32[]{:S(2)}) collective-permute-start(bf16[144,256]{1,0:T(8,128)(2,1)S(1)} %shard_map.107.refs_0_.refs_8_), channel_id=1, source_target_pairs={{0,2},{1,3},{2,0},{3,1},{4,6},{5,7},{6,4},{7,5},{8,10},{9,11},{10,... | collective-permute-start | bytes 221192 | tf_op jit(solution)/shard_map/ppermute | solution.py:32
  48.7 1.8 %collective-permute-done.18.refs_4_.refs_2_.refs_8_ = bf16[144,256]{1,0:T(8,128)(2,1)S(1)} collective-permute-done((bf16[144,256]{1,0:T(8,128)(2,1)S(1)}, bf16[144,256]{1,0:T(8,128)(2,1)S(1)}, u32[]{:S(2)}, u32[]{:S(2)}) %collective-permute-start.18) | collective-permute-done | bytes 73760 | tf_op jit(solution)/shard_map/ppermute | solution.py:32
  52.3 1.5 %collective-permute-start.25 = (bf16[4,128,256]{2,1,0:T(8,128)(2,1)S(1)}, bf16[4,128,256]{2,1,0:T(8,128)(2,1)S(1)}, u32[]{:S(2)}, u32[]{:S(2)}) collective-permute-start(bf16[4,128,256]{2,1,0:T(8,128)(2,1)S(1)} %shard_map.109.refs_4_), channel_id=1, source_target_pairs={{0,8},{8,0},{16,24},{24,16},{1,9},{9,1},{17,25},{25,17},{2,10},{10... | collective-permute-start | bytes 786440 | tf_op jit(solution)/shard_map/ppermute | solution.py:32
  53.8 1.5 %collective-permute-start.26 = (bf16[4,128,256]{2,1,0:T(8,128)(2,1)S(1)}, bf16[4,128,256]{2,1,0:T(8,128)(2,1)S(1)}, u32[]{:S(2)}, u32[]{:S(2)}) collective-permute-start(bf16[4,128,256]{2,1,0:T(8,128)(2,1)S(1)} %shard_map.109.refs_4_), channel_id=1, source_target_pairs={{0,16},{8,24},{16,0},{24,8},{1,17},{9,25},{17,1},{25,9},{2,18},{10... | collective-permute-start | bytes 786440 | tf_op jit(solution)/shard_map/ppermute | solution.py:32
  55.8 3.5 %shard_map.111 = (bf16[512,2048]{1,0:T(8,128)(2,1)}, bf16[512,2048]{1,0:T(8,128)(2,1)}, bf16[2,256,128]{2,1,0:T(8,128)(2,1)S(1)}, bf16[2,256,128]{2,1,0:T(8,128)(2,1)S(1)}) custom-call(s32[1]{0:T(128)} %bitcast.me_ref, bf16[128,256]{1,0:T(8,128)(2,1)S(1)} %collective-permute-done.1.refs_2_.refs_0_, ...), custom_call_target="tpu_custom_call" | custom-call | flops 536870912 | bytes 4194304 | tf_op jit(solution)/shard_map/pallas_call | solution.py:36
  59.9 3.5 %shard_map.112 = (bf16[512,2048]{1,0:T(8,128)(2,1)}, bf16[512,2048]{1,0:T(8,128)(2,1)}, bf16[2,256,128]{2,1,0:T(8,128)(2,1)S(1)}, bf16[2,256,128]{2,1,0:T(8,128)(2,1)S(1)}) custom-call(s32[1]{0:T(128)} %bitcast.me_ref, bf16[128,256]{1,0:T(8,128)(2,1)S(1)} %bitcast.27, ...), custom_call_target="tpu_custom_call", output_to_operand_aliasing={{0}: (19, {}), {1}: (20, {})} | custom-call | flops 536870912 | bytes 4194304 | tf_op jit(solution)/shard_map/pallas_call | solution.py:36
  63.6 1.5 %collective-permute-start.22 = (bf16[128,512]{1,0:T(8,128)(2,1)S(1)}, bf16[128,512]{1,0:T(8,128)(2,1)S(1)}, u32[]{:S(2)}, u32[]{:S(2)}) collective-permute-start(bf16[128,512]{1,0:T(8,128)(2,1)S(1)} %bitcast.18), channel_id=1, source_target_pairs={{0,8},{8,0},{16,24},{24,16},{1,9},{9,1},{17,25},{25,17},{2,10},{10... | collective-permute-start | bytes 393224 | tf_op jit(solution)/shard_map/ppermute | solution.py:32
  65.1 2.5 %collective-permute-start.40 = (bf16[256,128]{1,0:T(8,128)(2,1)S(1)}, bf16[256,128]{1,0:T(8,128)(2,1)S(1)}, u32[]{:S(2)}, u32[]{:S(2)}) collective-permute-start(bf16[256,128]{1,0:T(8,128)(2,1)S(1)} %get-tuple-element.56), channel_id=1, source_target_pairs={{0,6},{1,7},{2,4},{3,5},{4,2},{5,3},{6,0},{7,1},{8,14},{9,15},{10,... | collective-permute-start | bytes 196616 | tf_op jit(solution)/shard_map/ppermute | solution.py:32
  68.3 1.1 %collective-permute-done.22.refs_1_ = bf16[128,512]{1,0:T(8,128)(2,1)S(1)} collective-permute-done((bf16[128,512]{1,0:T(8,128)(2,1)S(1)}, bf16[128,512]{1,0:T(8,128)(2,1)S(1)}, u32[]{:S(2)}, u32[]{:S(2)}) %collective-permute-start.22) | collective-permute-done | bytes 131104 | tf_op jit(solution)/shard_map/ppermute | solution.py:32
  69.4 2.3 %collective-permute-start.41 = (bf16[256,128]{1,0:T(8,128)(2,1)S(1)}, bf16[256,128]{1,0:T(8,128)(2,1)S(1)}, u32[]{:S(2)}, u32[]{:S(2)}) collective-permute-start(bf16[256,128]{1,0:T(8,128)(2,1)S(1)} %get-tuple-element.57), channel_id=1, source_target_pairs={{0,4},{1,5},{2,6},{3,7},{4,0},{5,1},{6,2},{7,3},{8,12},{9,13},{10,... | collective-permute-start | bytes 196616 | tf_op jit(solution)/shard_map/ppermute | solution.py:32
  72.5 2.3 %collective-permute-done.41.refs_2_ = bf16[256,128]{1,0:T(8,128)(2,1)S(1)} collective-permute-done((bf16[256,128]{1,0:T(8,128)(2,1)S(1)}, bf16[256,128]{1,0:T(8,128)(2,1)S(1)}, u32[]{:S(2)}, u32[]{:S(2)}) %collective-permute-start.41) | collective-permute-done | bytes 65568 | tf_op jit(solution)/shard_map/ppermute | solution.py:32
  74.8 1.5 %collective-permute-start.23 = (bf16[128,512]{1,0:T(8,128)(2,1)S(1)}, bf16[128,512]{1,0:T(8,128)(2,1)S(1)}, u32[]{:S(2)}, u32[]{:S(2)}) collective-permute-start(bf16[128,512]{1,0:T(8,128)(2,1)S(1)} %bitcast.19), channel_id=1, source_target_pairs={{0,16},{8,24},{16,0},{24,8},{1,17},{9,25},{17,1},{25,9},{2,18},{10... | collective-permute-start | bytes 393224 | tf_op jit(solution)/shard_map/ppermute | solution.py:32
  76.3 2.1 %collective-permute-start.24 = (bf16[128,512]{1,0:T(8,128)(2,1)S(1)}, bf16[128,512]{1,0:T(8,128)(2,1)S(1)}, u32[]{:S(2)}, u32[]{:S(2)}) collective-permute-start(bf16[128,512]{1,0:T(8,128)(2,1)S(1)} %bitcast.20), channel_id=1, source_target_pairs={{0,24},{8,16},{16,8},{24,0},{1,25},{9,17},{17,9},{25,1},{2,26},{10... | collective-permute-start | bytes 393224 | tf_op jit(solution)/shard_map/ppermute | solution.py:32
  78.4 1.5 %shard_map.108 = bf16[128,512]{1,0:T(8,128)(2,1)} custom-call(s32[1]{0:T(128)} %bitcast.me_ref, bf16[144,256]{1,0:T(8,128)(2,1)S(1)} %shard_map.107.refs_0_.refs_8_, bf16[144,256]{1,0:T(8,128)(2,1)S(1)} %collective-permute-done.15.refs_1_.refs_11_.refs_9_, bf16[144,256]{1,0:T(8,128)(2,1)S(1)} %collective-permute-done.16.refs_2_.refs_1_.refs_10_, ...), custom_call_target="tpu_custom_call" | custom-call | tf_op jit(solution)/shard_map/pallas_call | solution.py:36
  80.6 1.9 %collective-permute-done.23.refs_2_ = bf16[128,512]{1,0:T(8,128)(2,1)S(1)} collective-permute-done((bf16[128,512]{1,0:T(8,128)(2,1)S(1)}, bf16[128,512]{1,0:T(8,128)(2,1)S(1)}, u32[]{:S(2)}, u32[]{:S(2)}) %collective-permute-start.23) | collective-permute-done | bytes 131104 | tf_op jit(solution)/shard_map/ppermute | solution.py:32
  82.6 2.6 %shard_map.110 = f32[512,2048]{1,0:T(8,128)} custom-call(s32[1]{0:T(128)} %bitcast.me_ref, bf16[128,512]{1,0:T(8,128)(2,1)S(1)} %bitcast.21, bf16[128,512]{1,0:T(8,128)(2,1)S(1)} %collective-permute-done.22.refs_1_, bf16[128,512]{1,0:T(8,128)(2,1)S(1)} %collective-permute-done.23.refs_2_, bf16[128,512]{1,0:T(8,128)(2,1)S(1)} %collective-permute-done.24.refs_3_, ...), custom_call_target="tpu_custom_call" | custom-call | tf_op jit(solution)/shard_map/pallas_call | solution.py:36
  (85 shorter events, 9.0 us)
Async XLA Ops:
  4.8 17.7 %collective-permute-start.11 = (bf16[4,128,256]{2,1,0:T(8,128)(2,1)}, bf16[4,128,256]{2,1,0:T(8,128)(2,1)S(1)}, u32[]{:S(2)}, u32[]{:S(2)}) collective-permute-start(bf16[4,128,256]{2,1,0:T(8,128)(2,1)} %get-tuple-element.40), channel_id=1, source_target_pairs={{0,1},{1,0},{2,3},{3,2},{4,5},{5,4},{6,7},{7,6},{8,9},{9,8},{10,11... | collective-permute-start | bytes 786440 | tf_op jit(solution)/shard_map/ppermute | solution.py:32
  5.4 5.3 %collective-permute-start = (bf16[128,256]{1,0:T(8,128)(2,1)S(1)}, bf16[128,256]{1,0:T(8,128)(2,1)S(1)}, u32[]{:S(2)}, u32[]{:S(2)}) collective-permute-start(bf16[128,256]{1,0:T(8,128)(2,1)S(1)} %bitcast.22), channel_id=1, source_target_pairs={{0,2},{1,3},{2,0},{3,1},{4,6},{5,7},{6,4},{7,5},{8,10},{9,11},{10,... | collective-permute-start | bytes 196616 | tf_op jit(solution)/shard_map/ppermute | solution.py:32
  8.1 7.7 %collective-permute-start.1 = (bf16[128,256]{1,0:T(8,128)(2,1)S(1)}, bf16[128,256]{1,0:T(8,128)(2,1)S(1)}, u32[]{:S(2)}, u32[]{:S(2)}) collective-permute-start(bf16[128,256]{1,0:T(8,128)(2,1)S(1)} %bitcast.23), channel_id=1, source_target_pairs={{0,4},{1,5},{2,6},{3,7},{4,0},{5,1},{6,2},{7,3},{8,12},{9,13},{10,... | collective-permute-start | bytes 196616 | tf_op jit(solution)/shard_map/ppermute | solution.py:32
  10.6 6.1 %collective-permute-start.2 = (bf16[128,256]{1,0:T(8,128)(2,1)S(1)}, bf16[128,256]{1,0:T(8,128)(2,1)S(1)}, u32[]{:S(2)}, u32[]{:S(2)}) collective-permute-start(bf16[128,256]{1,0:T(8,128)(2,1)S(1)} %bitcast.24), channel_id=1, source_target_pairs={{0,6},{1,7},{2,4},{3,5},{4,2},{5,3},{6,0},{7,1},{8,14},{9,15},{10,... | collective-permute-start | bytes 196616 | tf_op jit(solution)/shard_map/ppermute | solution.py:32
  10.6 6.1 %collective-permute-start.3 = (bf16[128,256]{1,0:T(8,128)(2,1)S(1)}, bf16[128,256]{1,0:T(8,128)(2,1)S(1)}, u32[]{:S(2)}, u32[]{:S(2)}) collective-permute-start(bf16[128,256]{1,0:T(8,128)(2,1)S(1)} %bitcast.25), channel_id=1, source_target_pairs={{0,1},{1,0},{2,3},{3,2},{4,5},{5,4},{6,7},{7,6},{8,9},{9,8},{10,11... | collective-permute-start | bytes 196616 | tf_op jit(solution)/shard_map/ppermute | solution.py:32
  10.7 6.0 %collective-permute-start.4 = (bf16[128,256]{1,0:T(8,128)(2,1)S(1)}, bf16[128,256]{1,0:T(8,128)(2,1)S(1)}, u32[]{:S(2)}, u32[]{:S(2)}) collective-permute-start(bf16[128,256]{1,0:T(8,128)(2,1)S(1)} %collective-permute-done.refs_1_.refs_2_), channel_id=1, source_target_pairs={{0,1},{1,0},{2,3},{3,2},{4,5},{5,4},{6,7},{7,6},{8,9},{9,8},{10,11... | collective-permute-start | bytes 196616 | tf_op jit(solution)/shard_map/ppermute | solution.py:32
  22.4 7.5 %collective-permute-start.7 = (bf16[4,272,128]{2,1,0:T(8,128)(2,1)S(1)}, bf16[4,272,128]{2,1,0:T(8,128)(2,1)S(1)}, u32[]{:S(2)}, u32[]{:S(2)}) collective-permute-start(bf16[4,272,128]{2,1,0:T(8,128)(2,1)S(1)} %get-tuple-element.34), channel_id=1, source_target_pairs={{0,1},{1,0},{2,3},{3,2},{4,5},{5,4},{6,7},{7,6},{8,9},{9,8},{10,11... | collective-permute-start | bytes 835592 | tf_op jit(solution)/shard_map/ppermute | solution.py:32
  22.6 10.3 %collective-permute-start.12 = (bf16[128,256]{1,0:T(8,128)(2,1)S(1)}, bf16[128,256]{1,0:T(8,128)(2,1)S(1)}, u32[]{:S(2)}, u32[]{:S(2)}) collective-permute-start(bf16[128,256]{1,0:T(8,128)(2,1)S(1)} %get-tuple-element.42), channel_id=1, source_target_pairs={{0,6},{1,7},{2,4},{3,5},{4,2},{5,3},{6,0},{7,1},{8,14},{9,15},{10,... | collective-permute-start | bytes 196616 | tf_op jit(solution)/shard_map/ppermute | solution.py:32
  25.4 8.2 %collective-permute-start.13 = (bf16[128,256]{1,0:T(8,128)(2,1)S(1)}, bf16[128,256]{1,0:T(8,128)(2,1)S(1)}, u32[]{:S(2)}, u32[]{:S(2)}) collective-permute-start(bf16[128,256]{1,0:T(8,128)(2,1)S(1)} %get-tuple-element.43), channel_id=1, source_target_pairs={{0,4},{1,5},{2,6},{3,7},{4,0},{5,1},{6,2},{7,3},{8,12},{9,13},{10,... | collective-permute-start | bytes 196616 | tf_op jit(solution)/shard_map/ppermute | solution.py:32
  25.4 8.2 %collective-permute-start.14 = (bf16[128,256]{1,0:T(8,128)(2,1)S(1)}, bf16[128,256]{1,0:T(8,128)(2,1)S(1)}, u32[]{:S(2)}, u32[]{:S(2)}) collective-permute-start(bf16[128,256]{1,0:T(8,128)(2,1)S(1)} %get-tuple-element.44), channel_id=1, source_target_pairs={{0,2},{1,3},{2,0},{3,1},{4,6},{5,7},{6,4},{7,5},{8,10},{9,11},{10,... | collective-permute-start | bytes 196616 | tf_op jit(solution)/shard_map/ppermute | solution.py:32
  30.0 7.3 %collective-permute-start.10 = (bf16[272,128]{1,0:T(8,128)(2,1)S(1)}, bf16[272,128]{1,0:T(8,128)(2,1)S(1)}, u32[]{:S(2)}, u32[]{:S(2)}) collective-permute-start(bf16[272,128]{1,0:T(8,128)(2,1)S(1)} %get-tuple-element.38), channel_id=1, source_target_pairs={{0,2},{1,3},{2,0},{3,1},{4,6},{5,7},{6,4},{7,5},{8,10},{9,11},{10,... | collective-permute-start | bytes 208904 | tf_op jit(solution)/shard_map/ppermute | solution.py:32
  30.5 7.0 %collective-permute-start.8 = (bf16[272,128]{1,0:T(8,128)(2,1)S(1)}, bf16[272,128]{1,0:T(8,128)(2,1)S(1)}, u32[]{:S(2)}, u32[]{:S(2)}) collective-permute-start(bf16[272,128]{1,0:T(8,128)(2,1)S(1)} %get-tuple-element.36), channel_id=1, source_target_pairs={{0,6},{1,7},{2,4},{3,5},{4,2},{5,3},{6,0},{7,1},{8,14},{9,15},{10,... | collective-permute-start | bytes 208904 | tf_op jit(solution)/shard_map/ppermute | solution.py:32
  32.9 10.3 %collective-permute-start.9 = (bf16[272,128]{1,0:T(8,128)(2,1)S(1)}, bf16[272,128]{1,0:T(8,128)(2,1)S(1)}, u32[]{:S(2)}, u32[]{:S(2)}) collective-permute-start(bf16[272,128]{1,0:T(8,128)(2,1)S(1)} %get-tuple-element.37), channel_id=1, source_target_pairs={{0,4},{1,5},{2,6},{3,7},{4,0},{5,1},{6,2},{7,3},{8,12},{9,13},{10,... | collective-permute-start | bytes 208904 | tf_op jit(solution)/shard_map/ppermute | solution.py:32
  33.6 12.3 %collective-permute-start.34 = (bf16[128,256]{1,0:T(8,128)(2,1)S(1)}, bf16[128,256]{1,0:T(8,128)(2,1)S(1)}, u32[]{:S(2)}, u32[]{:S(2)}) collective-permute-start(bf16[128,256]{1,0:T(8,128)(2,1)S(1)} %shard_map.106.refs_4_), channel_id=1, source_target_pairs={{0,4},{1,5},{2,6},{3,7},{4,0},{5,1},{6,2},{7,3},{8,12},{9,13},{10,... | collective-permute-start | bytes 196616 | tf_op jit(solution)/shard_map/ppermute | solution.py:32
  36.0 9.9 %collective-permute-start.36 = (bf16[128,256]{1,0:T(8,128)(2,1)S(1)}, bf16[128,256]{1,0:T(8,128)(2,1)S(1)}, u32[]{:S(2)}, u32[]{:S(2)}) collective-permute-start(bf16[128,256]{1,0:T(8,128)(2,1)S(1)} %shard_map.106.refs_4_), channel_id=1, source_target_pairs={{0,6},{1,7},{2,4},{3,5},{4,2},{5,3},{6,0},{7,1},{8,14},{9,15},{10,... | collective-permute-start | bytes 196616 | tf_op jit(solution)/shard_map/ppermute | solution.py:32
  37.3 9.1 %collective-permute-start.32 = (bf16[128,256]{1,0:T(8,128)(2,1)S(1)}, bf16[128,256]{1,0:T(8,128)(2,1)S(1)}, u32[]{:S(2)}, u32[]{:S(2)}) collective-permute-start(bf16[128,256]{1,0:T(8,128)(2,1)S(1)} %shard_map.106.refs_4_), channel_id=1, source_target_pairs={{0,2},{1,3},{2,0},{3,1},{4,6},{5,7},{6,4},{7,5},{8,10},{9,11},{10,... | collective-permute-start | bytes 196616 | tf_op jit(solution)/shard_map/ppermute | solution.py:32
  43.4 7.1 %collective-permute-start.18 = (bf16[144,256]{1,0:T(8,128)(2,1)S(1)}, bf16[144,256]{1,0:T(8,128)(2,1)S(1)}, u32[]{:S(2)}, u32[]{:S(2)}) collective-permute-start(bf16[144,256]{1,0:T(8,128)(2,1)S(1)} %shard_map.107.refs_0_.refs_8_), channel_id=1, source_target_pairs={{0,4},{1,5},{2,6},{3,7},{4,0},{5,1},{6,2},{7,3},{8,12},{9,13},{10,... | collective-permute-start | bytes 221192 | tf_op jit(solution)/shard_map/ppermute | solution.py:32
  43.5 7.1 %collective-permute-start.20 = (bf16[144,256]{1,0:T(8,128)(2,1)S(1)}, bf16[144,256]{1,0:T(8,128)(2,1)S(1)}, u32[]{:S(2)}, u32[]{:S(2)}) collective-permute-start(bf16[144,256]{1,0:T(8,128)(2,1)S(1)} %shard_map.107.refs_0_.refs_8_), channel_id=1, source_target_pairs={{0,6},{1,7},{2,4},{3,5},{4,2},{5,3},{6,0},{7,1},{8,14},{9,15},{10,... | collective-permute-start | bytes 221192 | tf_op jit(solution)/shard_map/ppermute | solution.py:32
  46.4 5.5 %collective-permute-start.16 = (bf16[144,256]{1,0:T(8,128)(2,1)S(1)}, bf16[144,256]{1,0:T(8,128)(2,1)S(1)}, u32[]{:S(2)}, u32[]{:S(2)}) collective-permute-start(bf16[144,256]{1,0:T(8,128)(2,1)S(1)} %shard_map.107.refs_0_.refs_8_), channel_id=1, source_target_pairs={{0,2},{1,3},{2,0},{3,1},{4,6},{5,7},{6,4},{7,5},{8,10},{9,11},{10,... | collective-permute-start | bytes 221192 | tf_op jit(solution)/shard_map/ppermute | solution.py:32
  50.6 5.3 %collective-permute-start.21 = (bf16[144,256]{1,0:T(8,128)(2,1)S(1)}, bf16[144,256]{1,0:T(8,128)(2,1)S(1)}, u32[]{:S(2)}, u32[]{:S(2)}) collective-permute-start(bf16[144,256]{1,0:T(8,128)(2,1)S(1)} %collective-permute-done.20.refs_6_.refs_3_.refs_10_), channel_id=1, source_target_pairs={{0,1},{1,0},{2,3},{3,2},{4,5},{5,4},{6,7},{7,6},{8,9},{9,8},{10,11... | collective-permute-start | bytes 221192 | tf_op jit(solution)/shard_map/ppermute | solution.py:32
  51.9 7.4 %collective-permute-start.15 = (bf16[144,256]{1,0:T(8,128)(2,1)S(1)}, bf16[144,256]{1,0:T(8,128)(2,1)S(1)}, u32[]{:S(2)}, u32[]{:S(2)}) collective-permute-start(bf16[144,256]{1,0:T(8,128)(2,1)S(1)} %shard_map.107.refs_0_.refs_8_), channel_id=1, source_target_pairs={{0,1},{1,0},{2,3},{3,2},{4,5},{5,4},{6,7},{7,6},{8,9},{9,8},{10,11... | collective-permute-start | bytes 221192 | tf_op jit(solution)/shard_map/ppermute | solution.py:32
  52.3 15.4 %collective-permute-start.25 = (bf16[4,128,256]{2,1,0:T(8,128)(2,1)S(1)}, bf16[4,128,256]{2,1,0:T(8,128)(2,1)S(1)}, u32[]{:S(2)}, u32[]{:S(2)}) collective-permute-start(bf16[4,128,256]{2,1,0:T(8,128)(2,1)S(1)} %shard_map.109.refs_4_), channel_id=1, source_target_pairs={{0,8},{8,0},{16,24},{24,16},{1,9},{9,1},{17,25},{25,17},{2,10},{10... | collective-permute-start | bytes 786440 | tf_op jit(solution)/shard_map/ppermute | solution.py:32
  53.8 13.9 %collective-permute-start.26 = (bf16[4,128,256]{2,1,0:T(8,128)(2,1)S(1)}, bf16[4,128,256]{2,1,0:T(8,128)(2,1)S(1)}, u32[]{:S(2)}, u32[]{:S(2)}) collective-permute-start(bf16[4,128,256]{2,1,0:T(8,128)(2,1)S(1)} %shard_map.109.refs_4_), channel_id=1, source_target_pairs={{0,16},{8,24},{16,0},{24,8},{1,17},{9,25},{17,1},{25,9},{2,18},{10... | collective-permute-start | bytes 786440 | tf_op jit(solution)/shard_map/ppermute | solution.py:32
  55.3 12.9 %collective-permute-start.27 = (bf16[4,128,256]{2,1,0:T(8,128)(2,1)S(1)}, bf16[4,128,256]{2,1,0:T(8,128)(2,1)S(1)}, u32[]{:S(2)}, u32[]{:S(2)}) collective-permute-start(bf16[4,128,256]{2,1,0:T(8,128)(2,1)S(1)} %shard_map.109.refs_4_), channel_id=1, source_target_pairs={{0,24},{8,16},{16,8},{24,0},{1,25},{9,17},{17,9},{25,1},{2,26},{10... | collective-permute-start | bytes 786440 | tf_op jit(solution)/shard_map/ppermute | solution.py:32
  63.6 5.9 %collective-permute-start.22 = (bf16[128,512]{1,0:T(8,128)(2,1)S(1)}, bf16[128,512]{1,0:T(8,128)(2,1)S(1)}, u32[]{:S(2)}, u32[]{:S(2)}) collective-permute-start(bf16[128,512]{1,0:T(8,128)(2,1)S(1)} %bitcast.18), channel_id=1, source_target_pairs={{0,8},{8,0},{16,24},{24,16},{1,9},{9,1},{17,25},{25,17},{2,10},{10... | collective-permute-start | bytes 393224 | tf_op jit(solution)/shard_map/ppermute | solution.py:32
  65.1 6.6 %collective-permute-start.40 = (bf16[256,128]{1,0:T(8,128)(2,1)S(1)}, bf16[256,128]{1,0:T(8,128)(2,1)S(1)}, u32[]{:S(2)}, u32[]{:S(2)}) collective-permute-start(bf16[256,128]{1,0:T(8,128)(2,1)S(1)} %get-tuple-element.56), channel_id=1, source_target_pairs={{0,6},{1,7},{2,4},{3,5},{4,2},{5,3},{6,0},{7,1},{8,14},{9,15},{10,... | collective-permute-start | bytes 196616 | tf_op jit(solution)/shard_map/ppermute | solution.py:32
  67.7 14.9 %collective-permute-start.28 = (bf16[4,128,256]{2,1,0:T(8,128)(2,1)S(1)}, bf16[4,128,256]{2,1,0:T(8,128)(2,1)S(1)}, u32[]{:S(2)}, u32[]{:S(2)}) collective-permute-start(bf16[4,128,256]{2,1,0:T(8,128)(2,1)S(1)} %collective-permute-done.25.refs_5_), channel_id=1, source_target_pairs={{0,1},{1,0},{2,3},{3,2},{4,5},{5,4},{6,7},{7,6},{8,9},{9,8},{10,11... | collective-permute-start | bytes 786440 | tf_op jit(solution)/shard_map/ppermute | solution.py:32
  67.7 14.9 %collective-permute-start.29 = (bf16[4,128,256]{2,1,0:T(8,128)(2,1)S(1)}, bf16[4,128,256]{2,1,0:T(8,128)(2,1)S(1)}, u32[]{:S(2)}, u32[]{:S(2)}) collective-permute-start(bf16[4,128,256]{2,1,0:T(8,128)(2,1)S(1)} %collective-permute-done.26.refs_6_), channel_id=1, source_target_pairs={{0,1},{1,0},{2,3},{3,2},{4,5},{5,4},{6,7},{7,6},{8,9},{9,8},{10,11... | collective-permute-start | bytes 786440 | tf_op jit(solution)/shard_map/ppermute | solution.py:32
  68.2 14.4 %collective-permute-start.30 = (bf16[4,128,256]{2,1,0:T(8,128)(2,1)S(1)}, bf16[4,128,256]{2,1,0:T(8,128)(2,1)S(1)}, u32[]{:S(2)}, u32[]{:S(2)}) collective-permute-start(bf16[4,128,256]{2,1,0:T(8,128)(2,1)S(1)} %collective-permute-done.27.refs_7_), channel_id=1, source_target_pairs={{0,1},{1,0},{2,3},{3,2},{4,5},{5,4},{6,7},{7,6},{8,9},{9,8},{10,11... | collective-permute-start | bytes 786440 | tf_op jit(solution)/shard_map/ppermute | solution.py:32
  69.4 5.4 %collective-permute-start.41 = (bf16[256,128]{1,0:T(8,128)(2,1)S(1)}, bf16[256,128]{1,0:T(8,128)(2,1)S(1)}, u32[]{:S(2)}, u32[]{:S(2)}) collective-permute-start(bf16[256,128]{1,0:T(8,128)(2,1)S(1)} %get-tuple-element.57), channel_id=1, source_target_pairs={{0,4},{1,5},{2,6},{3,7},{4,0},{5,1},{6,2},{7,3},{8,12},{9,13},{10,... | collective-permute-start | bytes 196616 | tf_op jit(solution)/shard_map/ppermute | solution.py:32
  74.8 7.8 %collective-permute-start.23 = (bf16[128,512]{1,0:T(8,128)(2,1)S(1)}, bf16[128,512]{1,0:T(8,128)(2,1)S(1)}, u32[]{:S(2)}, u32[]{:S(2)}) collective-permute-start(bf16[128,512]{1,0:T(8,128)(2,1)S(1)} %bitcast.19), channel_id=1, source_target_pairs={{0,16},{8,24},{16,0},{24,8},{1,17},{9,25},{17,1},{25,9},{2,18},{10... | collective-permute-start | bytes 393224 | tf_op jit(solution)/shard_map/ppermute | solution.py:32
  76.3 6.2 %collective-permute-start.24 = (bf16[128,512]{1,0:T(8,128)(2,1)S(1)}, bf16[128,512]{1,0:T(8,128)(2,1)S(1)}, u32[]{:S(2)}, u32[]{:S(2)}) collective-permute-start(bf16[128,512]{1,0:T(8,128)(2,1)S(1)} %bitcast.20), channel_id=1, source_target_pairs={{0,24},{8,16},{16,8},{24,0},{1,25},{9,17},{17,9},{25,1},{2,26},{10... | collective-permute-start | bytes 393224 | tf_op jit(solution)/shard_map/ppermute | solution.py:32
  (19 other events, 106.9 us)

commit v5 on v4

--- a/solution.py
+++ b/solution.py
@@ -12,8 +12,7 @@
 MASKED = -1e30
 EXTRA = 16
 MIB = 1 << 20
-GRAD_VMEM = 55
-ADD_COST = 20
+GRAD_VMEM = 49
 
 NT = (((1,), (1,)), ((), ()))
 NN = (((1,), (0,)), ((), ()))
@@ -96,26 +95,20 @@
     return ref.at[:, pl.ds(pl.multiple_of(owner * width, width), width)]
 
 
-def pair_of(ref, me, slot, width, pair):
-    at = jnp.bitwise_xor(me, slot) * width + pair * PAIR
-    return ref.at[:, pl.ds(pl.multiple_of(at, PAIR), PAIR)]
-
-
-def forward_kernel(parity, passages, me_ref, lengths_ref, *refs):
+def forward_kernel(parity, passages, lengths_ref, *refs):
     out_ref, weights_ref, tops_ref, q_buf, s_buf, bias_ref = refs[-6:]
     keys_ref, values_ref = refs[-8:-6]
-    me = me_ref[0]
     count, _, width = q_buf.shape
     pairs = width // PAIR
     for k in range(count):
         q_buf[k] = refs[k][...]
-    bias_ref[...] = mask_bias(lengths_ref, passages, keys_ref.shape[0] // passages)
+    bias_ref[...] = mask_bias(lengths_ref, passages, keys_ref.shape[1] // passages)
     lane_low = lax.broadcasted_iota(jnp.int32, (1, PAIR), 1) < HEAD_SIZE
 
     def score(k, p):
         queries = block_stack(q_buf[k, :, p * PAIR : (p + 1) * PAIR], lane_low)
         bias = bias_ref[...]
-        keys = pair_of(keys_ref, me, 2 * k + parity, width, p)[...]
+        keys = keys_ref[2 * k + parity, :, p * PAIR : (p + 1) * PAIR]
         scores = dot(keys, queries, NT) + jnp.concatenate([bias, bias], axis=1)
         s_buf[p] = scores
         return jnp.max(scores, axis=0, keepdims=True)
@@ -125,7 +118,7 @@
         total = jnp.sum(weights, axis=0, keepdims=True)
         rounded = weights.astype(jnp.bfloat16)
         weights_ref[k * pairs + p] = rounded
-        values = pair_of(values_ref, me, 2 * k + parity, width, p)[...]
+        values = values_ref[2 * k + parity, :, p * PAIR : (p + 1) * PAIR]
         mixed = dot(values, rounded, TN) / total
         out_ref[k, p * PAIR : (p + 1) * PAIR, :] = diagonal(mixed).astype(jnp.bfloat16)
         return top + jnp.log(total)
@@ -226,7 +219,7 @@
         return block_stack(g_buf[i, :, p * PAIR : (p + 1) * PAIR], lane_low)
 
     def prob_grad(i, p):
-        p_buf[p] = dot(pair_of(values_ref, me, first + i, width, p)[...], grads_of(i, p), NT)
+        p_buf[p] = dot(values_ref[first + i, :, p * PAIR : (p + 1) * PAIR], grads_of(i, p), NT)
 
     def row_pair(rows, at):
         return jnp.concatenate([rows[at : at + 1], rows[at + 1 : at + 2]], axis=1)
@@ -240,7 +233,7 @@
         score_grad = (probs * (p_buf[p] - row_pair(stats, heads + 2 * p))).astype(jnp.bfloat16)
         dv_buf[i, :, lanes] = dot(probs.astype(jnp.bfloat16), grads_of(i, p), NN).astype(jnp.bfloat16)
         dk_buf[i, :, lanes] = dot(score_grad, queries, NN).astype(jnp.bfloat16)
-        out_ref[k, lanes, :] = diagonal(dot(pair_of(keys_ref, me, first + i, width, p)[...], score_grad, TN)).astype(
+        out_ref[k, lanes, :] = diagonal(dot(keys_ref[first + i, :, lanes], score_grad, TN)).astype(
             jnp.bfloat16
         )
 
@@ -287,23 +280,30 @@
     refs[-1][...] = total.T.astype(jnp.bfloat16)
 
 
-def grad_partial_kernel(size, me_ref, cot_ref, weight_ref, even_ref, odd_ref, cot_buf, w_buf, sem, cot_sem):
+def grad_partial_kernel(size, me_ref, cot_ref, weight_ref, keys_ref, values_ref, *refs):
+    even_ref, odd_ref, k_out, v_out, cot_buf, w_buf, sem, cot_sem = refs
     me = me_ref[0]
     width = w_buf.shape[2]
 
-    def copy(s):
-        return pltpu.make_async_copy(columns_of(weight_ref, me, s, width), w_buf.at[s], sem.at[s])
-
+    def copy(ref, buf, lane, s):
+        return pltpu.make_async_copy(columns_of(ref, me, s, width), buf.at[s], sem.at[lane, s])
+
+    order = list(range(1, size, 2)) + list(range(0, size, 2))
     cot_copy = pltpu.make_async_copy(cot_ref, cot_buf, cot_sem)
     cot_copy.start()
-    order = list(range(1, size, 2)) + list(range(0, size, 2))
     for s in order:
-        copy(s).start()
+        copy(weight_ref, w_buf, 0, s).start()
+    for s in range(size):
+        copy(keys_ref, k_out, 1, s).start()
+        copy(values_ref, v_out, 2, s).start()
     cot_copy.wait()
     cot = cot_buf[...]
     for s in order:
-        copy(s).wait()
+        copy(weight_ref, w_buf, 0, s).wait()
         (odd_ref if s % 2 else even_ref)[s // 2] = dot(cot, w_buf[s], NN).astype(jnp.bfloat16)
+    for s in range(size):
+        copy(keys_ref, k_out, 1, s).wait()
+        copy(values_ref, v_out, 2, s).wait()
 
 
 def layer_out_kernel(size, me_ref, *refs):
@@ -376,34 +376,28 @@
     q_even = spread(query, size)
     slots = interleaved(q_even, across(q_even, size))
 
-    g_even, g_odd = call(
+    resident = shaped((size, key_count, width), bf16)
+    g_even, g_odd, slot_keys, slot_values = call(
         functools.partial(grad_partial_kernel, size),
         me,
         cot,
         out_weight,
-        out=[shaped((half, answers, width), bf16)] * 2,
-        ins=[SMEM, HBM, HBM],
-        outs=[VMEM] * 2,
+        key_rows,
+        value_rows,
+        out=[shaped((half, answers, width), bf16)] * 2 + [resident] * 2,
+        ins=[SMEM] + [HBM] * 4,
+        outs=[VMEM] * 4,
         scratch=[
             pltpu.VMEM((answers, model), bf16),
             pltpu.VMEM((size, model, width), bf16),
-            pltpu.SemaphoreType.DMA((size,)),
+            pltpu.SemaphoreType.DMA((3, size)),
             pltpu.SemaphoreType.DMA(()),
         ],
         vmem=GRAD_VMEM,
-        cost=cost(answers * model * inner, 0, 2 * model * inner),
     )
     g_other = swap(g_odd, "psg", size, 1)
     block = shaped((answers, width), bf16)
-    g_sums = call(
-        add_pair_kernel,
-        g_even,
-        g_other,
-        out=[block] * half,
-        ins=[VMEM] * 2,
-        outs=[VMEM] * half,
-        cost=cost(ADD_COST * answers * model * inner, 0, 2 * model * inner),
-    )
+    g_sums = call(add_pair_kernel, g_even, g_other, out=[block] * half, ins=[VMEM] * 2, outs=[VMEM] * half)
     g_parts = [swap(g_sums[d // 2], "psg", size, d) for d in far_first(size)]
 
     packed = shaped((width + EXTRA, answers), bf16)
@@ -412,17 +406,16 @@
     def forward(parity):
         return call(
             functools.partial(forward_kernel, parity, passages),
-            me,
             lengths,
             *slots[parity::2],
-            key_rows,
-            value_rows,
+            slot_keys,
+            slot_values,
             out=[
                 shaped((half, width + EXTRA, answers), bf16),
                 shaped((half * pairs, key_count, 2 * answers), bf16),
                 shaped((half, heads, answers), f32),
             ],
-            ins=[SMEM, SMEM] + [VMEM] * (half + 2),
+            ins=[SMEM] + [VMEM] * (half + 2),
             outs=[VMEM] * 3,
             scratch=[
                 pltpu.VMEM((half, answers, width), bf16),
@@ -465,8 +458,8 @@
             *slots[pick],
             *g_slots[pick],
             *c_slots[pick],
-            key_rows,
-            value_rows,
+            slot_keys,
+            slot_values,
             kept_even[0],
             kept_odd[0],
             kept_even[1],

time: 85.3 us -> 83.1 us (0.974)
  starting transfers between devices: 40 us -> 38 us
  waiting for transfers between devices: 20.6 us -> 22.1 us
  Pallas kernels: 22.1 us -> 21 us
    ppermute x43, starting transfers between devices: 40 us -> 38 us  [swap(): return lax.ppermute(x, axis, [(j, j ^ distance) for j in range(size)])]
    ppermute x43, waiting for transfers between devices: 20.6 us -> 22.1 us  [swap(): return lax.ppermute(x, axis, [(j, j ^ distance) for j in range(size)])]
    pallas_call x15, Pallas kernels: 22.1 us -> 21 us  [call(): pl.pallas_call(kernel, out_shape=out, in_specs=ins, out_specs=outs, scrat...]
  transfers between devices with their start and end apart: 43 -> 43, of which waited for: 13 -> 13; matrix products, arithmetic and copies ran while one was open for 0% -> 0% of each run, Pallas kernels for 18% -> 22%
where the time goes in v5:
time: 83.1 us; the launch traced here: 82.9 us
  starting transfers between devices  38 us (46%)
  waiting for transfers between devices  22.1 us (27%)
  Pallas kernels  21 us (25%)
  local copies, waits for them, and re-layouts  0.92 us (1%)
    ppermute x43, starting transfers between devices, swap(): return lax.ppermute(x, axis, [(j, j ^ distance) for j in range(size)])  38 us
    ppermute x43, waiting for transfers between devices, swap(): return lax.ppermute(x, axis, [(j, j ^ distance) for j in range(size)])  22.1 us
    pallas_call x15, Pallas kernels, call(): pl.pallas_call(kernel, out_shape=out, in_specs=ins, out_specs=outs, scrat...  21 us
  transfers between devices with their start and end apart: 43, of which 13 were waited for; matrix products, arithmetic and copies ran while one was open for 0% of the time, Pallas kernels for 22%

profile of v5, /device:TPU:0, one launch (start us, length us, event | category | flops | bytes accessed | tf_op | source)
XLA Modules:
  0.0 82.9 jit_solution(18095191257931665817)
XLA Ops:
  0.6 3.1 %collective-permute-start = (bf16[128,256]{1,0:T(8,128)(2,1)}, bf16[128,256]{1,0:T(8,128)(2,1)S(1)}, u32[]{:S(2)}, u32[]{:S(2)}) collective-permute-start(bf16[128,256]{1,0:T(8,128)(2,1)} %bitcast.14), channel_id=1, source_target_pairs={{0,2},{1,3},{2,0},{3,1},{4,6},{5,7},{6,4},{7,5},{8,10},{9,11},{10,... | collective-permute-start | bytes 196616 | tf_op jit(solution)/shard_map/ppermute | solution.py:31
  3.8 2.6 %collective-permute-start.1 = (bf16[128,256]{1,0:T(8,128)(2,1)}, bf16[128,256]{1,0:T(8,128)(2,1)S(1)}, u32[]{:S(2)}, u32[]{:S(2)}) collective-permute-start(bf16[128,256]{1,0:T(8,128)(2,1)} %bitcast.15), channel_id=1, source_target_pairs={{0,4},{1,5},{2,6},{3,7},{4,0},{5,1},{6,2},{7,3},{8,12},{9,13},{10,... | collective-permute-start | bytes 196616 | tf_op jit(solution)/shard_map/ppermute | solution.py:31
  6.9 4.4 %collective-permute-done.1.refs_2_.refs_0_ = bf16[128,256]{1,0:T(8,128)(2,1)S(1)} collective-permute-done((bf16[128,256]{1,0:T(8,128)(2,1)}, bf16[128,256]{1,0:T(8,128)(2,1)S(1)}, u32[]{:S(2)}, u32[]{:S(2)}) %collective-permute-start.1) | collective-permute-done | bytes 65568 | tf_op jit(solution)/shard_map/ppermute | solution.py:31
  11.2 1.4 %collective-permute-done.2.refs_3_.refs_2_ = bf16[128,256]{1,0:T(8,128)(2,1)S(1)} collective-permute-done((bf16[128,256]{1,0:T(8,128)(2,1)}, bf16[128,256]{1,0:T(8,128)(2,1)S(1)}, u32[]{:S(2)}, u32[]{:S(2)}) %collective-permute-start.2) | collective-permute-done | bytes 65568 | tf_op jit(solution)/shard_map/ppermute | solution.py:31
  12.6 0.9 %copy-done.1 = bf16[1,128,512]{2,1,0:T(8,128)(2,1)S(1)} copy-done((bf16[1,128,512]{2,1,0:T(8,128)(2,1)S(1)}, bf16[1,128,512]{2,1,0:T(8,128)(2,1)}, u32[]{:S(2)}) %copy-start.1) | copy-done | bytes 131096
  13.6 3.2 %shard_map.101 = (bf16[4,128,256]{2,1,0:T(8,128)(2,1)S(1)}, bf16[4,128,256]{2,1,0:T(8,128)(2,1)S(1)}, bf16[8,512,256]{2,1,0:T(8,128)(2,1)S(1)}, bf16[8,512,256]{2,1,0:T(8,128)(2,1)S(1)}) custom-call(s32[1]{0:T(128)} %bitcast.me_ref, bf16[128,512]{1,0:T(8,128)(2,1)S(1)} %bitcast.9, bf16[512,2048]{1,0:T(8,128)(2,1)} %refs_8_.1, bf16[512,2048]{1,0:T(8,128)(2,1)} %bitcast.20, ...), custom_call_target="tpu_custom_call" | custom-call | tf_op jit(solution)/shard_map/pallas_call | solution.py:35
  17.4 2.7 %shard_map.103 = (bf16[4,272,128]{2,1,0:T(8,128)(2,1)S(1)}, bf16[8,512,256]{2,1,0:T(8,128)(2,1)S(1)}, f32[4,4,128]{2,1,0:T(4,128)S(1)}) custom-call(s32[1,2]{1,0:T(1,128)S(1)} %copy-done.3, bf16[128,256]{1,0:T(8,128)(2,1)S(1)} %collective-permute-done.3.refs_0_.refs_1_, bf16[128,256]{1,0:T(8,128)(2,1)S(1)} %collective-permute-done.4.refs_1_.refs_3_, ...), custom_call_target="tpu_custom_call" | custom-call | flops 268435456 | bytes 2097152 | tf_op jit(solution)/shard_map/pallas_call | solution.py:35
  20.3 2.3 %collective-permute-start.12 = (bf16[128,256]{1,0:T(8,128)(2,1)S(1)}, bf16[128,256]{1,0:T(8,128)(2,1)S(1)}, u32[]{:S(2)}, u32[]{:S(2)}) collective-permute-start(bf16[128,256]{1,0:T(8,128)(2,1)S(1)} %get-tuple-element.46), channel_id=1, source_target_pairs={{0,6},{1,7},{2,4},{3,5},{4,2},{5,3},{6,0},{7,1},{8,14},{9,15},{10,... | collective-permute-start | bytes 196616 | tf_op jit(solution)/shard_map/ppermute | solution.py:31
  22.6 2.1 %collective-permute-start.14 = (bf16[128,256]{1,0:T(8,128)(2,1)S(1)}, bf16[128,256]{1,0:T(8,128)(2,1)S(1)}, u32[]{:S(2)}, u32[]{:S(2)}) collective-permute-start(bf16[128,256]{1,0:T(8,128)(2,1)S(1)} %get-tuple-element.48), channel_id=1, source_target_pairs={{0,2},{1,3},{2,0},{3,1},{4,6},{5,7},{6,4},{7,5},{8,10},{9,11},{10,... | collective-permute-start | bytes 196616 | tf_op jit(solution)/shard_map/ppermute | solution.py:31
  24.8 2.7 %shard_map.102 = (bf16[4,272,128]{2,1,0:T(8,128)(2,1)S(1)}, bf16[8,512,256]{2,1,0:T(8,128)(2,1)S(1)}, f32[4,4,128]{2,1,0:T(4,128)S(1)}) custom-call(s32[1,2]{1,0:T(1,128)S(1)} %copy-done.3, bf16[128,256]{1,0:T(8,128)(2,1)S(1)} %bitcast.18, bf16[128,256]{1,0:T(8,128)(2,1)S(1)} %collective-permute-done.refs_1_.refs_2_, ...), custom_call_target="tpu_custom_call" | custom-call | flops 268435456 | bytes 2097152 | tf_op jit(solution)/shard_map/pallas_call | solution.py:35
  27.8 2.3 %collective-permute-start.8 = (bf16[272,128]{1,0:T(8,128)(2,1)S(1)}, bf16[272,128]{1,0:T(8,128)(2,1)S(1)}, u32[]{:S(2)}, u32[]{:S(2)}) collective-permute-start(bf16[272,128]{1,0:T(8,128)(2,1)S(1)} %get-tuple-element.40), channel_id=1, source_target_pairs={{0,6},{1,7},{2,4},{3,5},{4,2},{5,3},{6,0},{7,1},{8,14},{9,15},{10,... | collective-permute-start | bytes 208904 | tf_op jit(solution)/shard_map/ppermute | solution.py:31
  30.1 1.2 %collective-permute-start.9 = (bf16[272,128]{1,0:T(8,128)(2,1)S(1)}, bf16[272,128]{1,0:T(8,128)(2,1)S(1)}, u32[]{:S(2)}, u32[]{:S(2)}) collective-permute-start(bf16[272,128]{1,0:T(8,128)(2,1)S(1)} %get-tuple-element.41), channel_id=1, source_target_pairs={{0,4},{1,5},{2,6},{3,7},{4,0},{5,1},{6,2},{7,3},{8,12},{9,13},{10,... | collective-permute-start | bytes 208904 | tf_op jit(solution)/shard_map/ppermute | solution.py:31
  31.3 1.8 %collective-permute-start.34 = (bf16[128,256]{1,0:T(8,128)(2,1)S(1)}, bf16[128,256]{1,0:T(8,128)(2,1)S(1)}, u32[]{:S(2)}, u32[]{:S(2)}) collective-permute-start(bf16[128,256]{1,0:T(8,128)(2,1)S(1)} %shard_map.106.refs_4_), channel_id=1, source_target_pairs={{0,4},{1,5},{2,6},{3,7},{4,0},{5,1},{6,2},{7,3},{8,12},{9,13},{10,... | collective-permute-start | bytes 196616 | tf_op jit(solution)/shard_map/ppermute | solution.py:31
  33.1 1.6 %collective-permute-start.36 = (bf16[128,256]{1,0:T(8,128)(2,1)S(1)}, bf16[128,256]{1,0:T(8,128)(2,1)S(1)}, u32[]{:S(2)}, u32[]{:S(2)}) collective-permute-start(bf16[128,256]{1,0:T(8,128)(2,1)S(1)} %shard_map.106.refs_4_), channel_id=1, source_target_pairs={{0,6},{1,7},{2,4},{3,5},{4,2},{5,3},{6,0},{7,1},{8,14},{9,15},{10,... | collective-permute-start | bytes 196616 | tf_op jit(solution)/shard_map/ppermute | solution.py:31
  34.9 6.3 %collective-permute-done.9.refs_2_ = bf16[272,128]{1,0:T(8,128)(2,1)S(1)} collective-permute-done((bf16[272,128]{1,0:T(8,128)(2,1)S(1)}, bf16[272,128]{1,0:T(8,128)(2,1)S(1)}, u32[]{:S(2)}, u32[]{:S(2)}) %collective-permute-start.9) | collective-permute-done | bytes 69664 | tf_op jit(solution)/shard_map/ppermute | solution.py:31
  41.5 1.7 %collective-permute-start.20 = (bf16[144,256]{1,0:T(8,128)(2,1)S(1)}, bf16[144,256]{1,0:T(8,128)(2,1)S(1)}, u32[]{:S(2)}, u32[]{:S(2)}) collective-permute-start(bf16[144,256]{1,0:T(8,128)(2,1)S(1)} %shard_map.107.refs_0_.refs_8_), channel_id=1, source_target_pairs={{0,6},{1,7},{2,4},{3,5},{4,2},{5,3},{6,0},{7,1},{8,14},{9,15},{10,... | collective-permute-start | bytes 221192 | tf_op jit(solution)/shard_map/ppermute | solution.py:31
  43.8 3.0 %collective-permute-start.16 = (bf16[144,256]{1,0:T(8,128)(2,1)S(1)}, bf16[144,256]{1,0:T(8,128)(2,1)S(1)}, u32[]{:S(2)}, u32[]{:S(2)}) collective-permute-start(bf16[144,256]{1,0:T(8,128)(2,1)S(1)} %shard_map.107.refs_0_.refs_8_), channel_id=1, source_target_pairs={{0,2},{1,3},{2,0},{3,1},{4,6},{5,7},{6,4},{7,5},{8,10},{9,11},{10,... | collective-permute-start | bytes 221192 | tf_op jit(solution)/shard_map/ppermute | solution.py:31
  46.8 1.8 %collective-permute-done.18.refs_4_.refs_2_.refs_8_ = bf16[144,256]{1,0:T(8,128)(2,1)S(1)} collective-permute-done((bf16[144,256]{1,0:T(8,128)(2,1)S(1)}, bf16[144,256]{1,0:T(8,128)(2,1)S(1)}, u32[]{:S(2)}, u32[]{:S(2)}) %collective-permute-start.18) | collective-permute-done | bytes 73760 | tf_op jit(solution)/shard_map/ppermute | solution.py:31
  50.4 1.5 %collective-permute-start.25 = (bf16[4,128,256]{2,1,0:T(8,128)(2,1)S(1)}, bf16[4,128,256]{2,1,0:T(8,128)(2,1)S(1)}, u32[]{:S(2)}, u32[]{:S(2)}) collective-permute-start(bf16[4,128,256]{2,1,0:T(8,128)(2,1)S(1)} %shard_map.109.refs_4_), channel_id=1, source_target_pairs={{0,8},{8,0},{16,24},{24,16},{1,9},{9,1},{17,25},{25,17},{2,10},{10... | collective-permute-start | bytes 786440 | tf_op jit(solution)/shard_map/ppermute | solution.py:31
  51.9 1.5 %collective-permute-start.26 = (bf16[4,128,256]{2,1,0:T(8,128)(2,1)S(1)}, bf16[4,128,256]{2,1,0:T(8,128)(2,1)S(1)}, u32[]{:S(2)}, u32[]{:S(2)}) collective-permute-start(bf16[4,128,256]{2,1,0:T(8,128)(2,1)S(1)} %shard_map.109.refs_4_), channel_id=1, source_target_pairs={{0,16},{8,24},{16,0},{24,8},{1,17},{9,25},{17,1},{25,9},{2,18},{10... | collective-permute-start | bytes 786440 | tf_op jit(solution)/shard_map/ppermute | solution.py:31
  53.9 3.5 %shard_map.111 = (bf16[512,2048]{1,0:T(8,128)(2,1)}, bf16[512,2048]{1,0:T(8,128)(2,1)}, bf16[2,256,128]{2,1,0:T(8,128)(2,1)S(1)}, bf16[2,256,128]{2,1,0:T(8,128)(2,1)S(1)}) custom-call(s32[1]{0:T(128)} %bitcast.me_ref, bf16[128,256]{1,0:T(8,128)(2,1)S(1)} %collective-permute-done.1.refs_2_.refs_0_, ...), custom_call_target="tpu_custom_call" | custom-call | flops 536870912 | bytes 4194304 | tf_op jit(solution)/shard_map/pallas_call | solution.py:35
  58.0 3.5 %shard_map.112 = (bf16[512,2048]{1,0:T(8,128)(2,1)}, bf16[512,2048]{1,0:T(8,128)(2,1)}, bf16[2,256,128]{2,1,0:T(8,128)(2,1)S(1)}, bf16[2,256,128]{2,1,0:T(8,128)(2,1)S(1)}) custom-call(s32[1]{0:T(128)} %bitcast.me_ref, bf16[128,256]{1,0:T(8,128)(2,1)S(1)} %bitcast.19, ...), custom_call_target="tpu_custom_call", output_to_operand_aliasing={{0}: (19, {}), {1}: (20, {})} | custom-call | flops 536870912 | bytes 4194304 | tf_op jit(solution)/shard_map/pallas_call | solution.py:35
  61.6 1.5 %collective-permute-start.22 = (bf16[128,512]{1,0:T(8,128)(2,1)S(1)}, bf16[128,512]{1,0:T(8,128)(2,1)S(1)}, u32[]{:S(2)}, u32[]{:S(2)}) collective-permute-start(bf16[128,512]{1,0:T(8,128)(2,1)S(1)} %bitcast.10), channel_id=1, source_target_pairs={{0,8},{8,0},{16,24},{24,16},{1,9},{9,1},{17,25},{25,17},{2,10},{10... | collective-permute-start | bytes 393224 | tf_op jit(solution)/shard_map/ppermute | solution.py:31
  63.2 1.8 %collective-permute-start.40 = (bf16[256,128]{1,0:T(8,128)(2,1)S(1)}, bf16[256,128]{1,0:T(8,128)(2,1)S(1)}, u32[]{:S(2)}, u32[]{:S(2)}) collective-permute-start(bf16[256,128]{1,0:T(8,128)(2,1)S(1)} %get-tuple-element.60), channel_id=1, source_target_pairs={{0,6},{1,7},{2,4},{3,5},{4,2},{5,3},{6,0},{7,1},{8,14},{9,15},{10,... | collective-permute-start | bytes 196616 | tf_op jit(solution)/shard_map/ppermute | solution.py:31
  66.2 1.3 %collective-permute-done.22.refs_1_ = bf16[128,512]{1,0:T(8,128)(2,1)S(1)} collective-permute-done((bf16[128,512]{1,0:T(8,128)(2,1)S(1)}, bf16[128,512]{1,0:T(8,128)(2,1)S(1)}, u32[]{:S(2)}, u32[]{:S(2)}) %collective-permute-start.22) | collective-permute-done | bytes 131104 | tf_op jit(solution)/shard_map/ppermute | solution.py:31
  67.5 1.5 %collective-permute-start.41 = (bf16[256,128]{1,0:T(8,128)(2,1)S(1)}, bf16[256,128]{1,0:T(8,128)(2,1)S(1)}, u32[]{:S(2)}, u32[]{:S(2)}) collective-permute-start(bf16[256,128]{1,0:T(8,128)(2,1)S(1)} %get-tuple-element.61), channel_id=1, source_target_pairs={{0,4},{1,5},{2,6},{3,7},{4,0},{5,1},{6,2},{7,3},{8,12},{9,13},{10,... | collective-permute-start | bytes 196616 | tf_op jit(solution)/shard_map/ppermute | solution.py:31
  70.1 2.8 %collective-permute-done.41.refs_2_ = bf16[256,128]{1,0:T(8,128)(2,1)S(1)} collective-permute-done((bf16[256,128]{1,0:T(8,128)(2,1)S(1)}, bf16[256,128]{1,0:T(8,128)(2,1)S(1)}, u32[]{:S(2)}, u32[]{:S(2)}) %collective-permute-start.41) | collective-permute-done | bytes 65568 | tf_op jit(solution)/shard_map/ppermute | solution.py:31
  72.9 1.5 %collective-permute-start.23 = (bf16[128,512]{1,0:T(8,128)(2,1)S(1)}, bf16[128,512]{1,0:T(8,128)(2,1)S(1)}, u32[]{:S(2)}, u32[]{:S(2)}) collective-permute-start(bf16[128,512]{1,0:T(8,128)(2,1)S(1)} %bitcast.11), channel_id=1, source_target_pairs={{0,16},{8,24},{16,0},{24,8},{1,17},{9,25},{17,1},{25,9},{2,18},{10... | collective-permute-start | bytes 393224 | tf_op jit(solution)/shard_map/ppermute | solution.py:31
  74.5 1.4 %collective-permute-start.24 = (bf16[128,512]{1,0:T(8,128)(2,1)S(1)}, bf16[128,512]{1,0:T(8,128)(2,1)S(1)}, u32[]{:S(2)}, u32[]{:S(2)}) collective-permute-start(bf16[128,512]{1,0:T(8,128)(2,1)S(1)} %bitcast.12), channel_id=1, source_target_pairs={{0,24},{8,16},{16,8},{24,0},{1,25},{9,17},{17,9},{25,1},{2,26},{10... | collective-permute-start | bytes 393224 | tf_op jit(solution)/shard_map/ppermute | solution.py:31
  75.9 1.5 %shard_map.108 = bf16[128,512]{1,0:T(8,128)(2,1)} custom-call(s32[1]{0:T(128)} %bitcast.me_ref, bf16[144,256]{1,0:T(8,128)(2,1)S(1)} %shard_map.107.refs_0_.refs_8_, bf16[144,256]{1,0:T(8,128)(2,1)S(1)} %collective-permute-done.15.refs_1_.refs_11_.refs_9_, bf16[144,256]{1,0:T(8,128)(2,1)S(1)} %collective-permute-done.16.refs_2_.refs_1_.refs_10_, ...), custom_call_target="tpu_custom_call" | custom-call | tf_op jit(solution)/shard_map/pallas_call | solution.py:35
  78.6 1.7 %collective-permute-done.24.refs_3_ = bf16[128,512]{1,0:T(8,128)(2,1)S(1)} collective-permute-done((bf16[128,512]{1,0:T(8,128)(2,1)S(1)}, bf16[128,512]{1,0:T(8,128)(2,1)S(1)}, u32[]{:S(2)}, u32[]{:S(2)}) %collective-permute-start.24) | collective-permute-done | bytes 131104 | tf_op jit(solution)/shard_map/ppermute | solution.py:31
  80.4 2.6 %shard_map.110 = f32[512,2048]{1,0:T(8,128)} custom-call(s32[1]{0:T(128)} %bitcast.me_ref, bf16[128,512]{1,0:T(8,128)(2,1)S(1)} %bitcast.13, bf16[128,512]{1,0:T(8,128)(2,1)S(1)} %collective-permute-done.22.refs_1_, bf16[128,512]{1,0:T(8,128)(2,1)S(1)} %collective-permute-done.23.refs_2_, bf16[128,512]{1,0:T(8,128)(2,1)S(1)} %collective-permute-done.24.refs_3_, ...), custom_call_target="tpu_custom_call" | custom-call | tf_op jit(solution)/shard_map/pallas_call | solution.py:35
  (77 shorter events, 9.2 us)
Async XLA Ops:
  0.6 5.7 %collective-permute-start = (bf16[128,256]{1,0:T(8,128)(2,1)}, bf16[128,256]{1,0:T(8,128)(2,1)S(1)}, u32[]{:S(2)}, u32[]{:S(2)}) collective-permute-start(bf16[128,256]{1,0:T(8,128)(2,1)} %bitcast.14), channel_id=1, source_target_pairs={{0,2},{1,3},{2,0},{3,1},{4,6},{5,7},{6,4},{7,5},{8,10},{9,11},{10,... | collective-permute-start | bytes 196616 | tf_op jit(solution)/shard_map/ppermute | solution.py:31
  3.8 7.5 %collective-permute-start.1 = (bf16[128,256]{1,0:T(8,128)(2,1)}, bf16[128,256]{1,0:T(8,128)(2,1)S(1)}, u32[]{:S(2)}, u32[]{:S(2)}) collective-permute-start(bf16[128,256]{1,0:T(8,128)(2,1)} %bitcast.15), channel_id=1, source_target_pairs={{0,4},{1,5},{2,6},{3,7},{4,0},{5,1},{6,2},{7,3},{8,12},{9,13},{10,... | collective-permute-start | bytes 196616 | tf_op jit(solution)/shard_map/ppermute | solution.py:31
  6.3 6.3 %collective-permute-start.2 = (bf16[128,256]{1,0:T(8,128)(2,1)}, bf16[128,256]{1,0:T(8,128)(2,1)S(1)}, u32[]{:S(2)}, u32[]{:S(2)}) collective-permute-start(bf16[128,256]{1,0:T(8,128)(2,1)} %bitcast.16), channel_id=1, source_target_pairs={{0,6},{1,7},{2,4},{3,5},{4,2},{5,3},{6,0},{7,1},{8,14},{9,15},{10,... | collective-permute-start | bytes 196616 | tf_op jit(solution)/shard_map/ppermute | solution.py:31
  6.3 11.0 %collective-permute-start.3 = (bf16[128,256]{1,0:T(8,128)(2,1)}, bf16[128,256]{1,0:T(8,128)(2,1)S(1)}, u32[]{:S(2)}, u32[]{:S(2)}) collective-permute-start(bf16[128,256]{1,0:T(8,128)(2,1)} %bitcast.17), channel_id=1, source_target_pairs={{0,1},{1,0},{2,3},{3,2},{4,5},{5,4},{6,7},{7,6},{8,9},{9,8},{10,11... | collective-permute-start | bytes 196616 | tf_op jit(solution)/shard_map/ppermute | solution.py:31
  6.4 11.0 %collective-permute-start.4 = (bf16[128,256]{1,0:T(8,128)(2,1)S(1)}, bf16[128,256]{1,0:T(8,128)(2,1)S(1)}, u32[]{:S(2)}, u32[]{:S(2)}) collective-permute-start(bf16[128,256]{1,0:T(8,128)(2,1)S(1)} %collective-permute-done.refs_1_.refs_2_), channel_id=1, source_target_pairs={{0,1},{1,0},{2,3},{3,2},{4,5},{5,4},{6,7},{7,6},{8,9},{9,8},{10,11... | collective-permute-start | bytes 196616 | tf_op jit(solution)/shard_map/ppermute | solution.py:31
  11.2 6.1 %collective-permute-start.5 = (bf16[128,256]{1,0:T(8,128)(2,1)S(1)}, bf16[128,256]{1,0:T(8,128)(2,1)S(1)}, u32[]{:S(2)}, u32[]{:S(2)}) collective-permute-start(bf16[128,256]{1,0:T(8,128)(2,1)S(1)} %collective-permute-done.1.refs_2_.refs_0_), channel_id=1, source_target_pairs={{0,1},{1,0},{2,3},{3,2},{4,5},{5,4},{6,7},{7,6},{8,9},{9,8},{10,11... | collective-permute-start | bytes 196616 | tf_op jit(solution)/shard_map/ppermute | solution.py:31
  20.1 7.4 %collective-permute-start.7 = (bf16[4,272,128]{2,1,0:T(8,128)(2,1)S(1)}, bf16[4,272,128]{2,1,0:T(8,128)(2,1)S(1)}, u32[]{:S(2)}, u32[]{:S(2)}) collective-permute-start(bf16[4,272,128]{2,1,0:T(8,128)(2,1)S(1)} %get-tuple-element.38), channel_id=1, source_target_pairs={{0,1},{1,0},{2,3},{3,2},{4,5},{5,4},{6,7},{7,6},{8,9},{9,8},{10,11... | collective-permute-start | bytes 835592 | tf_op jit(solution)/shard_map/ppermute | solution.py:31
  20.3 9.8 %collective-permute-start.12 = (bf16[128,256]{1,0:T(8,128)(2,1)S(1)}, bf16[128,256]{1,0:T(8,128)(2,1)S(1)}, u32[]{:S(2)}, u32[]{:S(2)}) collective-permute-start(bf16[128,256]{1,0:T(8,128)(2,1)S(1)} %get-tuple-element.46), channel_id=1, source_target_pairs={{0,6},{1,7},{2,4},{3,5},{4,2},{5,3},{6,0},{7,1},{8,14},{9,15},{10,... | collective-permute-start | bytes 196616 | tf_op jit(solution)/shard_map/ppermute | solution.py:31
  22.6 8.6 %collective-permute-start.13 = (bf16[128,256]{1,0:T(8,128)(2,1)S(1)}, bf16[128,256]{1,0:T(8,128)(2,1)S(1)}, u32[]{:S(2)}, u32[]{:S(2)}) collective-permute-start(bf16[128,256]{1,0:T(8,128)(2,1)S(1)} %get-tuple-element.47), channel_id=1, source_target_pairs={{0,4},{1,5},{2,6},{3,7},{4,0},{5,1},{6,2},{7,3},{8,12},{9,13},{10,... | collective-permute-start | bytes 196616 | tf_op jit(solution)/shard_map/ppermute | solution.py:31
  22.6 8.6 %collective-permute-start.14 = (bf16[128,256]{1,0:T(8,128)(2,1)S(1)}, bf16[128,256]{1,0:T(8,128)(2,1)S(1)}, u32[]{:S(2)}, u32[]{:S(2)}) collective-permute-start(bf16[128,256]{1,0:T(8,128)(2,1)S(1)} %get-tuple-element.48), channel_id=1, source_target_pairs={{0,2},{1,3},{2,0},{3,1},{4,6},{5,7},{6,4},{7,5},{8,10},{9,11},{10,... | collective-permute-start | bytes 196616 | tf_op jit(solution)/shard_map/ppermute | solution.py:31
  27.7 7.0 %collective-permute-start.10 = (bf16[272,128]{1,0:T(8,128)(2,1)S(1)}, bf16[272,128]{1,0:T(8,128)(2,1)S(1)}, u32[]{:S(2)}, u32[]{:S(2)}) collective-permute-start(bf16[272,128]{1,0:T(8,128)(2,1)S(1)} %get-tuple-element.42), channel_id=1, source_target_pairs={{0,2},{1,3},{2,0},{3,1},{4,6},{5,7},{6,4},{7,5},{8,10},{9,11},{10,... | collective-permute-start | bytes 208904 | tf_op jit(solution)/shard_map/ppermute | solution.py:31
  27.8 7.1 %collective-permute-start.8 = (bf16[272,128]{1,0:T(8,128)(2,1)S(1)}, bf16[272,128]{1,0:T(8,128)(2,1)S(1)}, u32[]{:S(2)}, u32[]{:S(2)}) collective-permute-start(bf16[272,128]{1,0:T(8,128)(2,1)S(1)} %get-tuple-element.40), channel_id=1, source_target_pairs={{0,6},{1,7},{2,4},{3,5},{4,2},{5,3},{6,0},{7,1},{8,14},{9,15},{10,... | collective-permute-start | bytes 208904 | tf_op jit(solution)/shard_map/ppermute | solution.py:31
  30.1 11.1 %collective-permute-start.9 = (bf16[272,128]{1,0:T(8,128)(2,1)S(1)}, bf16[272,128]{1,0:T(8,128)(2,1)S(1)}, u32[]{:S(2)}, u32[]{:S(2)}) collective-permute-start(bf16[272,128]{1,0:T(8,128)(2,1)S(1)} %get-tuple-element.41), channel_id=1, source_target_pairs={{0,4},{1,5},{2,6},{3,7},{4,0},{5,1},{6,2},{7,3},{8,12},{9,13},{10,... | collective-permute-start | bytes 208904 | tf_op jit(solution)/shard_map/ppermute | solution.py:31
  31.3 12.0 %collective-permute-start.34 = (bf16[128,256]{1,0:T(8,128)(2,1)S(1)}, bf16[128,256]{1,0:T(8,128)(2,1)S(1)}, u32[]{:S(2)}, u32[]{:S(2)}) collective-permute-start(bf16[128,256]{1,0:T(8,128)(2,1)S(1)} %shard_map.106.refs_4_), channel_id=1, source_target_pairs={{0,4},{1,5},{2,6},{3,7},{4,0},{5,1},{6,2},{7,3},{8,12},{9,13},{10,... | collective-permute-start | bytes 196616 | tf_op jit(solution)/shard_map/ppermute | solution.py:31
  33.1 10.2 %collective-permute-start.36 = (bf16[128,256]{1,0:T(8,128)(2,1)S(1)}, bf16[128,256]{1,0:T(8,128)(2,1)S(1)}, u32[]{:S(2)}, u32[]{:S(2)}) collective-permute-start(bf16[128,256]{1,0:T(8,128)(2,1)S(1)} %shard_map.106.refs_4_), channel_id=1, source_target_pairs={{0,6},{1,7},{2,4},{3,5},{4,2},{5,3},{6,0},{7,1},{8,14},{9,15},{10,... | collective-permute-start | bytes 196616 | tf_op jit(solution)/shard_map/ppermute | solution.py:31
  34.7 9.1 %collective-permute-start.32 = (bf16[128,256]{1,0:T(8,128)(2,1)S(1)}, bf16[128,256]{1,0:T(8,128)(2,1)S(1)}, u32[]{:S(2)}, u32[]{:S(2)}) collective-permute-start(bf16[128,256]{1,0:T(8,128)(2,1)S(1)} %shard_map.106.refs_4_), channel_id=1, source_target_pairs={{0,2},{1,3},{2,0},{3,1},{4,6},{5,7},{6,4},{7,5},{8,10},{9,11},{10,... | collective-permute-start | bytes 196616 | tf_op jit(solution)/shard_map/ppermute | solution.py:31
  41.4 7.3 %collective-permute-start.18 = (bf16[144,256]{1,0:T(8,128)(2,1)S(1)}, bf16[144,256]{1,0:T(8,128)(2,1)S(1)}, u32[]{:S(2)}, u32[]{:S(2)}) collective-permute-start(bf16[144,256]{1,0:T(8,128)(2,1)S(1)} %shard_map.107.refs_0_.refs_8_), channel_id=1, source_target_pairs={{0,4},{1,5},{2,6},{3,7},{4,0},{5,1},{6,2},{7,3},{8,12},{9,13},{10,... | collective-permute-start | bytes 221192 | tf_op jit(solution)/shard_map/ppermute | solution.py:31
  41.5 7.2 %collective-permute-start.20 = (bf16[144,256]{1,0:T(8,128)(2,1)S(1)}, bf16[144,256]{1,0:T(8,128)(2,1)S(1)}, u32[]{:S(2)}, u32[]{:S(2)}) collective-permute-start(bf16[144,256]{1,0:T(8,128)(2,1)S(1)} %shard_map.107.refs_0_.refs_8_), channel_id=1, source_target_pairs={{0,6},{1,7},{2,4},{3,5},{4,2},{5,3},{6,0},{7,1},{8,14},{9,15},{10,... | collective-permute-start | bytes 221192 | tf_op jit(solution)/shard_map/ppermute | solution.py:31
  43.3 5.9 %collective-permute-start.31 = (bf16[128,256]{1,0:T(8,128)(2,1)S(1)}, bf16[128,256]{1,0:T(8,128)(2,1)S(1)}, u32[]{:S(2)}, u32[]{:S(2)}) collective-permute-start(bf16[128,256]{1,0:T(8,128)(2,1)S(1)} %shard_map.106.refs_4_), channel_id=1, source_target_pairs={{0,1},{1,0},{2,3},{3,2},{4,5},{5,4},{6,7},{7,6},{8,9},{9,8},{10,11... | collective-permute-start | bytes 196616 | tf_op jit(solution)/shard_map/ppermute | solution.py:31
  43.3 6.0 %collective-permute-start.35 = (bf16[128,256]{1,0:T(8,128)(2,1)S(1)}, bf16[128,256]{1,0:T(8,128)(2,1)S(1)}, u32[]{:S(2)}, u32[]{:S(2)}) collective-permute-start(bf16[128,256]{1,0:T(8,128)(2,1)S(1)} %collective-permute-done.34.refs_4_), channel_id=1, source_target_pairs={{0,1},{1,0},{2,3},{3,2},{4,5},{5,4},{6,7},{7,6},{8,9},{9,8},{10,11... | collective-permute-start | bytes 196616 | tf_op jit(solution)/shard_map/ppermute | solution.py:31
  43.8 6.2 %collective-permute-start.16 = (bf16[144,256]{1,0:T(8,128)(2,1)S(1)}, bf16[144,256]{1,0:T(8,128)(2,1)S(1)}, u32[]{:S(2)}, u32[]{:S(2)}) collective-permute-start(bf16[144,256]{1,0:T(8,128)(2,1)S(1)} %shard_map.107.refs_0_.refs_8_), channel_id=1, source_target_pairs={{0,2},{1,3},{2,0},{3,1},{4,6},{5,7},{6,4},{7,5},{8,10},{9,11},{10,... | collective-permute-start | bytes 221192 | tf_op jit(solution)/shard_map/ppermute | solution.py:31
  50.0 7.4 %collective-permute-start.15 = (bf16[144,256]{1,0:T(8,128)(2,1)S(1)}, bf16[144,256]{1,0:T(8,128)(2,1)S(1)}, u32[]{:S(2)}, u32[]{:S(2)}) collective-permute-start(bf16[144,256]{1,0:T(8,128)(2,1)S(1)} %shard_map.107.refs_0_.refs_8_), channel_id=1, source_target_pairs={{0,1},{1,0},{2,3},{3,2},{4,5},{5,4},{6,7},{7,6},{8,9},{9,8},{10,11... | collective-permute-start | bytes 221192 | tf_op jit(solution)/shard_map/ppermute | solution.py:31
  50.4 14.6 %collective-permute-start.25 = (bf16[4,128,256]{2,1,0:T(8,128)(2,1)S(1)}, bf16[4,128,256]{2,1,0:T(8,128)(2,1)S(1)}, u32[]{:S(2)}, u32[]{:S(2)}) collective-permute-start(bf16[4,128,256]{2,1,0:T(8,128)(2,1)S(1)} %shard_map.109.refs_4_), channel_id=1, source_target_pairs={{0,8},{8,0},{16,24},{24,16},{1,9},{9,1},{17,25},{25,17},{2,10},{10... | collective-permute-start | bytes 786440 | tf_op jit(solution)/shard_map/ppermute | solution.py:31
  51.9 13.7 %collective-permute-start.26 = (bf16[4,128,256]{2,1,0:T(8,128)(2,1)S(1)}, bf16[4,128,256]{2,1,0:T(8,128)(2,1)S(1)}, u32[]{:S(2)}, u32[]{:S(2)}) collective-permute-start(bf16[4,128,256]{2,1,0:T(8,128)(2,1)S(1)} %shard_map.109.refs_4_), channel_id=1, source_target_pairs={{0,16},{8,24},{16,0},{24,8},{1,17},{9,25},{17,1},{25,9},{2,18},{10... | collective-permute-start | bytes 786440 | tf_op jit(solution)/shard_map/ppermute | solution.py:31
  53.4 12.2 %collective-permute-start.27 = (bf16[4,128,256]{2,1,0:T(8,128)(2,1)S(1)}, bf16[4,128,256]{2,1,0:T(8,128)(2,1)S(1)}, u32[]{:S(2)}, u32[]{:S(2)}) collective-permute-start(bf16[4,128,256]{2,1,0:T(8,128)(2,1)S(1)} %shard_map.109.refs_4_), channel_id=1, source_target_pairs={{0,24},{8,16},{16,8},{24,0},{1,25},{9,17},{17,9},{25,1},{2,26},{10... | collective-permute-start | bytes 786440 | tf_op jit(solution)/shard_map/ppermute | solution.py:31
  61.6 5.9 %collective-permute-start.22 = (bf16[128,512]{1,0:T(8,128)(2,1)S(1)}, bf16[128,512]{1,0:T(8,128)(2,1)S(1)}, u32[]{:S(2)}, u32[]{:S(2)}) collective-permute-start(bf16[128,512]{1,0:T(8,128)(2,1)S(1)} %bitcast.10), channel_id=1, source_target_pairs={{0,8},{8,0},{16,24},{24,16},{1,9},{9,1},{17,25},{25,17},{2,10},{10... | collective-permute-start | bytes 393224 | tf_op jit(solution)/shard_map/ppermute | solution.py:31
  63.2 6.1 %collective-permute-start.40 = (bf16[256,128]{1,0:T(8,128)(2,1)S(1)}, bf16[256,128]{1,0:T(8,128)(2,1)S(1)}, u32[]{:S(2)}, u32[]{:S(2)}) collective-permute-start(bf16[256,128]{1,0:T(8,128)(2,1)S(1)} %get-tuple-element.60), channel_id=1, source_target_pairs={{0,6},{1,7},{2,4},{3,5},{4,2},{5,3},{6,0},{7,1},{8,14},{9,15},{10,... | collective-permute-start | bytes 196616 | tf_op jit(solution)/shard_map/ppermute | solution.py:31
  65.0 15.4 %collective-permute-start.28 = (bf16[4,128,256]{2,1,0:T(8,128)(2,1)S(1)}, bf16[4,128,256]{2,1,0:T(8,128)(2,1)S(1)}, u32[]{:S(2)}, u32[]{:S(2)}) collective-permute-start(bf16[4,128,256]{2,1,0:T(8,128)(2,1)S(1)} %collective-permute-done.25.refs_5_), channel_id=1, source_target_pairs={{0,1},{1,0},{2,3},{3,2},{4,5},{5,4},{6,7},{7,6},{8,9},{9,8},{10,11... | collective-permute-start | bytes 786440 | tf_op jit(solution)/shard_map/ppermute | solution.py:31
  65.6 14.7 %collective-permute-start.29 = (bf16[4,128,256]{2,1,0:T(8,128)(2,1)S(1)}, bf16[4,128,256]{2,1,0:T(8,128)(2,1)S(1)}, u32[]{:S(2)}, u32[]{:S(2)}) collective-permute-start(bf16[4,128,256]{2,1,0:T(8,128)(2,1)S(1)} %collective-permute-done.26.refs_6_), channel_id=1, source_target_pairs={{0,1},{1,0},{2,3},{3,2},{4,5},{5,4},{6,7},{7,6},{8,9},{9,8},{10,11... | collective-permute-start | bytes 786440 | tf_op jit(solution)/shard_map/ppermute | solution.py:31
  65.6 14.7 %collective-permute-start.30 = (bf16[4,128,256]{2,1,0:T(8,128)(2,1)S(1)}, bf16[4,128,256]{2,1,0:T(8,128)(2,1)S(1)}, u32[]{:S(2)}, u32[]{:S(2)}) collective-permute-start(bf16[4,128,256]{2,1,0:T(8,128)(2,1)S(1)} %collective-permute-done.27.refs_7_), channel_id=1, source_target_pairs={{0,1},{1,0},{2,3},{3,2},{4,5},{5,4},{6,7},{7,6},{8,9},{9,8},{10,11... | collective-permute-start | bytes 786440 | tf_op jit(solution)/shard_map/ppermute | solution.py:31
  72.9 5.7 %collective-permute-start.23 = (bf16[128,512]{1,0:T(8,128)(2,1)S(1)}, bf16[128,512]{1,0:T(8,128)(2,1)S(1)}, u32[]{:S(2)}, u32[]{:S(2)}) collective-permute-start(bf16[128,512]{1,0:T(8,128)(2,1)S(1)} %bitcast.11), channel_id=1, source_target_pairs={{0,16},{8,24},{16,0},{24,8},{1,17},{9,25},{17,1},{25,9},{2,18},{10... | collective-permute-start | bytes 393224 | tf_op jit(solution)/shard_map/ppermute | solution.py:31
  74.5 5.9 %collective-permute-start.24 = (bf16[128,512]{1,0:T(8,128)(2,1)S(1)}, bf16[128,512]{1,0:T(8,128)(2,1)S(1)}, u32[]{:S(2)}, u32[]{:S(2)}) collective-permute-start(bf16[128,512]{1,0:T(8,128)(2,1)S(1)} %bitcast.12), channel_id=1, source_target_pairs={{0,24},{8,16},{16,8},{24,0},{1,25},{9,17},{17,9},{25,1},{2,26},{10... | collective-permute-start | bytes 393224 | tf_op jit(solution)/shard_map/ppermute | solution.py:31
  (15 other events, 72.7 us)
